TPU v7x, 128 devices: a whole 4x4x4 slice. The times are simulated.
128 devices in a mesh: req: 16 (over y, x), exp: 8 (over z, core).
Axes of the slice: x: 4, y: 4, z: 4, core: 2. Of those that a mesh axis runs over, the one named last changes fastest.
Arguments:
- attention_out: bfloat16 [2048, 4096], P('req'), may hold values from -6 to 6
- residual: bfloat16 [2048, 4096], P('req', 'exp'), may hold values from -6 to 6
- w_out: bfloat16 [4096, 4096], P('req', 'exp'), may hold values from -0.09375 to 0.09375
- router_w: float32 [4096, 8], P('exp'), may hold values from -0.09375 to 0.09375
- norm_gain: float32 [4096], P('exp'), may hold values from 0.5 to 1.5
- page_pool: bfloat16 [4096, 8, 2048], P('req', None, 'exp'), may hold values from -6 to 6
- page_table: int32 [2048, 2], P('req'), may hold values from 0 to 255, as said below
- cache_len: int32 [2048], P('req'), may hold values from 1 to 16
- came_from: int32 [2048], replicated, may hold values from 0 to 2047, as said below
- routes: int32 [2048, 2], P('req'), may hold values from 0 to 7, all different within a row; in each aligned block of 128 rows (0 to 127, 128 to 255, ...) at most 64 rows name the same one
- w_gate: bfloat16 [16, 4096, 7168], P('req', None, 'exp'), as said below
- w_up: bfloat16 [16, 4096, 7168], P('req', None, 'exp'), as said below
- w_down: bfloat16 [16, 7168, 4096], P('req', 'exp'), as said below
Outputs:
- mixed: float32 [2048, 4096], P('req', 'exp')
- new_pages: bfloat16 [2048, 2, 8, 2048], P('req', None, None, 'exp')
Inputs may be any that keep to these rules, and one draw needn't show every extreme that they name: page_table's entries for the requests of one req group are distinct. came_from is a permutation; from each req group 4 rows go to each of the other 15 groups, each group receives 4 rows from each of them, and all other rows keep their place. `routes`: within the rows of one req group every expert is named by at most 64 rows, and some expert by exactly 64 rows in some group. `w_gate`: slices e and e + 8 along the first dimension are equal. `w_up`: slices e and e + 8 along the first dimension are equal. `w_down`: slices e and e + 8 along the first dimension are equal.
All inputs are finite; a program needn't handle non-finite values.
Results may differ from a plain program's by a relative error of at most 0.0055.
Values may be sent and summed in bfloat16 or wider, within the bound.
A program may use at most 128 MiB of HBM per device.

v0:
```python
import jax
import jax.numpy as jnp
from jax import lax
from jax.sharding import PartitionSpec as P

D = 4096
CAP = 32
MIG_PAIR = 4


EPSILON = 1e-05


def pick_rows(source, row_index, live_slot):
    taken_rows = jnp.take(source, row_index, axis=0)
    return jnp.where(live_slot[:, None], taken_rows, jnp.zeros((), source.dtype))


def body(
    attention_out,
    residual,
    w_out,
    router_w,
    norm_gain,
    page_pool,
    page_table,
    cache_len,
    came_from,
    routes,
    w_gate,
    w_up,
    w_down,
):
    groups = lax.axis_size("req")
    own_group = lax.axis_index("req")
    row_req = attention_out.shape[0]
    rows_all = came_from.shape[0]
    pages_req = page_table.shape[1]
    page_len = page_pool.shape[1]
    kv_slice = page_pool.shape[2]
    experts = groups // 2
    targets = jnp.arange(groups, dtype=jnp.int32)
    local_ids = jnp.arange(row_req, dtype=jnp.int32)
    dest_of = (
        jnp.zeros((rows_all,), jnp.int32).at[came_from].set(jnp.arange(rows_all, dtype=jnp.int32))
    )
    dest_group = dest_of // row_req
    dest_hot = (
        (dest_group[:, None] == targets[None, :]).astype(jnp.int32).reshape(groups, row_req, groups)
    )
    pair_rank = jnp.sum((jnp.cumsum(dest_hot, axis=1) - dest_hot) * dest_hot, axis=2).reshape(
        rows_all
    )
    own_dest = lax.dynamic_slice_in_dim(dest_group, own_group * row_req, row_req)
    own_rank = lax.dynamic_slice_in_dim(pair_rank, own_group * row_req, row_req)
    chosen_send = (
        (own_dest[None, None, :] == targets[:, None, None])
        & (own_rank[None, None, :] == jnp.arange(MIG_PAIR, dtype=jnp.int32)[None, :, None])
        & (targets[:, None, None] != own_group)
    )
    send_index = jnp.sum(jnp.where(chosen_send, local_ids[None, None, :], 0), axis=2).reshape(-1)
    send_live = jnp.any(chosen_send, axis=2).reshape(-1)
    page_rows = jnp.take(page_pool, page_table.reshape(-1), axis=0).reshape(
        row_req, pages_req, page_len, kv_slice
    )
    position = (
        jnp.arange(pages_req, dtype=jnp.int32)[:, None] * page_len
        + jnp.arange(page_len, dtype=jnp.int32)[None, :]
    )
    kept_mask = position[None, :, :] < cache_len[:, None, None]
    page_rows = jnp.where(kept_mask[..., None], page_rows, jnp.zeros((), page_rows.dtype)).reshape(
        row_req, -1
    )
    moved_attn, moved_resid, moved_pages = (
        lax.all_to_all(
            pick_rows(attention_out, send_index, send_live),
            "req",
            split_axis=0,
            concat_axis=0,
            tiled=True,
        ),
        lax.all_to_all(
            pick_rows(residual, send_index, send_live),
            "req",
            split_axis=0,
            concat_axis=0,
            tiled=True,
        ),
        lax.all_to_all(
            pick_rows(page_rows, send_index, send_live),
            "req",
            split_axis=0,
            concat_axis=0,
            tiled=True,
        ),
    )
    new_source = lax.dynamic_slice_in_dim(came_from, own_group * row_req, row_req)
    source_group = new_source // row_req
    stays_home = source_group == own_group
    arrival = jnp.where(
        stays_home,
        new_source - own_group * row_req,
        row_req + source_group * MIG_PAIR + jnp.take(pair_rank, new_source),
    )
    attn_new = jnp.take(jnp.concatenate([attention_out, moved_attn], axis=0), arrival, axis=0)
    resid_new = jnp.take(jnp.concatenate([residual, moved_resid], axis=0), arrival, axis=0)
    new_pages = jnp.take(
        jnp.concatenate([page_rows, moved_pages], axis=0), arrival, axis=0
    ).reshape(row_req, pages_req, page_len, kv_slice)
    projected = jnp.dot(
        attn_new,
        lax.all_gather(w_out, "req", axis=0, tiled=True),
        preferred_element_type=jnp.float32,
    )
    hidden = resid_new.astype(jnp.float32) + projected
    squares = jnp.sum(hidden * hidden, axis=1)
    scaled = hidden * norm_gain[None, :]
    total_sq = lax.psum(squares, "exp")
    inverse = lax.rsqrt(total_sq / D + EPSILON)
    normed = scaled * inverse[:, None]
    logits = lax.psum(jnp.dot(normed, router_w, precision=lax.Precision.HIGHEST), "exp")
    normed_rows = normed.astype(jnp.bfloat16)
    expert_ids = jnp.arange(experts, dtype=jnp.int32)
    chosen = jnp.sum(
        jnp.where(routes[:, :, None] == expert_ids[None, None, :], logits[:, None, :], 0.0), axis=2
    )
    gate_first = jax.nn.sigmoid(chosen[:, 0] - chosen[:, 1])
    gate_second = jax.nn.sigmoid(chosen[:, 1] - chosen[:, 0])
    flat_routes = routes.reshape(-1)
    expert_hot = (flat_routes[:, None] == expert_ids[None, :]).astype(jnp.int32)
    expert_rank = jnp.sum((jnp.cumsum(expert_hot, axis=0) - expert_hot) * expert_hot, axis=1)
    target_dev = flat_routes + experts * (expert_rank % 2)
    slot_index = expert_rank // 2
    assign_ids = jnp.arange(flat_routes.shape[0], dtype=jnp.int32)
    chosen_slot = (target_dev[None, None, :] == targets[:, None, None]) & (
        slot_index[None, None, :] == jnp.arange(CAP, dtype=jnp.int32)[None, :, None]
    )
    slot_source = jnp.sum(
        jnp.where(chosen_slot, assign_ids[None, None, :] // 2, 0), axis=2
    ).reshape(-1)
    slot_live = jnp.any(chosen_slot, axis=2).reshape(-1)
    outgoing = pick_rows(normed_rows, slot_source, slot_live)
    arrived = lax.all_to_all(outgoing, "req", split_axis=0, concat_axis=0, tiled=True)
    rows_full = lax.all_gather(arrived, "exp", axis=1, tiled=True)
    gate_h = jnp.dot(rows_full, w_gate[0], preferred_element_type=jnp.float32)
    up_h = jnp.dot(rows_full, w_up[0], preferred_element_type=jnp.float32)
    active = (jax.nn.silu(gate_h) * up_h).astype(jnp.bfloat16)
    partial_value = lax.optimization_barrier(
        jnp.dot(active, w_down[0], preferred_element_type=jnp.float32).astype(jnp.bfloat16)
    )
    lookup = target_dev * CAP + slot_index
    returned = lax.all_to_all(partial_value, "req", split_axis=0, concat_axis=0, tiled=True)
    taken_rows = jnp.take(returned, lookup, axis=0).reshape(row_req, 2, -1)
    weighted = gate_first[:, None] * taken_rows[:, 0].astype(jnp.float32) + gate_second[
        :, None
    ] * taken_rows[:, 1].astype(jnp.float32)
    expert_part = lax.psum_scatter(
        weighted.astype(jnp.bfloat16), "exp", scatter_dimension=1, tiled=True
    ).astype(jnp.float32)
    mixed = hidden + expert_part
    return (mixed, new_pages)


def solution(mesh):
    in_specs = (
        P("req", None),
        P("req", "exp"),
        P("req", "exp"),
        P("exp", None),
        P("exp"),
        P("req", None, "exp"),
        P("req", None),
        P("req"),
        P(),
        P("req", None),
        P("req", None, "exp"),
        P("req", None, "exp"),
        P("req", "exp", None),
    )
    out_specs = (P("req", "exp"), P("req", None, None, "exp"))
    return jax.shard_map(body, mesh=mesh, in_specs=in_specs, out_specs=out_specs, check_vma=False)
```

profile of v0, /device:TPU:0, one launch (start us, length us, event | category | flops | bytes accessed | tf_op | source)
XLA Modules:
  0.0 285.6 jit_solution(12334850241228818001)
XLA Ops:
  7.2 0.7 all-gather.3.cloned.1.call-update
  7.9 0.7 compare_select_fusion.1
  8.6 8.0 %scatter_custom_fusion = s32[2048]{0:T(1024)S(1)} fusion(s32[2048]{0:T(1024)S(1)} %compare_select_fusion.1, s32[2048]{0:T(1024)S(1)} %iota.72, s32[]{:T(128)} %constant.182.clone.1), kind=kCustom, calls=%fused_computation.92 | custom fusion | bytes 8196 | tf_op jit(solution)/shard_map/scatter | solution.py:45
  16.9 2.8 select_reduce_fusion
  20.7 1.6 gather_fusion.1
  22.4 0.7 select_select_fusion.4
  23.1 7.1 %all-to-all-start = ((bf16[16,4,512]{2,1,0:T(4,128)(2,1)}), bf16[16,4,512]{2,1,0:T(4,128)(2,1)S(1)}, u32[]{:S(2)}, u32[]{:S(2)}) async-start(bf16[16,4,512]{2,1,0:T(4,128)(2,1)} %select_select_fusion.4), calls=%async_computation | async-start | bytes 131072 | tf_op jit(solution)/shard_map/all_to_all | solution.py:82
  30.3 0.8 copy.122
  31.5 0.8 copy.131
  32.3 0.7 compare_and_fusion.2
  33.1 0.6 reduce-window.6
  34.6 0.8 compare_select_fusion.15
  35.3 1.1 gather_fusion
  36.9 0.4 broadcast_in_dim.226
  37.7 0.4 broadcast_in_dim.228
  38.1 1.1 copy.133
  39.2 1.7 gather_fusion.5
  41.0 2.4 gather.47
  43.4 0.9 gather_fusion.6
  44.2 1.6 select_select_fusion
  45.8 0.9 gather_fusion.8
  46.8 1.0 select_select_fusion.1
  47.8 1.0 all_to_all.38
  48.8 0.8 compare_and_fusion.5
  49.6 7.2 %all-to-all-start.1 = ((bf16[16,4,4096]{2,1,0:T(4,128)(2,1)}), bf16[16,4,4096]{2,1,0:T(4,128)(2,1)S(1)}, u32[]{:S(2)}, u32[]{:S(2)}) async-start(bf16[16,4,4096]{2,1,0:T(4,128)(2,1)} %all_to_all.38), calls=%async_computation.1 | async-start | bytes 1048576 | tf_op jit(solution)/shard_map/all_to_all | solution.py:75
  57.4 0.8 gather_fusion.2
  58.2 13.6 %all-to-all-done.1 = bf16[16,4,4096]{2,1,0:T(4,128)(2,1)S(1)} async-done(((bf16[16,4,4096]{2,1,0:T(4,128)(2,1)}), bf16[16,4,4096]{2,1,0:T(4,128)(2,1)S(1)}, u32[]{:S(2)}, u32[]{:S(2)}) %all-to-all-start.1) | async-done | bytes 524320 | tf_op jit(solution)/shard_map/all_to_all | solution.py:75
  72.2 1.2 gather_fusion.7
  73.4 3.0 %multiply_reduce_fusion = (f32[128]{0:T(128)S(1)}, f32[128,512]{1,0:T(8,128)S(1)}) fusion(bf16[4096,512]{1,0:T(8,128)(2,1)} %all-gather.3.cloned.1.call-done, bf16[128,4096]{1,0:T(8,128)(2,1)S(1)} %gather_fusion.7, pred[128]{0:T(512)(128)(4,1)S(1)} %get-tuple-element.4, bf16[128,512]{1,0:T(8,128)(2,1)S(1)} %gather_fusion.2), kind=kOutput, calls=%fused_computation.47 | convolution fusion | flops 537722752 | bytes 5636736 | tf_op jit(solution)/shard_map/dot_general | solution.py:110
  76.4 14.3 %psum.14 = f32[128]{0:T(128)S(1)} all-reduce(f32[128]{0:T(128)S(1)} %get-tuple-element.14), channel_id=1, replica_groups=mesh['req'=16,'exp'=8] {'exp'}, use_global_device_ids=true, to_apply=%region_6.9 | all-reduce | flops 128 | bytes 1024 | tf_op jit(solution)/shard_map/psum | solution.py:118
  90.8 2.0 gather_fusion.3
  93.0 13.6 %all_to_all.54 = bf16[16,32,512]{2,1,0:T(8,128)(2,1)} all-to-all(bf16[16,32,512]{2,1,0:T(8,128)(2,1)S(1)} %select_select_fusion.3), channel_id=1, replica_groups=mesh['req'=16,'exp'=8] {'req'}, dimensions={0} | all-to-all | bytes 1048576 | tf_op jit(solution)/shard_map/all_to_all | solution.py:143
  106.6 28.7 %all-gather.5.cloned.1.call-done = bf16[512,4096]{1,0:T(8,128)(2,1)} async-done(((bf16[512,512]{1,0:T(8,128)(2,1)}), bf16[512,4096]{1,0:T(8,128)(2,1)}) %all-gather.5.cloned.1.call-update) | async-done | bytes 4194320 | tf_op jit(solution)/shard_map/all_gather | solution.py:144
  135.3 9.8 %fusion.4 = f32[512,896]{1,0:T(8,128)S(1)} fusion(bf16[512,4096]{1,0:T(8,128)(2,1)} %all-gather.5.cloned.1.call-done, bf16[1,4096,896]{2,1,0:T(8,128)(2,1)} %param.27), kind=kOutput, calls=%fused_computation.15 | convolution fusion | flops 3758096384 | bytes 13369344 | tf_op jit(solution)/shard_map/dot_general | solution.py:145
  145.1 16.3 %fusion.6 = bf16[512,4096]{1,0:T(8,128)(2,1)} fusion(bf16[1,896,4096]{2,1,0:T(8,128)(2,1)} %param.29, f32[512,896]{1,0:T(8,128)S(1)} %fusion.4, bf16[512,4096]{1,0:T(8,128)(2,1)} %all-gather.5.cloned.1.call-done, bf16[1,4096,896]{2,1,0:T(8,128)(2,1)} %param.28), kind=kOutput, calls=%fused_computation.17 | convolution fusion | flops 7521042432 | bytes 24903680 | tf_op jit(solution)/shard_map/dot_general | solution.py:149
  161.4 7.0 %all-to-all-start.3 = ((bf16[16,32,4096]{2,1,0:T(8,128)(2,1)}), bf16[16,32,4096]{2,1,0:T(8,128)(2,1)}, u32[]{:S(2)}, u32[]{:S(2)}) async-start(bf16[16,32,4096]{2,1,0:T(8,128)(2,1)} %bitcast.67), calls=%async_computation.3 | async-start | bytes 8388608 | tf_op jit(solution)/shard_map/all_to_all | solution.py:152
  169.3 13.8 %psum.15 = f32[128,8]{0,1:T(8,128)S(1)} all-reduce(f32[128,8]{0,1:T(8,128)S(1)} %fusion.25), channel_id=1, replica_groups=mesh['req'=16,'exp'=8] {'exp'}, use_global_device_ids=true, to_apply=%region_7.10 | all-reduce | flops 1024 | bytes 8192 | tf_op jit(solution)/shard_map/psum | solution.py:121
  183.1 49.0 %all-to-all-done.3 = bf16[16,32,4096]{2,1,0:T(8,128)(2,1)} async-done(((bf16[16,32,4096]{2,1,0:T(8,128)(2,1)}), bf16[16,32,4096]{2,1,0:T(8,128)(2,1)}, u32[]{:S(2)}, u32[]{:S(2)}) %all-to-all-start.3) | async-done | bytes 4194336 | tf_op jit(solution)/shard_map/all_to_all | solution.py:152
  232.1 6.6 %gather_fusion.4 = bf16[256,4096]{1,0:T(8,128)(2,1)S(1)} fusion(bf16[512,4096]{1,0:T(8,128)(2,1)} %bitcast.13, s32[1024]{0:T(1024)S(1)} %pad_clamp_fusion.1), kind=kCustom, calls=%fused_computation.8 | custom fusion | bytes 4195328 | tf_op jit(solution)/shard_map/jit(_take)/gather | solution.py:153
  238.8 2.7 gather.45
  241.4 4.0 %copy_select_fusion = bf16[128,2,4096]{2,0,1:T(8,128)(2,1)S(1)} fusion(bf16[128,2,4096]{2,1,0:T(2,128)(2,1)} %gather.45, pred[128,2]{0,1:T(4,128)(4,1)S(1)} %compare_and_fusion.3), kind=kLoop, calls=%fused_computation.22 | loop fusion | flops 1048576 | bytes 4194560 | tf_op jit(solution)/shard_map/jit(_take)/select_n | solution.py:153
  245.5 1.5 fusion.10
  247.2 15.8 %all_to_all.55 = bf16[16,4,4096]{2,1,0:T(4,128)(2,1)S(1)} all-to-all(bf16[16,4,4096]{2,1,0:T(4,128)(2,1)S(1)} %all_to_all.46), channel_id=1, replica_groups=mesh['req'=16,'exp'=8] {'req'}, dimensions={0} | all-to-all | bytes 1048576 | tf_op jit(solution)/shard_map/all_to_all | solution.py:89
  263.3 2.2 gather_fusion.9
  265.5 1.4 broadcast_select_fusion
  266.9 1.2 copy.134
  268.1 9.3 %reduce-scatter.2.cloned.1.call-done = bf16[128,512]{1,0:T(8,128)(2,1)} async-done(((bf16[128,4096]{1,0:T(8,128)(2,1)}), bf16[128,512]{1,0:T(8,128)(2,1)}) %reduce-scatter.2.cloned.1.call-update) | async-done | bytes 131088 | tf_op jit(solution)/shard_map/reduce_scatter | solution.py:157
  277.4 1.6 convert_add_fusion
  (99 shorter events, 5.9 us)
Async XLA Ops:
  7.2 32.1 %copy-start = (bf16[256,8,256]{2,1,0:T(8,128)(2,1)S(1)}, bf16[256,8,256]{2,1,0:T(8,128)(2,1)}, u32[]{:S(2)}) copy-start(bf16[256,8,256]{2,1,0:T(8,128)(2,1)} %param.22) | copy-start | bytes 3145732
  7.2 29.5 %copy-start.10 = (s32[128]{0:T(128)S(1)}, s32[128]{0:T(128)}, u32[]{:S(2)}) copy-start(s32[128]{0:T(128)} %param.24) | copy-start | bytes 1540
  7.2 66.2 %all-gather.3.cloned.1.call-start = ((), (), s32[]{:S(2)}) async-start(), calls=%async_computation.6 | async-start | bytes 4456448 | tf_op jit(solution)/shard_map/all_gather | solution.py:112
  23.1 26.5 %all-to-all-start = ((bf16[16,4,512]{2,1,0:T(4,128)(2,1)}), bf16[16,4,512]{2,1,0:T(4,128)(2,1)S(1)}, u32[]{:S(2)}, u32[]{:S(2)}) async-start(bf16[16,4,512]{2,1,0:T(4,128)(2,1)} %select_select_fusion.4), calls=%async_computation | async-start | bytes 131072 | tf_op jit(solution)/shard_map/all_to_all | solution.py:82
  39.2 4.1 %copy-start.4 = (bf16[128,4096]{1,0:T(8,128)(2,1)S(1)}, bf16[128,4096]{1,0:T(8,128)(2,1)}, u32[]{:S(2)}) copy-start(bf16[128,4096]{1,0:T(8,128)(2,1)} %param.17) | copy-start | bytes 3145732
  45.8 1.0 copy-start.2
  46.8 10.5 %copy-start.5 = (bf16[128,512]{1,0:T(8,128)(2,1)S(1)}, bf16[128,512]{1,0:T(8,128)(2,1)}, u32[]{:S(2)}) copy-start(bf16[128,512]{1,0:T(8,128)(2,1)} %param.18) | copy-start | bytes 393220
  49.6 22.2 %all-to-all-start.1 = ((bf16[16,4,4096]{2,1,0:T(4,128)(2,1)}), bf16[16,4,4096]{2,1,0:T(4,128)(2,1)S(1)}, u32[]{:S(2)}, u32[]{:S(2)}) async-start(bf16[16,4,4096]{2,1,0:T(4,128)(2,1)} %all_to_all.38), calls=%async_computation.1 | async-start | bytes 1048576 | tf_op jit(solution)/shard_map/all_to_all | solution.py:75
  56.9 78.5 %all-gather.5.cloned.1.call-start = ((), (), s32[]{:S(2)}) async-start(), calls=%async_computation.7 | async-start | bytes 4718592 | tf_op jit(solution)/shard_map/all_gather | solution.py:144
  73.4 17.4 %copy-start.9 = (f32[512]{0:T(512)S(1)}, f32[512]{0:T(512)}, u32[]{:S(2)}) copy-start(f32[512]{0:T(512)} %param.21) | copy-start | bytes 6148
  161.4 7.5 %copy-start.8 = (s32[128,2]{0,1:T(2,128)S(1)}, s32[128,2]{0,1:T(2,128)}, u32[]{:S(2)}) copy-start(s32[128,2]{0,1:T(2,128)} %param.26) | copy-start | bytes 3076
  161.4 7.5 %copy-start.7 = (f32[512,8]{0,1:T(8,128)S(1)}, f32[512,8]{0,1:T(8,128)}, u32[]{:S(2)}) copy-start(f32[512,8]{0,1:T(8,128)} %param.20) | copy-start | bytes 49156
  161.4 70.7 %all-to-all-start.3 = ((bf16[16,32,4096]{2,1,0:T(8,128)(2,1)}), bf16[16,32,4096]{2,1,0:T(8,128)(2,1)}, u32[]{:S(2)}, u32[]{:S(2)}) async-start(bf16[16,32,4096]{2,1,0:T(8,128)(2,1)} %bitcast.67), calls=%async_computation.3 | async-start | bytes 8388608 | tf_op jit(solution)/shard_map/all_to_all | solution.py:152
  168.4 109.0 %reduce-scatter.2.cloned.1.call-start = ((), (), s32[]{:S(2)}) async-start(), calls=%async_computation.8 | async-start | bytes 1179648 | tf_op jit(solution)/shard_map/reduce_scatter | solution.py:157
  245.4 1.5 copy-start.6
  246.9 16.2 %copy-start.3 = (bf16[128,4096]{1,0:T(8,128)(2,1)S(1)}, bf16[128,4096]{1,0:T(8,128)(2,1)}, u32[]{:S(2)}) copy-start(bf16[128,4096]{1,0:T(8,128)(2,1)} %copy-done.2) | copy-start | bytes 3145732
  263.3 15.8 %copy-start.1 = (bf16[256,8,256]{2,1,0:T(8,128)(2,1)S(1)}, bf16[256,8,256]{2,1,0:T(8,128)(2,1)}, u32[]{:S(2)}) copy-start(bf16[256,8,256]{2,1,0:T(8,128)(2,1)} %param.22) | copy-start | bytes 3145732
Sparse Core Ops, SparseCore 0:
  10.2 59.3 all-gather.2
  106.7 28.5 all-gather.4
  247.1 30.3 reduce-scatter.1
where the time goes:
time: 286 us
  waiting for transfers between devices  101 us (35%)
  blocking collectives  57.5 us (20%)
  local copies, waits for them, and re-layouts  40.8 us (14%)
  matrix products  29.5 us (10%)
  starting transfers between devices  21.5 us (8%)
  other arithmetic  20.6 us (7%)
  between operations  14.2 us (5%)
    all_to_all x1, waiting for transfers between devices, body(): lax.all_to_all(partial_value, 'req', split_axis=0, concat_axis=0, tiled=T...  49 us
    all_gather x1, waiting for transfers between devices, body(): rows_full = lax.all_gather(arrived, 'exp', axis=1, tiled=True)  28.7 us
    dot_general x1, matrix products, body(): jnp.dot(active, w_down[0], preferred_element_type=jnp.float32)  16.3 us
    all_to_all x1, blocking collectives, body(): lax.all_to_all(pick_rows(page_rows, send_index, send_live), 'req', split_...  15.8 us
    psum x1, blocking collectives, body(): total_sq = lax.psum(squares, 'exp')  14.3 us
    psum x1, blocking collectives, body(): lax.psum(jnp.dot(normed, router_w, precision=lax.Precision.HIGHEST), 'exp')  13.8 us
    all_to_all x1, waiting for transfers between devices, body(): lax.all_to_all(pick_rows(attention_out, send_index, send_live), 'req', sp...  13.6 us
    all_to_all x1, blocking collectives, body(): lax.all_to_all(outgoing, 'req', split_axis=0, concat_axis=0, tiled=True)  13.6 us
  transfers between devices with their start and end apart: 6, of which 4 were waited for; matrix products, arithmetic and copies ran while one was open for 15% of the time, Pallas kernels for 0%

commit v1 on v0

--- a/solution.py
+++ b/solution.py
@@ -107,6 +107,7 @@
     new_pages = jnp.take(
         jnp.concatenate([page_rows, moved_pages], axis=0), arrival, axis=0
     ).reshape(row_req, pages_req, page_len, kv_slice)
+    new_pages, attn_new = lax.optimization_barrier((new_pages, attn_new))
     projected = jnp.dot(
         attn_new,
         lax.all_gather(w_out, "req", axis=0, tiled=True),
@@ -115,10 +116,12 @@
     hidden = resid_new.astype(jnp.float32) + projected
     squares = jnp.sum(hidden * hidden, axis=1)
     scaled = hidden * norm_gain[None, :]
-    total_sq = lax.psum(squares, "exp")
+    raw_logits = jnp.dot(scaled, router_w, precision=lax.Precision.HIGHEST)
+    row_stats = lax.psum(jnp.concatenate([squares[:, None], raw_logits], axis=1), "exp")
+    total_sq = row_stats[:, 0]
     inverse = lax.rsqrt(total_sq / D + EPSILON)
     normed = scaled * inverse[:, None]
-    logits = lax.psum(jnp.dot(normed, router_w, precision=lax.Precision.HIGHEST), "exp")
+    logits = row_stats[:, 1:] * inverse[:, None]
     normed_rows = normed.astype(jnp.bfloat16)
     expert_ids = jnp.arange(experts, dtype=jnp.int32)
     chosen = jnp.sum(
@@ -148,15 +151,11 @@
     partial_value = lax.optimization_barrier(
         jnp.dot(active, w_down[0], preferred_element_type=jnp.float32).astype(jnp.bfloat16)
     )
+    summed_value = lax.psum_scatter(partial_value, "exp", scatter_dimension=1, tiled=True)
     lookup = target_dev * CAP + slot_index
-    returned = lax.all_to_all(partial_value, "req", split_axis=0, concat_axis=0, tiled=True)
-    taken_rows = jnp.take(returned, lookup, axis=0).reshape(row_req, 2, -1)
-    weighted = gate_first[:, None] * taken_rows[:, 0].astype(jnp.float32) + gate_second[
-        :, None
-    ] * taken_rows[:, 1].astype(jnp.float32)
-    expert_part = lax.psum_scatter(
-        weighted.astype(jnp.bfloat16), "exp", scatter_dimension=1, tiled=True
-    ).astype(jnp.float32)
+    returned = lax.all_to_all(summed_value, "req", split_axis=0, concat_axis=0, tiled=True)
+    taken_rows = jnp.take(returned, lookup, axis=0).reshape(row_req, 2, -1).astype(jnp.float32)
+    expert_part = gate_first[:, None] * taken_rows[:, 0] + gate_second[:, None] * taken_rows[:, 1]
     mixed = hidden + expert_part
     return (mixed, new_pages)
 

time: 286 us -> 246 us (0.86)
  blocking collectives: 57.5 us -> 27.8 us
  waiting for transfers between devices: 101 us -> 90.3 us
  starting transfers between devices: 21.5 us -> 25 us
    all_to_all x1 -> x2, waiting for transfers between devices: 49 us -> 19.6 us  [the longest x1 10.1 us: body(): lax.all_to_all(summed_value, 'req', split_axis=0, concat_axis=0, tiled=True)]
    reduce_scatter x1, waiting for transfers between devices: 9.32 us -> 37.5 us  [body(): lax.psum_scatter(partial_value, 'exp', scatter_dimension=1, tiled=True)]
    all_to_all x1 -> x0, blocking collectives: 15.8 us -> none  [body(): lax.all_to_all(pick_rows(page_rows, send_index, send_live), 'req', split_...]
    psum x2 -> x1, blocking collectives: 28.1 us -> 12.7 us  [body(): lax.psum(jnp.concatenate([squares[:, None], raw_logits], axis=1), 'exp')]
    all_to_all x1, waiting for transfers between devices: 13.6 us -> 5.09 us  [body(): lax.all_to_all(pick_rows(attention_out, send_index, send_live), 'req', sp...]
    gather x2, local copies, waits for them, and re-layouts: 9.27 us -> 1.26 us  [body(): jnp.take(returned, lookup, axis=0).reshape(row_req, 2, -1)]
    all_to_all x1 -> x2, starting transfers between devices: 6.99 us -> 14 us  [the longest x1 7.21 us: body(): lax.all_to_all(pick_rows(page_rows, send_index, send_live), 'req', split_...]
    all_to_all x1, starting transfers between devices: 7.23 us -> 3.57 us  [body(): lax.all_to_all(pick_rows(attention_out, send_index, send_live), 'req', sp...]
  transfers between devices with their start and end apart: 6 -> 7, of which waited for: 4 -> 5; matrix products, arithmetic and copies ran while one was open for 15% -> 19% of each run, Pallas kernels for 0% -> 0%
where the time goes in v1:
time: 246 us; the launch traced here: 245 us
  waiting for transfers between devices  90.3 us (37%)
  local copies, waits for them, and re-layouts  39.8 us (16%)
  matrix products  30 us (12%)
  blocking collectives  27.8 us (11%)
  starting transfers between devices  25 us (10%)
  other arithmetic  18.2 us (7%)
  between operations  14.2 us (6%)
    reduce_scatter x1, waiting for transfers between devices, body(): lax.psum_scatter(partial_value, 'exp', scatter_dimension=1, tiled=True)  37.5 us
    all_gather x1, waiting for transfers between devices, body(): rows_full = lax.all_gather(arrived, 'exp', axis=1, tiled=True)  27.4 us
    dot_general x1, matrix products, body(): jnp.dot(active, w_down[0], preferred_element_type=jnp.float32)  16.6 us
    all_to_all x1, blocking collectives, body(): lax.all_to_all(outgoing, 'req', split_axis=0, concat_axis=0, tiled=True)  15.1 us
    psum x1, blocking collectives, body(): lax.psum(jnp.concatenate([squares[:, None], raw_logits], axis=1), 'exp')  12.7 us
    dot_general x1, matrix products, body(): gate_h = jnp.dot(rows_full, w_gate[0], preferred_element_type=jnp.float32)  10.1 us
    all_to_all x1, waiting for transfers between devices, body(): lax.all_to_all(summed_value, 'req', split_axis=0, concat_axis=0, tiled=True)  10.1 us
    all_to_all x1, waiting for transfers between devices, body(): lax.all_to_all(pick_rows(page_rows, send_index, send_live), 'req', split_...  9.49 us
  transfers between devices with their start and end apart: 7, of which 5 were waited for; matrix products, arithmetic and copies ran while one was open for 19% of the time, Pallas kernels for 0%

profile of v1, /device:TPU:0, one launch (start us, length us, event | category | flops | bytes accessed | tf_op | source)
XLA Modules:
  0.0 245.3 jit_solution(16196144901007019465)
XLA Ops:
  7.9 0.7 compare_select_fusion.1
  8.6 8.0 %scatter_custom_fusion = s32[2048]{0:T(1024)S(1)} fusion(s32[2048]{0:T(1024)S(1)} %compare_select_fusion.1, s32[2048]{0:T(1024)S(1)} %iota.72, s32[]{:T(128)} %constant.182.clone.1), kind=kCustom, calls=%fused_computation.91 | custom fusion | bytes 8196 | tf_op jit(solution)/shard_map/scatter | solution.py:45
  16.9 2.8 %select_reduce_fusion = s32[16,128]{0,1:T(8,128)S(1)} fusion(s32[16,128]{0,1:T(8,128)S(1)} %copy.115), kind=kOutput, calls=%fused_computation.26 | output fusion | flops 4388864 | bytes 16384 | tf_op jit(solution)/shard_map/jit(cumsum)/reduce_window_sum | solution.py:51
  20.7 1.6 gather_fusion.1
  22.4 0.7 select_select_fusion.4
  23.1 7.1 %all-to-all-start = ((bf16[16,4,512]{2,1,0:T(4,128)(2,1)}), bf16[16,4,512]{2,1,0:T(4,128)(2,1)S(1)}, u32[]{:S(2)}, u32[]{:S(2)}) async-start(bf16[16,4,512]{2,1,0:T(4,128)(2,1)} %select_select_fusion.4), calls=%async_computation | async-start | bytes 131072 | tf_op jit(solution)/shard_map/all_to_all | solution.py:82
  30.2 0.8 copy.124
  31.2 0.8 compare_and_fusion.3
  32.3 0.8 copy.121
  34.6 0.8 compare_select_fusion.15
  35.4 1.1 gather_fusion
  36.8 0.9 broadcast_compare_fusion
  38.1 1.1 copy.132
  39.7 1.1 copy.133
  40.8 1.7 gather_fusion.3
  42.5 1.6 gather.43
  44.1 1.7 gather_fusion.8
  45.8 1.4 select_select_fusion
  47.2 0.9 gather_fusion.6
  48.6 1.2 select_select_fusion.1
  49.8 0.8 compare_and_fusion.5
  50.6 2.1 all_to_all.38
  52.6 7.2 %all-to-all-start.1 = ((bf16[16,4,4096]{2,1,0:T(4,128)(2,1)}), bf16[16,4,4096]{2,1,0:T(4,128)(2,1)S(1)}, u32[]{:S(2)}, u32[]{:S(2)}) async-start(bf16[16,4,4096]{2,1,0:T(4,128)(2,1)} %all_to_all.38), calls=%async_computation.1 | async-start | bytes 1048576 | tf_op jit(solution)/shard_map/all_to_all | solution.py:89
  59.9 2.0 all_to_all.41
  62.3 9.5 %all-to-all-done.1 = bf16[16,4,4096]{2,1,0:T(4,128)(2,1)S(1)} async-done(((bf16[16,4,4096]{2,1,0:T(4,128)(2,1)}), bf16[16,4,4096]{2,1,0:T(4,128)(2,1)S(1)}, u32[]{:S(2)}, u32[]{:S(2)}) %all-to-all-start.1) | async-done | bytes 524320 | tf_op jit(solution)/shard_map/all_to_all | solution.py:89
  71.8 3.6 %all-to-all-start.2 = ((bf16[16,4,4096]{2,1,0:T(4,128)(2,1)}), bf16[16,4,4096]{2,1,0:T(4,128)(2,1)S(1)}, u32[]{:S(2)}, u32[]{:S(2)}) async-start(bf16[16,4,4096]{2,1,0:T(4,128)(2,1)} %all_to_all.41), calls=%async_computation.2 | async-start | bytes 1048576 | tf_op jit(solution)/shard_map/all_to_all | solution.py:75
  75.7 0.8 gather_fusion.2
  76.5 0.9 all_to_all.40
  77.4 1.5 pad_maximum_fusion
  78.9 2.2 gather_fusion.7
  81.1 5.1 %all-to-all-done.2 = bf16[16,4,4096]{2,1,0:T(4,128)(2,1)S(1)} async-done(((bf16[16,4,4096]{2,1,0:T(4,128)(2,1)}), bf16[16,4,4096]{2,1,0:T(4,128)(2,1)S(1)}, u32[]{:S(2)}, u32[]{:S(2)}) %all-to-all-start.2) | async-done | bytes 524320 | tf_op jit(solution)/shard_map/all_to_all | solution.py:75
  86.2 0.9 all_to_all.43
  87.1 1.5 pad_maximum_fusion.1
  88.6 2.2 gather_fusion.9
  90.7 1.8 broadcast_select_fusion
  92.6 1.2 copy.134
  93.8 3.0 %multiply_reduce_fusion = (f32[128]{0:T(128)S(1)}, f32[128,512]{1,0:T(8,128)S(1)}) fusion(bf16[128,4096]{1,0:T(8,128)(2,1)S(1)} %get-tuple-element.6, bf16[4096,512]{1,0:T(8,128)(2,1)} %all-gather.3.cloned.1.call-done, bf16[128,512]{1,0:T(8,128)(2,1)S(1)} %gather_fusion.2, pred[128]{0:T(512)(128)(4,1)S(1)} %get-tuple-element.8), kind=kOutput, calls=%fused_computation.46 | convolution fusion | flops 537198464 | bytes 5636736 | tf_op jit(solution)/shard_map/dot_general | solution.py:111
  97.1 12.7 %psum.7 = f32[128,9]{0,1:T(8,128)S(1)} all-reduce(f32[128,9]{0,1:T(8,128)S(1)} %pad_maximum_fusion.3), channel_id=1, replica_groups=mesh['req'=16,'exp'=8] {'exp'}, use_global_device_ids=true, to_apply=%region_6.9 | all-reduce | flops 1152 | bytes 9216 | tf_op jit(solution)/shard_map/psum | solution.py:120
  109.9 2.0 gather_fusion.4
  112.1 15.1 %all_to_all.54 = bf16[16,32,512]{2,1,0:T(8,128)(2,1)} all-to-all(bf16[16,32,512]{2,1,0:T(8,128)(2,1)S(1)} %select_select_fusion.3), channel_id=1, replica_groups=mesh['req'=16,'exp'=8] {'req'}, dimensions={0} | all-to-all | bytes 1048576 | tf_op jit(solution)/shard_map/all_to_all | solution.py:146
  127.3 27.4 %all-gather.5.cloned.1.call-done = bf16[512,4096]{1,0:T(8,128)(2,1)} async-done(((bf16[512,512]{1,0:T(8,128)(2,1)}), bf16[512,4096]{1,0:T(8,128)(2,1)}) %all-gather.5.cloned.1.call-update) | async-done | bytes 4194320 | tf_op jit(solution)/shard_map/all_gather | solution.py:147
  154.7 10.1 %fusion.4 = f32[512,896]{1,0:T(8,128)} fusion(bf16[512,4096]{1,0:T(8,128)(2,1)} %all-gather.5.cloned.1.call-done, bf16[1,4096,896]{2,1,0:T(8,128)(2,1)} %param.27), kind=kOutput, calls=%fused_computation.15 | convolution fusion | flops 3758096384 | bytes 13369344 | tf_op jit(solution)/shard_map/dot_general | solution.py:148
  164.9 16.6 %fusion.6 = bf16[512,4096]{1,0:T(8,128)(2,1)} fusion(bf16[1,896,4096]{2,1,0:T(8,128)(2,1)} %param.29, f32[512,896]{1,0:T(8,128)} %fusion.4, bf16[512,4096]{1,0:T(8,128)(2,1)} %all-gather.5.cloned.1.call-done, bf16[1,4096,896]{2,1,0:T(8,128)(2,1)} %param.28), kind=kOutput, calls=%fused_computation.17 | convolution fusion | flops 7521042432 | bytes 24903680 | tf_op jit(solution)/shard_map/dot_general | solution.py:152
  182.1 37.5 %reduce-scatter.2.cloned.1.call-done = bf16[512,512]{1,0:T(8,128)(2,1)} async-done(((bf16[512,4096]{1,0:T(8,128)(2,1)}), bf16[512,512]{1,0:T(8,128)(2,1)}) %reduce-scatter.2.cloned.1.call-update) | async-done | bytes 524304 | tf_op jit(solution)/shard_map/reduce_scatter | solution.py:154
  219.6 6.8 %all-to-all-start.4 = ((bf16[16,32,512]{2,1,0:T(8,128)(2,1)}), bf16[16,32,512]{2,1,0:T(8,128)(2,1)S(1)}, u32[]{:S(2)}, u32[]{:S(2)}) async-start(bf16[16,32,512]{2,1,0:T(8,128)(2,1)} %bitcast.83), calls=%async_computation.5 | async-start | bytes 1048576 | tf_op jit(solution)/shard_map/all_to_all | solution.py:156
  226.5 10.1 %all-to-all-done.4 = bf16[16,32,512]{2,1,0:T(8,128)(2,1)S(1)} async-done(((bf16[16,32,512]{2,1,0:T(8,128)(2,1)}), bf16[16,32,512]{2,1,0:T(8,128)(2,1)S(1)}, u32[]{:S(2)}, u32[]{:S(2)}) %all-to-all-start.4) | async-done | bytes 524320 | tf_op jit(solution)/shard_map/all_to_all | solution.py:156
  236.6 1.2 gather_fusion.5
  238.0 0.8 fusion.21
  (94 shorter events, 7.8 us)
Async XLA Ops:
  7.2 33.6 %copy-start = (bf16[256,8,256]{2,1,0:T(8,128)(2,1)S(1)}, bf16[256,8,256]{2,1,0:T(8,128)(2,1)}, u32[]{:S(2)}) copy-start(bf16[256,8,256]{2,1,0:T(8,128)(2,1)} %param.22) | copy-start | bytes 3145732
  7.2 86.6 %all-gather.3.cloned.1.call-start = ((), (), s32[]{:S(2)}) async-start(), calls=%async_computation.6 | async-start | bytes 4456448 | tf_op jit(solution)/shard_map/all_gather | solution.py:113
  23.1 29.5 %all-to-all-start = ((bf16[16,4,512]{2,1,0:T(4,128)(2,1)}), bf16[16,4,512]{2,1,0:T(4,128)(2,1)S(1)}, u32[]{:S(2)}, u32[]{:S(2)}) async-start(bf16[16,4,512]{2,1,0:T(4,128)(2,1)} %select_select_fusion.4), calls=%async_computation | async-start | bytes 131072 | tf_op jit(solution)/shard_map/all_to_all | solution.py:82
  31.2 12.9 %copy-start.2 = (bf16[128,4096]{1,0:T(8,128)(2,1)S(1)}, bf16[128,4096]{1,0:T(8,128)(2,1)}, u32[]{:S(2)}) copy-start(bf16[128,4096]{1,0:T(8,128)(2,1)} %param.17) | copy-start | bytes 3145732
  47.2 5.5 %copy-start.1 = (bf16[128,4096]{1,0:T(8,128)(2,1)}, bf16[128,4096]{1,0:T(8,128)(2,1)S(1)}, u32[]{:S(2)}) copy-start(bf16[128,4096]{1,0:T(8,128)(2,1)S(1)} %select_select_fusion) | copy-start | bytes 3145732
  47.2 1.4 copy-start.4
  48.1 27.5 %copy-start.3 = (bf16[128,512]{1,0:T(8,128)(2,1)S(1)}, bf16[128,512]{1,0:T(8,128)(2,1)}, u32[]{:S(2)}) copy-start(bf16[128,512]{1,0:T(8,128)(2,1)} %param.18) | copy-start | bytes 393220
  52.6 19.2 %all-to-all-start.1 = ((bf16[16,4,4096]{2,1,0:T(4,128)(2,1)}), bf16[16,4,4096]{2,1,0:T(4,128)(2,1)S(1)}, u32[]{:S(2)}, u32[]{:S(2)}) async-start(bf16[16,4,4096]{2,1,0:T(4,128)(2,1)} %all_to_all.38), calls=%async_computation.1 | async-start | bytes 1048576 | tf_op jit(solution)/shard_map/all_to_all | solution.py:89
  71.8 14.4 %all-to-all-start.2 = ((bf16[16,4,4096]{2,1,0:T(4,128)(2,1)}), bf16[16,4,4096]{2,1,0:T(4,128)(2,1)S(1)}, u32[]{:S(2)}, u32[]{:S(2)}) async-start(bf16[16,4,4096]{2,1,0:T(4,128)(2,1)} %all_to_all.41), calls=%async_computation.2 | async-start | bytes 1048576 | tf_op jit(solution)/shard_map/all_to_all | solution.py:75
  75.4 79.3 %all-gather.5.cloned.1.call-start = ((), (), s32[]{:S(2)}) async-start(), calls=%async_computation.7 | async-start | bytes 4718592 | tf_op jit(solution)/shard_map/all_gather | solution.py:147
  92.5 4.3 %copy-start.5 = (f32[512,8]{0,1:T(8,128)S(1)}, f32[512,8]{0,1:T(8,128)}, u32[]{:S(2)}) copy-start(f32[512,8]{0,1:T(8,128)} %param.20) | copy-start | bytes 49156
  92.6 4.3 %copy-start.7 = (f32[512]{0:T(512)S(1)}, f32[512]{0:T(512)}, u32[]{:S(2)}) copy-start(f32[512]{0:T(512)} %param.21) | copy-start | bytes 6148
  127.2 92.4 %reduce-scatter.2.cloned.1.call-start = ((), (), s32[]{:S(2)}) async-start(), calls=%async_computation.8 | async-start | bytes 4718592 | tf_op jit(solution)/shard_map/reduce_scatter | solution.py:154
  181.4 0.7 copy-start.6
  219.6 17.0 %all-to-all-start.4 = ((bf16[16,32,512]{2,1,0:T(8,128)(2,1)}), bf16[16,32,512]{2,1,0:T(8,128)(2,1)S(1)}, u32[]{:S(2)}, u32[]{:S(2)}) async-start(bf16[16,32,512]{2,1,0:T(8,128)(2,1)} %bitcast.83), calls=%async_computation.5 | async-start | bytes 1048576 | tf_op jit(solution)/shard_map/all_to_all | solution.py:156
Sparse Core Ops, SparseCore 0:
  10.2 57.1 all-gather.2
  127.3 27.3 all-gather.4
  181.6 38.0 reduce-scatter.1

commit v2 on v1

--- a/solution.py
+++ b/solution.py
@@ -60,18 +60,7 @@
     )
     send_index = jnp.sum(jnp.where(chosen_send, local_ids[None, None, :], 0), axis=2).reshape(-1)
     send_live = jnp.any(chosen_send, axis=2).reshape(-1)
-    page_rows = jnp.take(page_pool, page_table.reshape(-1), axis=0).reshape(
-        row_req, pages_req, page_len, kv_slice
-    )
-    position = (
-        jnp.arange(pages_req, dtype=jnp.int32)[:, None] * page_len
-        + jnp.arange(page_len, dtype=jnp.int32)[None, :]
-    )
-    kept_mask = position[None, :, :] < cache_len[:, None, None]
-    page_rows = jnp.where(kept_mask[..., None], page_rows, jnp.zeros((), page_rows.dtype)).reshape(
-        row_req, -1
-    )
-    moved_attn, moved_resid, moved_pages = (
+    moved_attn, moved_resid = (
         lax.all_to_all(
             pick_rows(attention_out, send_index, send_live),
             "req",
@@ -81,13 +70,6 @@
         ),
         lax.all_to_all(
             pick_rows(residual, send_index, send_live),
-            "req",
-            split_axis=0,
-            concat_axis=0,
-            tiled=True,
-        ),
-        lax.all_to_all(
-            pick_rows(page_rows, send_index, send_live),
             "req",
             split_axis=0,
             concat_axis=0,
@@ -104,10 +86,6 @@
     )
     attn_new = jnp.take(jnp.concatenate([attention_out, moved_attn], axis=0), arrival, axis=0)
     resid_new = jnp.take(jnp.concatenate([residual, moved_resid], axis=0), arrival, axis=0)
-    new_pages = jnp.take(
-        jnp.concatenate([page_rows, moved_pages], axis=0), arrival, axis=0
-    ).reshape(row_req, pages_req, page_len, kv_slice)
-    new_pages, attn_new = lax.optimization_barrier((new_pages, attn_new))
     projected = jnp.dot(
         attn_new,
         lax.all_gather(w_out, "req", axis=0, tiled=True),
@@ -144,14 +122,41 @@
     slot_live = jnp.any(chosen_slot, axis=2).reshape(-1)
     outgoing = pick_rows(normed_rows, slot_source, slot_live)
     arrived = lax.all_to_all(outgoing, "req", split_axis=0, concat_axis=0, tiled=True)
-    rows_full = lax.all_gather(arrived, "exp", axis=1, tiled=True)
-    gate_h = jnp.dot(rows_full, w_gate[0], preferred_element_type=jnp.float32)
-    up_h = jnp.dot(rows_full, w_up[0], preferred_element_type=jnp.float32)
-    active = (jax.nn.silu(gate_h) * up_h).astype(jnp.bfloat16)
-    partial_value = lax.optimization_barrier(
-        jnp.dot(active, w_down[0], preferred_element_type=jnp.float32).astype(jnp.bfloat16)
+    half = arrived.shape[0] // 2
+    summed_parts = []
+    for part in range(2):
+        rows_full = lax.all_gather(
+            arrived[part * half:(part + 1) * half], "exp", axis=1, tiled=True
+        )
+        gate_h = jnp.dot(rows_full, w_gate[0], preferred_element_type=jnp.float32)
+        up_h = jnp.dot(rows_full, w_up[0], preferred_element_type=jnp.float32)
+        active = (jax.nn.silu(gate_h) * up_h).astype(jnp.bfloat16)
+        partial_value = lax.optimization_barrier(
+            jnp.dot(active, w_down[0], preferred_element_type=jnp.float32).astype(jnp.bfloat16)
+        )
+        if part == 1:
+            partial_value, page_pool = lax.optimization_barrier((partial_value, page_pool))
+        summed_parts.append(
+            lax.psum_scatter(partial_value, "exp", scatter_dimension=1, tiled=True)
+        )
+    summed_value = jnp.concatenate(summed_parts, axis=0)
+    page_rows = jnp.take(page_pool, page_table.reshape(-1), axis=0).reshape(
+        row_req, pages_req, page_len, kv_slice
     )
-    summed_value = lax.psum_scatter(partial_value, "exp", scatter_dimension=1, tiled=True)
+    position = (
+        jnp.arange(pages_req, dtype=jnp.int32)[:, None] * page_len
+        + jnp.arange(page_len, dtype=jnp.int32)[None, :]
+    )
+    kept_mask = position[None, :, :] < cache_len[:, None, None]
+    page_rows = jnp.where(kept_mask[..., None], page_rows, jnp.zeros((), page_rows.dtype)).reshape(
+        row_req, -1
+    )
+    moved_pages = lax.all_to_all(
+        pick_rows(page_rows, send_index, send_live), "req", split_axis=0, concat_axis=0, tiled=True
+    )
+    new_pages = jnp.take(
+        jnp.concatenate([page_rows, moved_pages], axis=0), arrival, axis=0
+    ).reshape(row_req, pages_req, page_len, kv_slice)
     lookup = target_dev * CAP + slot_index
     returned = lax.all_to_all(summed_value, "req", split_axis=0, concat_axis=0, tiled=True)
     taken_rows = jnp.take(returned, lookup, axis=0).reshape(row_req, 2, -1).astype(jnp.float32)

time: 246 us -> 256 us (1.041)
  matrix products: 30 us -> 39.3 us
  local copies, waits for them, and re-layouts: 39.8 us -> 32.6 us
  waiting for transfers between devices: 90.3 us -> 93.8 us
  starting transfers between devices: 25 us -> 28.1 us
    reduce_scatter x1 -> x2, waiting for transfers between devices: 37.5 us -> 22.3 us  [body(): lax.psum_scatter(partial_value, 'exp', scatter_dimension=1, tiled=True)]
    all_to_all x1, waiting for transfers between devices: 5.09 us -> 16.4 us  [body(): lax.all_to_all(pick_rows(attention_out, send_index, send_live), 'req', sp...]
    dot_general x1 -> x2, matrix products: 16.6 us -> 23.5 us  [body(): jnp.dot(active, w_down[0], preferred_element_type=jnp.float32)]
    all_gather x1, waiting for transfers between devices: 0.01 us -> 3.42 us  [body(): lax.all_gather(w_out, 'req', axis=0, tiled=True)]
    all_to_all x1, starting transfers between devices: 3.57 us -> 6.97 us  [body(): lax.all_to_all(pick_rows(attention_out, send_index, send_live), 'req', sp...]
    all_gather x1 -> x2, waiting for transfers between devices: 27.4 us -> 30.5 us  [body(): lax.all_gather(arrived[part * half:(part + 1) * half], 'exp', axis=1, til...]
    all_to_all x1, waiting for transfers between devices: 10.1 us -> 7.51 us  [body(): lax.all_to_all(summed_value, 'req', split_axis=0, concat_axis=0, tiled=True)]
    dot_general x1 -> x2, matrix products: 10.1 us -> 12.1 us  [body(): gate_h = jnp.dot(rows_full, w_gate[0], preferred_element_type=jnp.float32)]
  transfers between devices with their start and end apart: 7 -> 9, of which waited for: 5 -> 8; matrix products, arithmetic and copies ran while one was open for 19% -> 30% of each run, Pallas kernels for 0% -> 0%
where the time goes in v2:
time: 256 us
  waiting for transfers between devices  93.8 us (37%)
  matrix products  39.3 us (15%)
  local copies, waits for them, and re-layouts  32.6 us (13%)
  blocking collectives  30.3 us (12%)
  starting transfers between devices  28.1 us (11%)
  other arithmetic  17.2 us (7%)
  between operations  14.3 us (6%)
    all_gather x2, waiting for transfers between devices, body(): lax.all_gather(arrived[part * half:(part + 1) * half], 'exp', axis=1, til...  30.5 us
    dot_general x2, matrix products, body(): jnp.dot(active, w_down[0], preferred_element_type=jnp.float32)  23.5 us
    reduce_scatter x2, waiting for transfers between devices, body(): lax.psum_scatter(partial_value, 'exp', scatter_dimension=1, tiled=True)  22.3 us
    all_to_all x1, waiting for transfers between devices, body(): lax.all_to_all(pick_rows(attention_out, send_index, send_live), 'req', sp...  16.4 us
    all_to_all x1, blocking collectives, body(): lax.all_to_all(outgoing, 'req', split_axis=0, concat_axis=0, tiled=True)  15.2 us
    psum x1, blocking collectives, body(): lax.psum(jnp.concatenate([squares[:, None], raw_logits], axis=1), 'exp')  15.1 us
    dot_general x2, matrix products, body(): gate_h = jnp.dot(rows_full, w_gate[0], preferred_element_type=jnp.float32)  12.1 us
    all_to_all x1, waiting for transfers between devices, body(): lax.all_to_all(pick_rows(page_rows, send_index, send_live), 'req', split_...  11.9 us
  transfers between devices with their start and end apart: 9, of which 8 were waited for; matrix products, arithmetic and copies ran while one was open for 30% of the time, Pallas kernels for 0%

profile of v2, /device:TPU:0, one launch (start us, length us, event | category | flops | bytes accessed | tf_op | source)
XLA Modules:
  0.0 255.6 jit_solution(9440138711308423616)
XLA Ops:
  7.2 0.7 all-gather.4.cloned.1.call-update
  7.9 0.7 compare_select_fusion.1
  8.6 8.0 %scatter_custom_fusion = s32[2048]{0:T(1024)S(1)} fusion(s32[2048]{0:T(1024)S(1)} %compare_select_fusion.1, s32[2048]{0:T(1024)S(1)} %iota.72, s32[]{:T(128)} %constant.183.clone.1), kind=kCustom, calls=%fused_computation.106 | custom fusion | bytes 8196 | tf_op jit(solution)/shard_map/scatter | solution.py:45
  16.8 2.8 %select_reduce_fusion = s32[16,128]{0,1:T(8,128)S(1)} fusion(s32[16,128]{0,1:T(8,128)S(1)} %copy.115), kind=kOutput, calls=%fused_computation.37 | output fusion | flops 4388864 | bytes 16384 | tf_op jit(solution)/shard_map/jit(cumsum)/reduce_window_sum | solution.py:51
  20.6 1.6 gather_fusion.1
  22.4 0.8 select_select_fusion.4
  23.1 7.1 %all-to-all-start = ((bf16[16,4,512]{2,1,0:T(4,128)(2,1)}), bf16[16,4,512]{2,1,0:T(4,128)(2,1)S(1)}, u32[]{:S(2)}, u32[]{:S(2)}) async-start(bf16[16,4,512]{2,1,0:T(4,128)(2,1)} %select_select_fusion.4), calls=%async_computation | async-start | bytes 131072 | tf_op jit(solution)/shard_map/all_to_all | solution.py:71
  30.4 0.8 copy.122
  31.5 0.9 gather_fusion.6
  32.6 1.0 all_to_all.36
  33.6 0.8 compare_select_fusion.15
  34.3 1.1 gather_fusion
  36.9 0.8 compare_and_fusion.5
  38.0 7.0 %all-to-all-start.1 = ((bf16[16,4,4096]{2,1,0:T(4,128)(2,1)}), bf16[16,4,4096]{2,1,0:T(4,128)(2,1)S(1)}, u32[]{:S(2)}, u32[]{:S(2)}) async-start(bf16[16,4,4096]{2,1,0:T(4,128)(2,1)} %all_to_all.36), calls=%async_computation.1 | async-start | bytes 1048576 | tf_op jit(solution)/shard_map/all_to_all | solution.py:64
  45.5 0.8 gather_fusion.2
  46.3 16.4 %all-to-all-done.1 = bf16[16,4,4096]{2,1,0:T(4,128)(2,1)S(1)} async-done(((bf16[16,4,4096]{2,1,0:T(4,128)(2,1)}), bf16[16,4,4096]{2,1,0:T(4,128)(2,1)S(1)}, u32[]{:S(2)}, u32[]{:S(2)}) %all-to-all-start.1) | async-done | bytes 524320 | tf_op jit(solution)/shard_map/all_to_all | solution.py:64
  62.9 1.4 pad_maximum_fusion
  64.2 2.2 gather_fusion.7
  66.4 3.4 %all-gather.4.cloned.1.call-done = bf16[4096,512]{1,0:T(8,128)(2,1)} async-done(((bf16[256,512]{1,0:T(8,128)(2,1)}), bf16[4096,512]{1,0:T(8,128)(2,1)}) %all-gather.4.cloned.1.call-update) | async-done | bytes 4194320 | tf_op jit(solution)/shard_map/all_gather | solution.py:91
  69.8 3.4 %multiply_reduce_fusion = (f32[128]{0:T(128)S(1)}, f32[128,512]{1,0:T(8,128)S(1)}) fusion(bf16[4096,512]{1,0:T(8,128)(2,1)} %all-gather.4.cloned.1.call-done, bf16[128,4096]{1,0:T(8,128)(2,1)} %gather_fusion.7, pred[128]{0:T(512)(128)(4,1)S(1)} %get-tuple-element.8, bf16[128,512]{1,0:T(8,128)(2,1)S(1)} %gather_fusion.2), kind=kOutput, calls=%fused_computation.61 | convolution fusion | flops 537722752 | bytes 5636736 | tf_op jit(solution)/shard_map/dot_general | solution.py:89
  73.5 15.1 %psum.7 = f32[128,9]{0,1:T(8,128)S(1)} all-reduce(f32[128,9]{0,1:T(8,128)S(1)} %pad_maximum_fusion.4), channel_id=1, replica_groups=mesh['req'=16,'exp'=8] {'exp'}, use_global_device_ids=true, to_apply=%region_6.9 | all-reduce | flops 1152 | bytes 9216 | tf_op jit(solution)/shard_map/psum | solution.py:98
  88.7 2.0 gather_fusion.3
  90.9 15.2 %all_to_all.51 = bf16[16,32,512]{2,1,0:T(8,128)(2,1)S(1)} all-to-all(bf16[16,32,512]{2,1,0:T(8,128)(2,1)S(1)} %select_select_fusion.3), channel_id=1, replica_groups=mesh['req'=16,'exp'=8] {'req'}, dimensions={0} | all-to-all | bytes 1048576 | tf_op jit(solution)/shard_map/all_to_all | solution.py:124
  106.1 0.8 fusion.77
  107.9 20.7 %all-gather.8.cloned.1.call-done = bf16[256,4096]{1,0:T(8,128)(2,1)} async-done(((bf16[256,512]{1,0:T(8,128)(2,1)}), bf16[256,4096]{1,0:T(8,128)(2,1)}) %all-gather.8.cloned.1.call-update) | async-done | bytes 2097168 | tf_op jit(solution)/shard_map/all_gather | solution.py:128
  128.6 6.1 %fusion.8 = f32[256,896]{1,0:T(8,128)S(1)} fusion(bf16[256,4096]{1,0:T(8,128)(2,1)} %all-gather.8.cloned.1.call-done, bf16[1,4096,896]{2,1,0:T(8,128)(2,1)} %param.27), kind=kOutput, calls=%fused_computation.19 | convolution fusion | flops 1879048192 | bytes 10354688 | tf_op jit(solution)/shard_map/dot_general | solution.py:131
  134.7 11.7 %fusion.15 = bf16[256,4096]{1,0:T(8,128)(2,1)} fusion(bf16[1,896,4096]{2,1,0:T(8,128)(2,1)} %param.29, bf16[256,4096]{1,0:T(8,128)(2,1)} %all-gather.8.cloned.1.call-done, bf16[1,4096,896]{2,1,0:T(8,128)(2,1)} %param.28, f32[256,896]{1,0:T(8,128)S(1)} %fusion.8), kind=kOutput, calls=%fused_computation.24 | convolution fusion | flops 3760521216 | bytes 19791872 | tf_op jit(solution)/shard_map/dot_general | solution.py:135
  146.9 9.8 %all-gather.6.cloned.1.call-done = bf16[256,4096]{1,0:T(8,128)(2,1)} async-done(((bf16[256,512]{1,0:T(8,128)(2,1)}), bf16[256,4096]{1,0:T(8,128)(2,1)}) %all-gather.6.cloned.1.call-update) | async-done | bytes 2097168 | tf_op jit(solution)/shard_map/all_gather | solution.py:128
  156.7 6.1 %fusion.10 = f32[256,896]{1,0:T(8,128)S(1)} fusion(bf16[256,4096]{1,0:T(8,128)(2,1)} %all-gather.6.cloned.1.call-done, bf16[1,4096,896]{2,1,0:T(8,128)(2,1)} %param.27), kind=kOutput, calls=%fused_computation.21 | convolution fusion | flops 1879048192 | bytes 10354688 | tf_op jit(solution)/shard_map/dot_general | solution.py:131
  162.8 11.8 %fusion.12 = bf16[256,4096]{1,0:T(8,128)(2,1)} fusion(bf16[1,896,4096]{2,1,0:T(8,128)(2,1)} %param.29, bf16[256,4096]{1,0:T(8,128)(2,1)} %all-gather.6.cloned.1.call-done, bf16[1,4096,896]{2,1,0:T(8,128)(2,1)} %param.28, f32[256,896]{1,0:T(8,128)S(1)} %fusion.10), kind=kOutput, calls=%fused_computation.23 | convolution fusion | flops 3760521216 | bytes 19791872 | tf_op jit(solution)/shard_map/dot_general | solution.py:135
  175.3 1.1 copy.132
  177.1 1.1 copy.133
  178.4 0.8 gather_fusion.5
  179.7 1.4 select_select_fusion
  181.1 0.9 gather_fusion.8
  182.2 1.0 all_to_all.43
  183.1 6.8 %all-to-all-start.4 = ((bf16[16,4,4096]{2,1,0:T(4,128)(2,1)}), bf16[16,4,4096]{2,1,0:T(4,128)(2,1)S(1)}, u32[]{:S(2)}, u32[]{:S(2)}) async-start(bf16[16,4,4096]{2,1,0:T(4,128)(2,1)} %all_to_all.43), calls=%async_computation.6 | async-start | bytes 1048576 | tf_op jit(solution)/shard_map/all_to_all | solution.py:154
  190.0 11.9 %all-to-all-done.4 = bf16[16,4,4096]{2,1,0:T(4,128)(2,1)S(1)} async-done(((bf16[16,4,4096]{2,1,0:T(4,128)(2,1)}), bf16[16,4,4096]{2,1,0:T(4,128)(2,1)S(1)}, u32[]{:S(2)}, u32[]{:S(2)}) %all-to-all-start.4) | async-done | bytes 524320 | tf_op jit(solution)/shard_map/all_to_all | solution.py:154
  202.0 1.5 pad_maximum_fusion.1
  203.5 2.2 gather_fusion.9
  205.7 22.3 %reduce-scatter.3.cloned.1.call-done = bf16[256,512]{1,0:T(8,128)(2,1)} async-done(((bf16[256,4096]{1,0:T(8,128)(2,1)}), bf16[256,512]{1,0:T(8,128)(2,1)}) %reduce-scatter.3.cloned.1.call-update) | async-done | bytes 262160 | tf_op jit(solution)/shard_map/reduce_scatter | solution.py:140
  228.0 1.9 pad_maximum_fusion.2
  229.9 6.8 %all-to-all-start.3 = ((bf16[16,32,512]{2,1,0:T(8,128)(2,1)}), bf16[16,32,512]{2,1,0:T(8,128)(2,1)S(1)}, u32[]{:S(2)}, u32[]{:S(2)}) async-start(bf16[16,32,512]{2,1,0:T(8,128)(2,1)} %bitcast.15), calls=%async_computation.5 | async-start | bytes 1048576 | tf_op jit(solution)/shard_map/all_to_all | solution.py:161
  236.7 1.4 broadcast_select_fusion
  238.1 1.2 copy.134
  239.3 7.5 %all-to-all-done.3 = bf16[16,32,512]{2,1,0:T(8,128)(2,1)S(1)} async-done(((bf16[16,32,512]{2,1,0:T(8,128)(2,1)}), bf16[16,32,512]{2,1,0:T(8,128)(2,1)S(1)}, u32[]{:S(2)}, u32[]{:S(2)}) %all-to-all-start.3) | async-done | bytes 524320 | tf_op jit(solution)/shard_map/all_to_all | solution.py:161
  246.8 1.2 gather_fusion.4
  248.2 0.8 fusion.47
  (107 shorter events, 8.8 us)
Async XLA Ops:
  7.2 171.2 %copy-start = (bf16[256,8,256]{2,1,0:T(8,128)(2,1)S(1)}, bf16[256,8,256]{2,1,0:T(8,128)(2,1)}, u32[]{:S(2)}) copy-start(bf16[256,8,256]{2,1,0:T(8,128)(2,1)} %param.22) | copy-start | bytes 3145732
  7.2 24.4 %copy-start.2 = (bf16[128,4096]{1,0:T(8,128)(2,1)S(1)}, bf16[128,4096]{1,0:T(8,128)(2,1)}, u32[]{:S(2)}) copy-start(bf16[128,4096]{1,0:T(8,128)(2,1)} %param.17) | copy-start | bytes 3145732
  7.2 62.6 %all-gather.4.cloned.1.call-start = ((), (), s32[]{:S(2)}) async-start(), calls=%async_computation.7 | async-start | bytes 4456448 | tf_op jit(solution)/shard_map/all_gather | solution.py:91
  23.1 14.9 %all-to-all-start = ((bf16[16,4,512]{2,1,0:T(4,128)(2,1)}), bf16[16,4,512]{2,1,0:T(4,128)(2,1)S(1)}, u32[]{:S(2)}, u32[]{:S(2)}) async-start(bf16[16,4,512]{2,1,0:T(4,128)(2,1)} %select_select_fusion.4), calls=%async_computation | async-start | bytes 131072 | tf_op jit(solution)/shard_map/all_to_all | solution.py:71
  32.4 13.0 %copy-start.3 = (bf16[128,512]{1,0:T(8,128)(2,1)S(1)}, bf16[128,512]{1,0:T(8,128)(2,1)}, u32[]{:S(2)}) copy-start(bf16[128,512]{1,0:T(8,128)(2,1)} %param.18) | copy-start | bytes 393220
  38.0 24.7 %all-to-all-start.1 = ((bf16[16,4,4096]{2,1,0:T(4,128)(2,1)}), bf16[16,4,4096]{2,1,0:T(4,128)(2,1)S(1)}, u32[]{:S(2)}, u32[]{:S(2)}) async-start(bf16[16,4,4096]{2,1,0:T(4,128)(2,1)} %all_to_all.36), calls=%async_computation.1 | async-start | bytes 1048576 | tf_op jit(solution)/shard_map/all_to_all | solution.py:64
  45.0 83.7 %all-gather.8.cloned.1.call-start = ((), (), s32[]{:S(2)}) async-start(), calls=%async_computation.10 | async-start | bytes 2359296 | tf_op jit(solution)/shard_map/all_gather | solution.py:128
  66.4 6.8 %copy-start.4 = (f32[512,8]{0,1:T(8,128)S(1)}, f32[512,8]{0,1:T(8,128)}, u32[]{:S(2)}) copy-start(f32[512,8]{0,1:T(8,128)} %param.20) | copy-start | bytes 49156
  66.4 6.8 %copy-start.6 = (f32[512]{0:T(512)S(1)}, f32[512]{0:T(512)}, u32[]{:S(2)}) copy-start(f32[512]{0:T(512)} %param.21) | copy-start | bytes 6148
  106.9 49.8 %all-gather.6.cloned.1.call-start = ((), (), s32[]{:S(2)}) async-start(), calls=%async_computation.8 | async-start | bytes 2359296 | tf_op jit(solution)/shard_map/all_gather | solution.py:128
  107.7 98.0 %reduce-scatter.5.cloned.1.call-start = ((), (), s32[]{:S(2)}) async-start(), calls=%async_computation.11 | async-start | bytes 2359296 | tf_op jit(solution)/shard_map/reduce_scatter | solution.py:140
  146.5 81.5 %reduce-scatter.3.cloned.1.call-start = ((), (), s32[]{:S(2)}) async-start(), calls=%async_computation.9 | async-start | bytes 2359296 | tf_op jit(solution)/shard_map/reduce_scatter | solution.py:140
  162.8 11.8 %copy-start.8 = (s32[128]{0:T(128)S(1)}, s32[128]{0:T(128)}, u32[]{:S(2)}) copy-start(s32[128]{0:T(128)} %param.24) | copy-start | bytes 1540
  174.6 1.8 copy-start.7
  174.6 3.8 %copy-start.5 = (s32[128,2]{0,1:T(2,128)S(1)}, s32[128,2]{0,1:T(2,128)}, u32[]{:S(2)}) copy-start(s32[128,2]{0,1:T(2,128)} %param.26) | copy-start | bytes 3076
  181.1 2.0 copy-start.1
  183.1 18.8 %all-to-all-start.4 = ((bf16[16,4,4096]{2,1,0:T(4,128)(2,1)}), bf16[16,4,4096]{2,1,0:T(4,128)(2,1)S(1)}, u32[]{:S(2)}, u32[]{:S(2)}) async-start(bf16[16,4,4096]{2,1,0:T(4,128)(2,1)} %all_to_all.43), calls=%async_computation.6 | async-start | bytes 1048576 | tf_op jit(solution)/shard_map/all_to_all | solution.py:154
  229.9 17.0 %all-to-all-start.3 = ((bf16[16,32,512]{2,1,0:T(8,128)(2,1)}), bf16[16,32,512]{2,1,0:T(8,128)(2,1)S(1)}, u32[]{:S(2)}, u32[]{:S(2)}) async-start(bf16[16,32,512]{2,1,0:T(8,128)(2,1)} %bitcast.15), calls=%async_computation.5 | async-start | bytes 1048576 | tf_op jit(solution)/shard_map/all_to_all | solution.py:161
Sparse Core Ops, SparseCore 0:
  10.2 59.6 all-gather.3
  107.1 21.5 all-gather.7
  130.9 25.7 all-gather.5
  159.0 34.1 reduce-scatter.4
  195.5 32.5 reduce-scatter.2

commit v3 on v2

--- a/solution.py
+++ b/solution.py
@@ -122,24 +122,15 @@
     slot_live = jnp.any(chosen_slot, axis=2).reshape(-1)
     outgoing = pick_rows(normed_rows, slot_source, slot_live)
     arrived = lax.all_to_all(outgoing, "req", split_axis=0, concat_axis=0, tiled=True)
-    half = arrived.shape[0] // 2
-    summed_parts = []
-    for part in range(2):
-        rows_full = lax.all_gather(
-            arrived[part * half:(part + 1) * half], "exp", axis=1, tiled=True
-        )
-        gate_h = jnp.dot(rows_full, w_gate[0], preferred_element_type=jnp.float32)
-        up_h = jnp.dot(rows_full, w_up[0], preferred_element_type=jnp.float32)
-        active = (jax.nn.silu(gate_h) * up_h).astype(jnp.bfloat16)
-        partial_value = lax.optimization_barrier(
-            jnp.dot(active, w_down[0], preferred_element_type=jnp.float32).astype(jnp.bfloat16)
-        )
-        if part == 1:
-            partial_value, page_pool = lax.optimization_barrier((partial_value, page_pool))
-        summed_parts.append(
-            lax.psum_scatter(partial_value, "exp", scatter_dimension=1, tiled=True)
-        )
-    summed_value = jnp.concatenate(summed_parts, axis=0)
+    rows_full = lax.all_gather(arrived, "exp", axis=1, tiled=True)
+    gate_h = jnp.dot(rows_full, w_gate[0], preferred_element_type=jnp.float32)
+    up_h = jnp.dot(rows_full, w_up[0], preferred_element_type=jnp.float32)
+    active = (jax.nn.silu(gate_h) * up_h).astype(jnp.bfloat16)
+    partial_value = lax.optimization_barrier(
+        jnp.dot(active, w_down[0], preferred_element_type=jnp.float32).astype(jnp.bfloat16)
+    )
+    partial_value, page_pool = lax.optimization_barrier((partial_value, page_pool))
+    summed_value = lax.psum_scatter(partial_value, "exp", scatter_dimension=1, tiled=True)
     page_rows = jnp.take(page_pool, page_table.reshape(-1), axis=0).reshape(
         row_req, pages_req, page_len, kv_slice
     )

time: 256 us -> 226 us (0.88)
  waiting for transfers between devices: 93.8 us -> 75.2 us
  matrix products: 39.3 us -> 29.7 us
    reduce_scatter x2 -> x1, waiting for transfers between devices: 22.3 us -> 6.57 us  [body(): lax.psum_scatter(partial_value, 'exp', scatter_dimension=1, tiled=True)]
    dot_general x2 -> x1, matrix products: 23.5 us -> 16.2 us  [body(): jnp.dot(active, w_down[0], preferred_element_type=jnp.float32)]
    dot_general x2 -> x1, matrix products: 12.1 us -> 9.79 us  [body(): gate_h = jnp.dot(rows_full, w_gate[0], preferred_element_type=jnp.float32)]
    all_gather x2 -> x1, waiting for transfers between devices: 30.5 us -> 28.4 us  [body(): rows_full = lax.all_gather(arrived, 'exp', axis=1, tiled=True)]
  transfers between devices with their start and end apart: 9 -> 7, of which waited for: 8 -> 7; matrix products, arithmetic and copies ran while one was open for 30% -> 18% of each run, Pallas kernels for 0% -> 0%
where the time goes in v3:
time: 226 us; the launch traced here: 225 us
  waiting for transfers between devices  75.2 us (33%)
  local copies, waits for them, and re-layouts  32.2 us (14%)
  blocking collectives  30.4 us (13%)
  matrix products  29.7 us (13%)
  starting transfers between devices  27.9 us (12%)
  other arithmetic  15.3 us (7%)
  between operations  14.3 us (6%)
    all_gather x1, waiting for transfers between devices, body(): rows_full = lax.all_gather(arrived, 'exp', axis=1, tiled=True)  28.4 us
    all_to_all x1, waiting for transfers between devices, body(): lax.all_to_all(pick_rows(attention_out, send_index, send_live), 'req', sp...  16.4 us
    dot_general x1, matrix products, body(): jnp.dot(active, w_down[0], preferred_element_type=jnp.float32)  16.2 us
    all_to_all x1, blocking collectives, body(): lax.all_to_all(outgoing, 'req', split_axis=0, concat_axis=0, tiled=True)  15.3 us
    psum x1, blocking collectives, body(): lax.psum(jnp.concatenate([squares[:, None], raw_logits], axis=1), 'exp')  15.1 us
    all_to_all x1, waiting for transfers between devices, body(): lax.all_to_all(pick_rows(page_rows, send_index, send_live), 'req', split_...  11.9 us
    dot_general x1, matrix products, body(): gate_h = jnp.dot(rows_full, w_gate[0], preferred_element_type=jnp.float32)  9.79 us
    scatter x1, local copies, waits for them, and re-layouts, body(): jnp.zeros((rows_all,), jnp.int32).at[came_from]  8.04 us
  transfers between devices with their start and end apart: 7, of which 7 were waited for; matrix products, arithmetic and copies ran while one was open for 18% of the time, Pallas kernels for 0%

profile of v3, /device:TPU:0, one launch (start us, length us, event | category | flops | bytes accessed | tf_op | source)
XLA Modules:
  0.0 224.9 jit_solution(11997066119131765174)
XLA Ops:
  7.2 0.7 all-gather.3.cloned.1.call-update
  7.9 0.7 compare_select_fusion.1
  8.6 8.0 %scatter_custom_fusion = s32[2048]{0:T(1024)S(1)} fusion(s32[2048]{0:T(1024)S(1)} %compare_select_fusion.1, s32[2048]{0:T(1024)S(1)} %iota.72, s32[]{:T(128)} %constant.182.clone.1), kind=kCustom, calls=%fused_computation.93 | custom fusion | bytes 8196 | tf_op jit(solution)/shard_map/scatter | solution.py:45
  16.8 2.8 %select_reduce_fusion = s32[16,128]{0,1:T(8,128)S(1)} fusion(s32[16,128]{0,1:T(8,128)S(1)} %copy.115), kind=kOutput, calls=%fused_computation.27 | output fusion | flops 4388864 | bytes 16384 | tf_op jit(solution)/shard_map/jit(cumsum)/reduce_window_sum | solution.py:51
  20.6 1.6 gather_fusion.1
  22.4 0.8 select_select_fusion.4
  23.1 7.1 %all-to-all-start = ((bf16[16,4,512]{2,1,0:T(4,128)(2,1)}), bf16[16,4,512]{2,1,0:T(4,128)(2,1)S(1)}, u32[]{:S(2)}, u32[]{:S(2)}) async-start(bf16[16,4,512]{2,1,0:T(4,128)(2,1)} %select_select_fusion.4), calls=%async_computation | async-start | bytes 131072 | tf_op jit(solution)/shard_map/all_to_all | solution.py:71
  30.4 0.8 copy.122
  31.6 0.9 gather_fusion.6
  32.6 1.0 all_to_all.38
  33.6 0.8 compare_select_fusion.15
  34.3 1.1 gather_fusion
  35.5 0.6 reduce-window.6
  36.9 0.8 compare_and_fusion.5
  38.0 7.0 %all-to-all-start.1 = ((bf16[16,4,4096]{2,1,0:T(4,128)(2,1)}), bf16[16,4,4096]{2,1,0:T(4,128)(2,1)S(1)}, u32[]{:S(2)}, u32[]{:S(2)}) async-start(bf16[16,4,4096]{2,1,0:T(4,128)(2,1)} %all_to_all.38), calls=%async_computation.1 | async-start | bytes 1048576 | tf_op jit(solution)/shard_map/all_to_all | solution.py:64
  45.5 0.8 gather_fusion.2
  46.3 16.4 %all-to-all-done.1 = bf16[16,4,4096]{2,1,0:T(4,128)(2,1)S(1)} async-done(((bf16[16,4,4096]{2,1,0:T(4,128)(2,1)}), bf16[16,4,4096]{2,1,0:T(4,128)(2,1)S(1)}, u32[]{:S(2)}, u32[]{:S(2)}) %all-to-all-start.1) | async-done | bytes 524320 | tf_op jit(solution)/shard_map/all_to_all | solution.py:64
  62.9 1.4 pad_maximum_fusion
  64.2 2.2 gather_fusion.7
  66.4 3.4 %all-gather.3.cloned.1.call-done = bf16[4096,512]{1,0:T(8,128)(2,1)} async-done(((bf16[256,512]{1,0:T(8,128)(2,1)}), bf16[4096,512]{1,0:T(8,128)(2,1)}) %all-gather.3.cloned.1.call-update) | async-done | bytes 4194320 | tf_op jit(solution)/shard_map/all_gather | solution.py:91
  69.8 3.4 %multiply_reduce_fusion = (f32[128]{0:T(128)S(1)}, f32[128,512]{1,0:T(8,128)S(1)}) fusion(bf16[4096,512]{1,0:T(8,128)(2,1)} %all-gather.3.cloned.1.call-done, bf16[128,4096]{1,0:T(8,128)(2,1)} %gather_fusion.7, pred[128]{0:T(512)(128)(4,1)S(1)} %get-tuple-element.8, bf16[128,512]{1,0:T(8,128)(2,1)S(1)} %gather_fusion.2), kind=kOutput, calls=%fused_computation.48 | convolution fusion | flops 537722752 | bytes 5636736 | tf_op jit(solution)/shard_map/dot_general | solution.py:89
  73.5 15.1 %psum.7 = f32[128,9]{0,1:T(8,128)S(1)} all-reduce(f32[128,9]{0,1:T(8,128)S(1)} %pad_maximum_fusion.3), channel_id=1, replica_groups=mesh['req'=16,'exp'=8] {'exp'}, use_global_device_ids=true, to_apply=%region_6.9 | all-reduce | flops 1152 | bytes 9216 | tf_op jit(solution)/shard_map/psum | solution.py:98
  88.7 2.0 gather_fusion.3
  90.9 15.3 %all_to_all.54 = bf16[16,32,512]{2,1,0:T(8,128)(2,1)} all-to-all(bf16[16,32,512]{2,1,0:T(8,128)(2,1)S(1)} %select_select_fusion.3), channel_id=1, replica_groups=mesh['req'=16,'exp'=8] {'req'}, dimensions={0} | all-to-all | bytes 1048576 | tf_op jit(solution)/shard_map/all_to_all | solution.py:124
  106.4 28.4 %all-gather.5.cloned.1.call-done = bf16[512,4096]{1,0:T(8,128)(2,1)} async-done(((bf16[512,512]{1,0:T(8,128)(2,1)}), bf16[512,4096]{1,0:T(8,128)(2,1)}) %all-gather.5.cloned.1.call-update) | async-done | bytes 4194320 | tf_op jit(solution)/shard_map/all_gather | solution.py:125
  134.9 9.8 %fusion.4 = f32[512,896]{1,0:T(8,128)S(1)} fusion(bf16[512,4096]{1,0:T(8,128)(2,1)} %all-gather.5.cloned.1.call-done, bf16[1,4096,896]{2,1,0:T(8,128)(2,1)} %param.27), kind=kOutput, calls=%fused_computation.15 | convolution fusion | flops 3758096384 | bytes 13369344 | tf_op jit(solution)/shard_map/dot_general | solution.py:126
  144.7 16.2 %fusion.6 = bf16[512,4096]{1,0:T(8,128)(2,1)} fusion(bf16[1,896,4096]{2,1,0:T(8,128)(2,1)} %param.29, f32[512,896]{1,0:T(8,128)S(1)} %fusion.4, bf16[512,4096]{1,0:T(8,128)(2,1)} %all-gather.5.cloned.1.call-done, bf16[1,4096,896]{2,1,0:T(8,128)(2,1)} %param.28), kind=kOutput, calls=%fused_computation.17 | convolution fusion | flops 7521042432 | bytes 24903680 | tf_op jit(solution)/shard_map/dot_general | solution.py:130
  161.2 0.4 copy-done.7
  162.1 0.4 broadcast_in_dim.231
  162.6 1.1 copy.132
  163.8 0.4 broadcast_in_dim.233
  164.3 1.1 copy.133
  165.6 0.8 gather_fusion.5
  166.3 0.5 gather.47
  166.9 1.4 select_select_fusion
  168.3 0.9 gather_fusion.8
  169.3 1.0 all_to_all.46
  170.3 6.8 %all-to-all-start.4 = ((bf16[16,4,4096]{2,1,0:T(4,128)(2,1)}), bf16[16,4,4096]{2,1,0:T(4,128)(2,1)S(1)}, u32[]{:S(2)}, u32[]{:S(2)}) async-start(bf16[16,4,4096]{2,1,0:T(4,128)(2,1)} %all_to_all.46), calls=%async_computation.5 | async-start | bytes 1048576 | tf_op jit(solution)/shard_map/all_to_all | solution.py:145
  177.2 11.9 %all-to-all-done.4 = bf16[16,4,4096]{2,1,0:T(4,128)(2,1)S(1)} async-done(((bf16[16,4,4096]{2,1,0:T(4,128)(2,1)}), bf16[16,4,4096]{2,1,0:T(4,128)(2,1)S(1)}, u32[]{:S(2)}, u32[]{:S(2)}) %all-to-all-start.4) | async-done | bytes 524320 | tf_op jit(solution)/shard_map/all_to_all | solution.py:145
  189.2 1.4 pad_maximum_fusion.1
  190.6 2.2 gather_fusion.9
  192.8 6.6 %reduce-scatter.2.cloned.1.call-done = bf16[512,512]{1,0:T(8,128)(2,1)} async-done(((bf16[512,4096]{1,0:T(8,128)(2,1)}), bf16[512,512]{1,0:T(8,128)(2,1)}) %reduce-scatter.2.cloned.1.call-update) | async-done | bytes 524304 | tf_op jit(solution)/shard_map/reduce_scatter | solution.py:133
  199.3 6.7 %all-to-all-start.3 = ((bf16[16,32,512]{2,1,0:T(8,128)(2,1)}), bf16[16,32,512]{2,1,0:T(8,128)(2,1)S(1)}, u32[]{:S(2)}, u32[]{:S(2)}) async-start(bf16[16,32,512]{2,1,0:T(8,128)(2,1)} %bitcast.81), calls=%async_computation.4 | async-start | bytes 1048576 | tf_op jit(solution)/shard_map/all_to_all | solution.py:152
  206.0 1.4 broadcast_select_fusion
  207.4 1.2 copy.134
  208.6 7.5 %all-to-all-done.3 = bf16[16,32,512]{2,1,0:T(8,128)(2,1)S(1)} async-done(((bf16[16,32,512]{2,1,0:T(8,128)(2,1)}), bf16[16,32,512]{2,1,0:T(8,128)(2,1)S(1)}, u32[]{:S(2)}, u32[]{:S(2)}) %all-to-all-start.3) | async-done | bytes 524320 | tf_op jit(solution)/shard_map/all_to_all | solution.py:152
  216.1 1.2 gather_fusion.4
  217.5 0.8 fusion.24
  (97 shorter events, 6.0 us)
Async XLA Ops:
  7.2 158.4 %copy-start = (bf16[256,8,256]{2,1,0:T(8,128)(2,1)S(1)}, bf16[256,8,256]{2,1,0:T(8,128)(2,1)}, u32[]{:S(2)}) copy-start(bf16[256,8,256]{2,1,0:T(8,128)(2,1)} %param.22) | copy-start | bytes 3145732
  7.2 24.4 %copy-start.2 = (bf16[128,4096]{1,0:T(8,128)(2,1)S(1)}, bf16[128,4096]{1,0:T(8,128)(2,1)}, u32[]{:S(2)}) copy-start(bf16[128,4096]{1,0:T(8,128)(2,1)} %param.17) | copy-start | bytes 3145732
  7.2 62.6 %all-gather.3.cloned.1.call-start = ((), (), s32[]{:S(2)}) async-start(), calls=%async_computation.6 | async-start | bytes 4456448 | tf_op jit(solution)/shard_map/all_gather | solution.py:91
  23.1 14.9 %all-to-all-start = ((bf16[16,4,512]{2,1,0:T(4,128)(2,1)}), bf16[16,4,512]{2,1,0:T(4,128)(2,1)S(1)}, u32[]{:S(2)}, u32[]{:S(2)}) async-start(bf16[16,4,512]{2,1,0:T(4,128)(2,1)} %select_select_fusion.4), calls=%async_computation | async-start | bytes 131072 | tf_op jit(solution)/shard_map/all_to_all | solution.py:71
  31.5 13.9 %copy-start.3 = (bf16[128,512]{1,0:T(8,128)(2,1)S(1)}, bf16[128,512]{1,0:T(8,128)(2,1)}, u32[]{:S(2)}) copy-start(bf16[128,512]{1,0:T(8,128)(2,1)} %param.18) | copy-start | bytes 393220
  38.0 24.7 %all-to-all-start.1 = ((bf16[16,4,4096]{2,1,0:T(4,128)(2,1)}), bf16[16,4,4096]{2,1,0:T(4,128)(2,1)S(1)}, u32[]{:S(2)}, u32[]{:S(2)}) async-start(bf16[16,4,4096]{2,1,0:T(4,128)(2,1)} %all_to_all.38), calls=%async_computation.1 | async-start | bytes 1048576 | tf_op jit(solution)/shard_map/all_to_all | solution.py:64
  45.0 89.9 %all-gather.5.cloned.1.call-start = ((), (), s32[]{:S(2)}) async-start(), calls=%async_computation.7 | async-start | bytes 4718592 | tf_op jit(solution)/shard_map/all_gather | solution.py:125
  66.4 6.8 %copy-start.4 = (f32[512,8]{0,1:T(8,128)S(1)}, f32[512,8]{0,1:T(8,128)}, u32[]{:S(2)}) copy-start(f32[512,8]{0,1:T(8,128)} %param.20) | copy-start | bytes 49156
  66.4 6.8 %copy-start.6 = (f32[512]{0:T(512)S(1)}, f32[512]{0:T(512)}, u32[]{:S(2)}) copy-start(f32[512]{0:T(512)} %param.21) | copy-start | bytes 6148
  106.2 93.1 %reduce-scatter.2.cloned.1.call-start = ((), (), s32[]{:S(2)}) async-start(), calls=%async_computation.8 | async-start | bytes 4718592 | tf_op jit(solution)/shard_map/reduce_scatter | solution.py:133
  160.9 0.7 copy-start.7
  160.9 1.0 copy-start.8
  160.9 4.6 %copy-start.5 = (s32[128,2]{0,1:T(2,128)S(1)}, s32[128,2]{0,1:T(2,128)}, u32[]{:S(2)}) copy-start(s32[128,2]{0,1:T(2,128)} %param.26) | copy-start | bytes 3076
  168.3 20.8 %copy-start.1 = (bf16[128,4096]{1,0:T(8,128)(2,1)}, bf16[128,4096]{1,0:T(8,128)(2,1)S(1)}, u32[]{:S(2)}) copy-start(bf16[128,4096]{1,0:T(8,128)(2,1)S(1)} %select_select_fusion) | copy-start | bytes 3145732
  170.3 18.8 %all-to-all-start.4 = ((bf16[16,4,4096]{2,1,0:T(4,128)(2,1)}), bf16[16,4,4096]{2,1,0:T(4,128)(2,1)S(1)}, u32[]{:S(2)}, u32[]{:S(2)}) async-start(bf16[16,4,4096]{2,1,0:T(4,128)(2,1)} %all_to_all.46), calls=%async_computation.5 | async-start | bytes 1048576 | tf_op jit(solution)/shard_map/all_to_all | solution.py:145
  199.3 16.8 %all-to-all-start.3 = ((bf16[16,32,512]{2,1,0:T(8,128)(2,1)}), bf16[16,32,512]{2,1,0:T(8,128)(2,1)S(1)}, u32[]{:S(2)}, u32[]{:S(2)}) async-start(bf16[16,32,512]{2,1,0:T(8,128)(2,1)} %bitcast.81), calls=%async_computation.4 | async-start | bytes 1048576 | tf_op jit(solution)/shard_map/all_to_all | solution.py:152
Sparse Core Ops, SparseCore 0:
  10.2 59.6 all-gather.2
  106.3 28.4 all-gather.4
  161.1 38.2 reduce-scatter.1

commit v4 on v3

--- a/solution.py
+++ b/solution.py
@@ -1,7 +1,10 @@
 import jax
 import jax.numpy as jnp
 from jax import lax
+from jax.experimental import pallas as pl
+from jax.experimental.pallas import tpu as pltpu
 from jax.sharding import PartitionSpec as P
+import functools
 
 D = 4096
 CAP = 32
@@ -9,6 +12,58 @@
 
 
 EPSILON = 1e-05
+
+MESH = pl.DeviceIdType.MESH
+
+
+def exchange_kernel(axis, n, gather, x_ref, y_ref, send_sems, recv_sems):
+    me = lax.axis_index(axis)
+    barrier = pltpu.get_barrier_semaphore()
+    for k in range(1, n):
+        pl.semaphore_signal(
+            barrier, inc=1, device_id={axis: lax.rem(me + k, n)}, device_id_type=MESH
+        )
+    pl.semaphore_wait(barrier, n - 1)
+    copies = []
+    for k in range(1, n):
+        peer = lax.rem(me + k, n)
+        copy = pltpu.make_async_remote_copy(
+            src_ref=x_ref if gather else x_ref.at[peer],
+            dst_ref=y_ref.at[me],
+            send_sem=send_sems.at[k],
+            recv_sem=recv_sems.at[k],
+            device_id={axis: peer},
+            device_id_type=MESH,
+        )
+        copy.start()
+        copies.append(copy)
+    if gather:
+        y_ref[me] = x_ref[...]
+    else:
+        y_ref[me] = x_ref[me]
+    for k in range(1, n):
+        copies[k - 1].wait_send()
+        source = lax.rem(me + n - k, n)
+        pltpu.make_async_remote_copy(
+            src_ref=x_ref if gather else x_ref.at[source],
+            dst_ref=y_ref.at[source],
+            send_sem=send_sems.at[k],
+            recv_sem=recv_sems.at[k],
+            device_id={axis: source},
+            device_id_type=MESH,
+        ).wait_recv()
+
+
+def exchange(x, axis, n, gather, collective_id):
+    out_shape = (n,) + x.shape if gather else x.shape
+    return pl.pallas_call(
+        functools.partial(exchange_kernel, axis, n, gather),
+        out_shape=jax.ShapeDtypeStruct(out_shape, x.dtype),
+        in_specs=[pl.BlockSpec(memory_space=pltpu.VMEM)],
+        out_specs=pl.BlockSpec(memory_space=pltpu.VMEM),
+        scratch_shapes=[pltpu.SemaphoreType.DMA((n,)), pltpu.SemaphoreType.DMA((n,))],
+        compiler_params=pltpu.CompilerParams(collective_id=collective_id, has_side_effects=True),
+    )(x)
 
 
 def pick_rows(source, row_index, live_slot):
@@ -95,7 +150,10 @@
     squares = jnp.sum(hidden * hidden, axis=1)
     scaled = hidden * norm_gain[None, :]
     raw_logits = jnp.dot(scaled, router_w, precision=lax.Precision.HIGHEST)
-    row_stats = lax.psum(jnp.concatenate([squares[:, None], raw_logits], axis=1), "exp")
+    stats_t = jnp.concatenate([squares[None, :], raw_logits.T], axis=0)
+    stats_t = jnp.pad(stats_t, ((0, 16 - stats_t.shape[0]), (0, 0)))
+    n_exp = lax.axis_size("exp")
+    row_stats = jnp.sum(exchange(stats_t, "exp", n_exp, True, 0), axis=0)[:9].T
     total_sq = row_stats[:, 0]
     inverse = lax.rsqrt(total_sq / D + EPSILON)
     normed = scaled * inverse[:, None]
@@ -121,7 +179,9 @@
     ).reshape(-1)
     slot_live = jnp.any(chosen_slot, axis=2).reshape(-1)
     outgoing = pick_rows(normed_rows, slot_source, slot_live)
-    arrived = lax.all_to_all(outgoing, "req", split_axis=0, concat_axis=0, tiled=True)
+    arrived = exchange(
+        outgoing.reshape(groups, -1, outgoing.shape[-1]), "req", groups, False, 1
+    ).reshape(outgoing.shape)
     rows_full = lax.all_gather(arrived, "exp", axis=1, tiled=True)
     gate_h = jnp.dot(rows_full, w_gate[0], preferred_element_type=jnp.float32)
     up_h = jnp.dot(rows_full, w_up[0], preferred_element_type=jnp.float32)
@@ -149,7 +209,9 @@
         jnp.concatenate([page_rows, moved_pages], axis=0), arrival, axis=0
     ).reshape(row_req, pages_req, page_len, kv_slice)
     lookup = target_dev * CAP + slot_index
-    returned = lax.all_to_all(summed_value, "req", split_axis=0, concat_axis=0, tiled=True)
+    returned = exchange(
+        summed_value.reshape(groups, -1, summed_value.shape[-1]), "req", groups, False, 2
+    ).reshape(summed_value.shape)
     taken_rows = jnp.take(returned, lookup, axis=0).reshape(row_req, 2, -1).astype(jnp.float32)
     expert_part = gate_first[:, None] * taken_rows[:, 0] + gate_second[:, None] * taken_rows[:, 1]
     mixed = hidden + expert_part

time: 226 us -> 220 us (0.973)
  Pallas kernels: 0 us -> 35.1 us
  blocking collectives: 30.4 us -> 0 us
  waiting for transfers between devices: 75.2 us -> 67.8 us
  starting transfers between devices: 27.9 us -> 21.2 us
  other arithmetic: 15.3 us -> 17.6 us
    pallas_call x0 -> x3, Pallas kernels: none -> 35.1 us  [exchange(): pl.pallas_call(functools.partial(exchange_kernel, axis, n, gather), out_s...]
    all_to_all x1 -> x0, blocking collectives: 15.3 us -> none  [body(): lax.all_to_all(outgoing, 'req', split_axis=0, concat_axis=0, tiled=True)]
    psum x1 -> x0, blocking collectives: 15.1 us -> none  [body(): lax.psum(jnp.concatenate([squares[:, None], raw_logits], axis=1), 'exp')]
    all_to_all x1 -> x0, waiting for transfers between devices: 7.51 us -> none  [body(): lax.all_to_all(summed_value, 'req', split_axis=0, concat_axis=0, tiled=True)]
    all_to_all x1 -> x0, starting transfers between devices: 6.67 us -> none  [body(): lax.all_to_all(summed_value, 'req', split_axis=0, concat_axis=0, tiled=True)]
    all_gather x1, waiting for transfers between devices: 28.4 us -> 31.2 us  [body(): rows_full = lax.all_gather(arrived, 'exp', axis=1, tiled=True)]
    reduce_scatter x1, waiting for transfers between devices: 6.57 us -> 3.93 us  [body(): lax.psum_scatter(partial_value, 'exp', scatter_dimension=1, tiled=True)]
  transfers between devices with their start and end apart: 7 -> 6, of which waited for: 7 -> 6; matrix products, arithmetic and copies ran while one was open for 18% -> 18% of each run, Pallas kernels for 0% -> 0%
where the time goes in v4:
time: 220 us; the launch traced here: 219 us
  waiting for transfers between devices  67.8 us (31%)
  Pallas kernels  35.1 us (16%)
  local copies, waits for them, and re-layouts  33.4 us (15%)
  matrix products  29.7 us (14%)
  starting transfers between devices  21.2 us (10%)
  other arithmetic  17.6 us (8%)
  between operations  14.3 us (6%)
    pallas_call x3, Pallas kernels, exchange(): pl.pallas_call(functools.partial(exchange_kernel, axis, n, gather), out_s...  35.1 us
    all_gather x1, waiting for transfers between devices, body(): rows_full = lax.all_gather(arrived, 'exp', axis=1, tiled=True)  31.2 us
    all_to_all x1, waiting for transfers between devices, body(): lax.all_to_all(pick_rows(attention_out, send_index, send_live), 'req', sp...  16.4 us
    dot_general x1, matrix products, body(): jnp.dot(active, w_down[0], preferred_element_type=jnp.float32)  16.2 us
    all_to_all x1, waiting for transfers between devices, body(): lax.all_to_all(pick_rows(page_rows, send_index, send_live), 'req', split_...  11.9 us
    dot_general x1, matrix products, body(): gate_h = jnp.dot(rows_full, w_gate[0], preferred_element_type=jnp.float32)  9.79 us
    scatter x1, local copies, waits for them, and re-layouts, body(): jnp.zeros((rows_all,), jnp.int32).at[came_from]  8.04 us
    all_to_all x1, starting transfers between devices, body(): lax.all_to_all(pick_rows(residual, send_index, send_live), 'req', split_a...  7.12 us
  transfers between devices with their start and end apart: 6, of which 6 were waited for; matrix products, arithmetic and copies ran while one was open for 18% of the time, Pallas kernels for 0%

profile of v4, /device:TPU:0, one launch (start us, length us, event | category | flops | bytes accessed | tf_op | source)
XLA Modules:
  0.0 219.0 jit_solution(16982070502255490575)
XLA Ops:
  7.2 0.7 all-gather.3.cloned.1.call-update
  7.9 0.7 compare_select_fusion.1
  8.6 8.0 %scatter_custom_fusion = s32[2048]{0:T(1024)S(1)} fusion(s32[2048]{0:T(1024)S(1)} %compare_select_fusion.1, s32[2048]{0:T(1024)S(1)} %iota.72, s32[]{:T(128)} %constant.183.clone.1), kind=kCustom, calls=%fused_computation.95 | custom fusion | bytes 8196 | tf_op jit(solution)/shard_map/scatter | solution.py:100
  16.8 2.8 %select_reduce_fusion = s32[16,128]{0,1:T(8,128)S(1)} fusion(s32[16,128]{0,1:T(8,128)S(1)} %copy.115), kind=kOutput, calls=%fused_computation.28 | output fusion | flops 4388864 | bytes 16384 | tf_op jit(solution)/shard_map/jit(cumsum)/reduce_window_sum | solution.py:106
  20.6 1.6 gather_fusion.1
  22.4 0.8 select_select_fusion.4
  23.1 7.1 %all-to-all-start = ((bf16[16,4,512]{2,1,0:T(4,128)(2,1)}), bf16[16,4,512]{2,1,0:T(4,128)(2,1)S(1)}, u32[]{:S(2)}, u32[]{:S(2)}) async-start(bf16[16,4,512]{2,1,0:T(4,128)(2,1)} %select_select_fusion.4), calls=%async_computation | async-start | bytes 131072 | tf_op jit(solution)/shard_map/all_to_all | solution.py:126
  30.4 0.8 copy.122
  31.6 0.9 gather_fusion.6
  32.6 1.0 all_to_all.24
  33.6 0.8 compare_select_fusion.15
  34.3 1.1 gather_fusion
  35.5 0.6 reduce-window.6
  36.9 0.8 compare_and_fusion.5
  38.0 7.0 %all-to-all-start.1 = ((bf16[16,4,4096]{2,1,0:T(4,128)(2,1)}), bf16[16,4,4096]{2,1,0:T(4,128)(2,1)S(1)}, u32[]{:S(2)}, u32[]{:S(2)}) async-start(bf16[16,4,4096]{2,1,0:T(4,128)(2,1)} %all_to_all.24), calls=%async_computation.1 | async-start | bytes 1048576 | tf_op jit(solution)/shard_map/all_to_all | solution.py:119
  45.5 0.8 gather_fusion.2
  46.3 16.4 %all-to-all-done.1 = bf16[16,4,4096]{2,1,0:T(4,128)(2,1)S(1)} async-done(((bf16[16,4,4096]{2,1,0:T(4,128)(2,1)}), bf16[16,4,4096]{2,1,0:T(4,128)(2,1)S(1)}, u32[]{:S(2)}, u32[]{:S(2)}) %all-to-all-start.1) | async-done | bytes 524320 | tf_op jit(solution)/shard_map/all_to_all | solution.py:119
  62.9 1.4 pad_maximum_fusion
  64.2 2.2 gather_fusion.7
  66.4 3.4 %all-gather.3.cloned.1.call-done = bf16[4096,512]{1,0:T(8,128)(2,1)} async-done(((bf16[256,512]{1,0:T(8,128)(2,1)}), bf16[4096,512]{1,0:T(8,128)(2,1)}) %all-gather.3.cloned.1.call-update) | async-done | bytes 4194320 | tf_op jit(solution)/shard_map/all_gather | solution.py:146
  69.8 3.4 %multiply_reduce_fusion = (f32[128]{0:T(128)S(1)}, f32[128,512]{1,0:T(8,128)S(1)}) fusion(bf16[4096,512]{1,0:T(8,128)(2,1)} %all-gather.3.cloned.1.call-done, bf16[128,4096]{1,0:T(8,128)(2,1)} %gather_fusion.7, pred[128]{0:T(512)(128)(4,1)S(1)} %get-tuple-element.8, bf16[128,512]{1,0:T(8,128)(2,1)S(1)} %gather_fusion.2), kind=kOutput, calls=%fused_computation.49 | convolution fusion | flops 537722752 | bytes 5636736 | tf_op jit(solution)/shard_map/dot_general | solution.py:144
  73.5 0.7 select_maximum_fusion.x_ref
  74.2 7.7 %shard_map.140 = f32[8,16,128]{2,1,0:T(8,128)} custom-call(f32[16,128]{1,0:T(8,128)} %select_maximum_fusion.x_ref), custom_call_target="tpu_custom_call" | custom-call | tf_op jit(solution)/shard_map/pallas_call | solution.py:59
  81.8 0.9 reduce_sum.70
  82.8 2.0 gather_fusion.3
  84.8 1.0 select_select_fusion.3.x_ref
  85.8 14.4 %shard_map.141 = bf16[16,32,512]{2,1,0:T(8,128)(2,1)} custom-call(bf16[16,32,512]{2,1,0:T(8,128)(2,1)} %select_select_fusion.3.x_ref), custom_call_target="tpu_custom_call" | custom-call | tf_op jit(solution)/shard_map/pallas_call | solution.py:59
  100.4 31.2 %all-gather.5.cloned.1.call-done = bf16[512,4096]{1,0:T(8,128)(2,1)} async-done(((bf16[512,512]{1,0:T(8,128)(2,1)}), bf16[512,4096]{1,0:T(8,128)(2,1)}) %all-gather.5.cloned.1.call-update) | async-done | bytes 4194320 | tf_op jit(solution)/shard_map/all_gather | solution.py:185
  131.6 9.8 %fusion.4 = f32[512,896]{1,0:T(8,128)S(1)} fusion(bf16[512,4096]{1,0:T(8,128)(2,1)} %all-gather.5.cloned.1.call-done, bf16[1,4096,896]{2,1,0:T(8,128)(2,1)} %param.27), kind=kOutput, calls=%fused_computation.15 | convolution fusion | flops 3758096384 | bytes 13369344 | tf_op jit(solution)/shard_map/dot_general | solution.py:186
  141.4 16.2 %fusion.6 = bf16[512,4096]{1,0:T(8,128)(2,1)} fusion(bf16[1,896,4096]{2,1,0:T(8,128)(2,1)} %param.29, f32[512,896]{1,0:T(8,128)S(1)} %fusion.4, bf16[512,4096]{1,0:T(8,128)(2,1)} %all-gather.5.cloned.1.call-done, bf16[1,4096,896]{2,1,0:T(8,128)(2,1)} %param.28), kind=kOutput, calls=%fused_computation.17 | convolution fusion | flops 7521042432 | bytes 24903680 | tf_op jit(solution)/shard_map/dot_general | solution.py:190
  158.9 0.4 broadcast_in_dim.231
  159.3 1.1 copy.132
  161.0 1.1 copy.133
  162.3 0.8 gather_fusion.5
  163.0 0.5 gather.47
  163.6 1.4 select_select_fusion
  165.0 0.9 gather_fusion.8
  166.0 1.0 all_to_all.27
  167.0 6.8 %all-to-all-start.2 = ((bf16[16,4,4096]{2,1,0:T(4,128)(2,1)}), bf16[16,4,4096]{2,1,0:T(4,128)(2,1)S(1)}, u32[]{:S(2)}, u32[]{:S(2)}) async-start(bf16[16,4,4096]{2,1,0:T(4,128)(2,1)} %all_to_all.27), calls=%async_computation.3 | async-start | bytes 1048576 | tf_op jit(solution)/shard_map/all_to_all | solution.py:205
  173.9 11.9 %all-to-all-done.2 = bf16[16,4,4096]{2,1,0:T(4,128)(2,1)S(1)} async-done(((bf16[16,4,4096]{2,1,0:T(4,128)(2,1)}), bf16[16,4,4096]{2,1,0:T(4,128)(2,1)S(1)}, u32[]{:S(2)}, u32[]{:S(2)}) %all-to-all-start.2) | async-done | bytes 524320 | tf_op jit(solution)/shard_map/all_to_all | solution.py:205
  185.9 1.4 pad_maximum_fusion.1
  187.3 2.2 gather_fusion.9
  189.5 1.4 broadcast_select_fusion
  190.9 1.2 copy.134
  192.1 3.9 %reduce-scatter.2.cloned.1.call-done = bf16[512,512]{1,0:T(8,128)(2,1)} async-done(((bf16[512,4096]{1,0:T(8,128)(2,1)}), bf16[512,512]{1,0:T(8,128)(2,1)}) %reduce-scatter.2.cloned.1.call-update) | async-done | bytes 524304 | tf_op jit(solution)/shard_map/reduce_scatter | solution.py:193
  196.0 13.0 %shard_map.142 = bf16[16,32,512]{2,1,0:T(8,128)(2,1)} custom-call(bf16[16,32,512]{2,1,0:T(8,128)(2,1)} %bitcast.85), custom_call_target="tpu_custom_call" | custom-call | tf_op jit(solution)/shard_map/pallas_call | solution.py:59
  209.1 2.3 %gather_fusion.4 = bf16[256,512]{1,0:T(8,128)(2,1)S(1)} fusion(bf16[512,512]{1,0:T(8,128)(2,1)} %bitcast.76, s32[1024]{0:T(1024)S(1)} %pad_clamp_fusion.1), kind=kCustom, calls=%fused_computation.8 | custom fusion | bytes 525312 | tf_op jit(solution)/shard_map/jit(_take)/gather | solution.py:215
  211.6 0.8 fusion.24
  (98 shorter events, 6.6 us)
Async XLA Ops:
  7.2 155.1 %copy-start = (bf16[256,8,256]{2,1,0:T(8,128)(2,1)S(1)}, bf16[256,8,256]{2,1,0:T(8,128)(2,1)}, u32[]{:S(2)}) copy-start(bf16[256,8,256]{2,1,0:T(8,128)(2,1)} %param.22) | copy-start | bytes 3145732
  7.2 24.4 %copy-start.2 = (bf16[128,4096]{1,0:T(8,128)(2,1)S(1)}, bf16[128,4096]{1,0:T(8,128)(2,1)}, u32[]{:S(2)}) copy-start(bf16[128,4096]{1,0:T(8,128)(2,1)} %param.17) | copy-start | bytes 3145732
  7.2 62.6 %all-gather.3.cloned.1.call-start = ((), (), s32[]{:S(2)}) async-start(), calls=%async_computation.4 | async-start | bytes 4456448 | tf_op jit(solution)/shard_map/all_gather | solution.py:146
  23.1 14.9 %all-to-all-start = ((bf16[16,4,512]{2,1,0:T(4,128)(2,1)}), bf16[16,4,512]{2,1,0:T(4,128)(2,1)S(1)}, u32[]{:S(2)}, u32[]{:S(2)}) async-start(bf16[16,4,512]{2,1,0:T(4,128)(2,1)} %select_select_fusion.4), calls=%async_computation | async-start | bytes 131072 | tf_op jit(solution)/shard_map/all_to_all | solution.py:126
  31.5 13.9 %copy-start.3 = (bf16[128,512]{1,0:T(8,128)(2,1)S(1)}, bf16[128,512]{1,0:T(8,128)(2,1)}, u32[]{:S(2)}) copy-start(bf16[128,512]{1,0:T(8,128)(2,1)} %param.18) | copy-start | bytes 393220
  38.0 24.7 %all-to-all-start.1 = ((bf16[16,4,4096]{2,1,0:T(4,128)(2,1)}), bf16[16,4,4096]{2,1,0:T(4,128)(2,1)S(1)}, u32[]{:S(2)}, u32[]{:S(2)}) async-start(bf16[16,4,4096]{2,1,0:T(4,128)(2,1)} %all_to_all.24), calls=%async_computation.1 | async-start | bytes 1048576 | tf_op jit(solution)/shard_map/all_to_all | solution.py:119
  45.0 86.6 %all-gather.5.cloned.1.call-start = ((), (), s32[]{:S(2)}) async-start(), calls=%async_computation.5 | async-start | bytes 4718592 | tf_op jit(solution)/shard_map/all_gather | solution.py:185
  66.4 6.8 %copy-start.4 = (f32[512,8]{0,1:T(8,128)S(1)}, f32[512,8]{0,1:T(8,128)}, u32[]{:S(2)}) copy-start(f32[512,8]{0,1:T(8,128)} %param.20) | copy-start | bytes 49156
  66.4 6.8 %copy-start.6 = (f32[512]{0:T(512)S(1)}, f32[512]{0:T(512)}, u32[]{:S(2)}) copy-start(f32[512]{0:T(512)} %param.21) | copy-start | bytes 6148
  100.2 95.8 %reduce-scatter.2.cloned.1.call-start = ((), (), s32[]{:S(2)}) async-start(), calls=%async_computation.6 | async-start | bytes 4718592 | tf_op jit(solution)/shard_map/reduce_scatter | solution.py:193
  157.6 0.7 copy-start.7
  157.6 1.0 copy-start.8
  157.6 4.6 %copy-start.5 = (s32[128,2]{0,1:T(2,128)S(1)}, s32[128,2]{0,1:T(2,128)}, u32[]{:S(2)}) copy-start(s32[128,2]{0,1:T(2,128)} %param.26) | copy-start | bytes 3076
  165.0 20.8 %copy-start.1 = (bf16[128,4096]{1,0:T(8,128)(2,1)}, bf16[128,4096]{1,0:T(8,128)(2,1)S(1)}, u32[]{:S(2)}) copy-start(bf16[128,4096]{1,0:T(8,128)(2,1)S(1)} %select_select_fusion) | copy-start | bytes 3145732
  167.0 18.8 %all-to-all-start.2 = ((bf16[16,4,4096]{2,1,0:T(4,128)(2,1)}), bf16[16,4,4096]{2,1,0:T(4,128)(2,1)S(1)}, u32[]{:S(2)}, u32[]{:S(2)}) async-start(bf16[16,4,4096]{2,1,0:T(4,128)(2,1)} %all_to_all.27), calls=%async_computation.3 | async-start | bytes 1048576 | tf_op jit(solution)/shard_map/all_to_all | solution.py:205
Sparse Core Ops, SparseCore 0:
  10.2 59.6 all-gather.2
  100.3 31.2 all-gather.4
  157.8 38.2 reduce-scatter.1

commit v5 on v4

--- a/solution.py
+++ b/solution.py
@@ -66,6 +66,80 @@
     )(x)
 
 
+def exp_gather_kernel(n, x_ref, y_ref, send_sems, recv_sems):
+    chips = n // 2
+    width = x_ref.shape[1]
+    half = x_ref.shape[0] // 2
+    me = lax.axis_index("exp")
+    z, core = me // 2, me % 2
+    sib = 2 * z + 1 - core
+    up = 2 * lax.rem(z + 1, chips) + core
+    dn = 2 * lax.rem(z + chips - 1, chips) + core
+    far = 2 * lax.rem(z + 2, chips) + core
+
+    def cols(block):
+        return pl.ds(pl.multiple_of(block * width, width), width)
+
+    def rows(part):
+        return pl.ds(part * half, half)
+
+    barrier = pltpu.get_barrier_semaphore()
+    for peer in (sib, up, dn):
+        pl.semaphore_signal(barrier, inc=1, device_id={"exp": peer}, device_id_type=MESH)
+    pl.semaphore_wait(barrier, 3)
+
+    def remote(src, dst, slot, peer):
+        return pltpu.make_async_remote_copy(
+            src_ref=src, dst_ref=dst, send_sem=send_sems.at[slot],
+            recv_sem=recv_sems.at[slot], device_id={"exp": peer}, device_id_type=MESH,
+        )
+
+    own_cols = cols(me)
+    first = [
+        remote(x_ref, y_ref.at[:, own_cols], 0, up),
+        remote(x_ref, y_ref.at[:, own_cols], 1, dn),
+        remote(x_ref, y_ref.at[:, own_cols], 2, sib),
+    ]
+    for copy in first:
+        copy.start()
+    y_ref[:, own_cols] = x_ref[...]
+    remote(x_ref, y_ref.at[:, cols(dn)], 0, dn).wait_recv()
+    remote(x_ref, y_ref.at[:, cols(up)], 1, up).wait_recv()
+    second = [
+        remote(y_ref.at[rows(1), cols(dn)], y_ref.at[rows(1), cols(dn)], 3, up),
+        remote(y_ref.at[rows(0), cols(up)], y_ref.at[rows(0), cols(up)], 4, dn),
+        remote(y_ref.at[:, cols(dn)], y_ref.at[:, cols(dn)], 5, sib),
+        remote(y_ref.at[:, cols(up)], y_ref.at[:, cols(up)], 6, sib),
+    ]
+    for copy in second:
+        copy.start()
+    remote(y_ref.at[rows(1), cols(far)], y_ref.at[rows(1), cols(far)], 3, dn).wait_recv()
+    remote(y_ref.at[rows(0), cols(far)], y_ref.at[rows(0), cols(far)], 4, up).wait_recv()
+    third = remote(y_ref.at[:, cols(far)], y_ref.at[:, cols(far)], 7, sib)
+    third.start()
+    sib_z = 2 * z + 1 - core
+    sib_up = 2 * lax.rem(z + 1, chips) + 1 - core
+    sib_dn = 2 * lax.rem(z + chips - 1, chips) + 1 - core
+    sib_far = 2 * lax.rem(z + 2, chips) + 1 - core
+    remote(x_ref, y_ref.at[:, cols(sib_z)], 2, sib).wait_recv()
+    remote(y_ref.at[:, cols(sib_dn)], y_ref.at[:, cols(sib_dn)], 5, sib).wait_recv()
+    remote(y_ref.at[:, cols(sib_up)], y_ref.at[:, cols(sib_up)], 6, sib).wait_recv()
+    remote(y_ref.at[:, cols(sib_far)], y_ref.at[:, cols(sib_far)], 7, sib).wait_recv()
+    for copy in first + second + [third]:
+        copy.wait_send()
+
+
+def exp_gather(x, n, collective_id):
+    return pl.pallas_call(
+        functools.partial(exp_gather_kernel, n),
+        out_shape=jax.ShapeDtypeStruct((x.shape[0], n * x.shape[1]), x.dtype),
+        in_specs=[pl.BlockSpec(memory_space=pltpu.VMEM)],
+        out_specs=pl.BlockSpec(memory_space=pltpu.VMEM),
+        scratch_shapes=[pltpu.SemaphoreType.DMA((8,)), pltpu.SemaphoreType.DMA((8,))],
+        compiler_params=pltpu.CompilerParams(collective_id=collective_id, has_side_effects=True),
+    )(x)
+
+
 def pick_rows(source, row_index, live_slot):
     taken_rows = jnp.take(source, row_index, axis=0)
     return jnp.where(live_slot[:, None], taken_rows, jnp.zeros((), source.dtype))
@@ -182,7 +256,7 @@
     arrived = exchange(
         outgoing.reshape(groups, -1, outgoing.shape[-1]), "req", groups, False, 1
     ).reshape(outgoing.shape)
-    rows_full = lax.all_gather(arrived, "exp", axis=1, tiled=True)
+    rows_full = exp_gather(arrived, lax.axis_size("exp"), 3)
     gate_h = jnp.dot(rows_full, w_gate[0], preferred_element_type=jnp.float32)
     up_h = jnp.dot(rows_full, w_up[0], preferred_element_type=jnp.float32)
     active = (jax.nn.silu(gate_h) * up_h).astype(jnp.bfloat16)

time: 220 us -> 213 us (0.968)
  waiting for transfers between devices: 67.8 us -> 35.6 us
  Pallas kernels: 35.1 us -> 61.2 us
    all_gather x1 -> x0, waiting for transfers between devices: 31.2 us -> none  [body(): rows_full = lax.all_gather(arrived, 'exp', axis=1, tiled=True)]
    pallas_call x0 -> x1, Pallas kernels: none -> 26.1 us  [exp_gather(): pl.pallas_call(functools.partial(exp_gather_kernel, n), out_shape=jax.Sha...]
    unnamed x23 -> x25, local copies, waits for them, and re-layouts: 4.74 us -> 4.75 us
  transfers between devices with their start and end apart: 6 -> 5, of which waited for: 6 -> 5; matrix products, arithmetic and copies ran while one was open for 18% -> 19% of each run, Pallas kernels for 0% -> 0%
where the time goes in v5:
time: 213 us
  Pallas kernels  61.2 us (29%)
  waiting for transfers between devices  35.6 us (17%)
  local copies, waits for them, and re-layouts  34.2 us (16%)
  matrix products  29.7 us (14%)
  starting transfers between devices  19.6 us (9%)
  other arithmetic  17.7 us (8%)
  between operations  14.6 us (7%)
    pallas_call x3, Pallas kernels, exchange(): pl.pallas_call(functools.partial(exchange_kernel, axis, n, gather), out_s...  35.1 us
    pallas_call x1, Pallas kernels, exp_gather(): pl.pallas_call(functools.partial(exp_gather_kernel, n), out_shape=jax.Sha...  26.1 us
    dot_general x1, matrix products, body(): jnp.dot(active, w_down[0], preferred_element_type=jnp.float32)  16.2 us
    all_to_all x1, waiting for transfers between devices, body(): lax.all_to_all(pick_rows(attention_out, send_index, send_live), 'req', sp...  15.7 us
    all_to_all x1, waiting for transfers between devices, body(): lax.all_to_all(pick_rows(page_rows, send_index, send_live), 'req', split_...  12 us
    dot_general x1, matrix products, body(): gate_h = jnp.dot(rows_full, w_gate[0], preferred_element_type=jnp.float32)  9.81 us
    scatter x1, local copies, waits for them, and re-layouts, body(): jnp.zeros((rows_all,), jnp.int32).at[came_from]  8.04 us
    all_to_all x1, starting transfers between devices, body(): lax.all_to_all(pick_rows(residual, send_index, send_live), 'req', split_a...  7.12 us
  transfers between devices with their start and end apart: 5, of which 5 were waited for; matrix products, arithmetic and copies ran while one was open for 19% of the time, Pallas kernels for 0%

profile of v5, /device:TPU:0, one launch (start us, length us, event | category | flops | bytes accessed | tf_op | source)
XLA Modules:
  0.0 212.5 jit_solution(11101481905290251217)
XLA Ops:
  7.2 0.7 all-gather.2.cloned.1.call-update
  7.9 0.7 compare_select_fusion.1
  8.6 8.0 %scatter_custom_fusion = s32[2048]{0:T(1024)S(1)} fusion(s32[2048]{0:T(1024)S(1)} %compare_select_fusion.1, s32[2048]{0:T(1024)S(1)} %iota.72, s32[]{:T(128)} %constant.183.clone.1), kind=kCustom, calls=%fused_computation.95 | custom fusion | bytes 8196 | tf_op jit(solution)/shard_map/scatter | solution.py:174
  16.8 2.8 %select_reduce_fusion = s32[16,128]{0,1:T(8,128)S(1)} fusion(s32[16,128]{0,1:T(8,128)S(1)} %copy.115), kind=kOutput, calls=%fused_computation.28 | output fusion | flops 4388864 | bytes 16384 | tf_op jit(solution)/shard_map/jit(cumsum)/reduce_window_sum | solution.py:180
  20.6 1.6 gather_fusion.1
  22.4 0.8 select_select_fusion.4
  23.1 7.1 %all-to-all-start = ((bf16[16,4,512]{2,1,0:T(4,128)(2,1)}), bf16[16,4,512]{2,1,0:T(4,128)(2,1)S(1)}, u32[]{:S(2)}, u32[]{:S(2)}) async-start(bf16[16,4,512]{2,1,0:T(4,128)(2,1)} %select_select_fusion.4), calls=%async_computation | async-start | bytes 131072 | tf_op jit(solution)/shard_map/all_to_all | solution.py:200
  30.4 0.8 copy.122
  31.6 0.9 gather_fusion.6
  32.6 1.0 all_to_all.24
  33.6 0.8 compare_select_fusion.15
  34.3 1.1 gather_fusion
  35.5 0.6 reduce-window.6
  36.9 0.8 compare_and_fusion.5
  38.0 7.0 %all-to-all-start.1 = ((bf16[16,4,4096]{2,1,0:T(4,128)(2,1)}), bf16[16,4,4096]{2,1,0:T(4,128)(2,1)S(1)}, u32[]{:S(2)}, u32[]{:S(2)}) async-start(bf16[16,4,4096]{2,1,0:T(4,128)(2,1)} %all_to_all.24), calls=%async_computation.1 | async-start | bytes 1048576 | tf_op jit(solution)/shard_map/all_to_all | solution.py:193
  45.5 1.5 gather_fusion.2
  47.0 15.7 %all-to-all-done.1 = bf16[16,4,4096]{2,1,0:T(4,128)(2,1)S(1)} async-done(((bf16[16,4,4096]{2,1,0:T(4,128)(2,1)}), bf16[16,4,4096]{2,1,0:T(4,128)(2,1)S(1)}, u32[]{:S(2)}, u32[]{:S(2)}) %all-to-all-start.1) | async-done | bytes 524320 | tf_op jit(solution)/shard_map/all_to_all | solution.py:193
  62.9 1.4 pad_maximum_fusion
  64.3 2.2 %gather_fusion.7 = bf16[128,4096]{1,0:T(8,128)(2,1)} fusion(bf16[192,4096]{1,0:T(8,128)(2,1)S(1)} %pad_maximum_fusion, s32[1024]{0:T(1024)S(1)} %pad_clamp_fusion.4), kind=kCustom, calls=%fused_computation.1.clone | custom fusion | bytes 2097664 | tf_op jit(solution)/shard_map/jit(_take)/gather | solution.py:216
  66.4 3.4 %all-gather.2.cloned.1.call-done = bf16[4096,512]{1,0:T(8,128)(2,1)} async-done(((bf16[256,512]{1,0:T(8,128)(2,1)}), bf16[4096,512]{1,0:T(8,128)(2,1)}) %all-gather.2.cloned.1.call-update) | async-done | bytes 4194320 | tf_op jit(solution)/shard_map/all_gather | solution.py:220
  69.8 3.4 %multiply_reduce_fusion = (f32[128]{0:T(128)S(1)}, f32[128,512]{1,0:T(8,128)S(1)}) fusion(bf16[4096,512]{1,0:T(8,128)(2,1)} %all-gather.2.cloned.1.call-done, bf16[128,4096]{1,0:T(8,128)(2,1)} %gather_fusion.7, pred[128]{0:T(512)(128)(4,1)S(1)} %get-tuple-element.8, bf16[128,512]{1,0:T(8,128)(2,1)S(1)} %copy-done.4), kind=kOutput, calls=%fused_computation.49 | convolution fusion | flops 537722752 | bytes 5636736 | tf_op jit(solution)/shard_map/dot_general | solution.py:218
  73.5 0.7 select_maximum_fusion.x_ref
  74.2 7.7 %shard_map.140 = f32[8,16,128]{2,1,0:T(8,128)} custom-call(f32[16,128]{1,0:T(8,128)} %select_maximum_fusion.x_ref), custom_call_target="tpu_custom_call" | custom-call | tf_op jit(solution)/shard_map/pallas_call | solution.py:59
  81.8 0.9 reduce_sum.70
  82.8 2.2 %gather_fusion.3 = bf16[512,512]{1,0:T(8,128)(2,1)S(1)} fusion(bf16[128,512]{1,0:T(8,128)(2,1)S(1)} %multiply_convert_fusion.1, s32[1024]{0:T(1024)S(1)} %pad_clamp_fusion.2), kind=kCustom, calls=%fused_computation.7 | custom fusion | bytes 1050624 | tf_op jit(solution)/shard_map/jit(_take)/gather | solution.py:144
  85.0 1.0 select_select_fusion.3.x_ref
  86.0 14.4 %shard_map.141 = bf16[16,32,512]{2,1,0:T(8,128)(2,1)} custom-call(bf16[16,32,512]{2,1,0:T(8,128)(2,1)} %select_select_fusion.3.x_ref), custom_call_target="tpu_custom_call" | custom-call | tf_op jit(solution)/shard_map/pallas_call | solution.py:59
  100.4 26.1 %shard_map.142 = bf16[512,4096]{1,0:T(8,128)(2,1)} custom-call(bf16[512,512]{1,0:T(8,128)(2,1)} %bitcast.79), custom_call_target="tpu_custom_call" | custom-call | tf_op jit(solution)/shard_map/pallas_call | solution.py:133
  126.4 9.8 %fusion.4 = f32[512,896]{1,0:T(8,128)S(1)} fusion(bf16[512,4096]{1,0:T(8,128)(2,1)} %shard_map.142, bf16[1,4096,896]{2,1,0:T(8,128)(2,1)} %param.27), kind=kOutput, calls=%fused_computation.15 | convolution fusion | flops 3758096384 | bytes 13369344 | tf_op jit(solution)/shard_map/dot_general | solution.py:260
  136.2 16.2 %fusion.6 = bf16[512,4096]{1,0:T(8,128)(2,1)} fusion(bf16[1,896,4096]{2,1,0:T(8,128)(2,1)} %param.29, f32[512,896]{1,0:T(8,128)S(1)} %fusion.4, bf16[512,4096]{1,0:T(8,128)(2,1)} %shard_map.142, bf16[1,4096,896]{2,1,0:T(8,128)(2,1)} %param.28), kind=kOutput, calls=%fused_computation.17 | convolution fusion | flops 7521042432 | bytes 24903680 | tf_op jit(solution)/shard_map/dot_general | solution.py:264
  153.7 0.4 broadcast_in_dim.231
  154.2 1.1 copy.132
  155.9 1.1 copy.133
  157.1 0.8 gather_fusion.5
  157.9 0.5 gather.47
  158.4 1.4 select_select_fusion
  159.9 0.9 gather_fusion.8
  160.9 1.0 all_to_all.27
  161.9 5.4 %all-to-all-start.2 = ((bf16[16,4,4096]{2,1,0:T(4,128)(2,1)}), bf16[16,4,4096]{2,1,0:T(4,128)(2,1)S(1)}, u32[]{:S(2)}, u32[]{:S(2)}) async-start(bf16[16,4,4096]{2,1,0:T(4,128)(2,1)} %all_to_all.27), calls=%async_computation.3 | async-start | bytes 1048576 | tf_op jit(solution)/shard_map/all_to_all | solution.py:279
  167.4 12.0 %all-to-all-done.2 = bf16[16,4,4096]{2,1,0:T(4,128)(2,1)S(1)} async-done(((bf16[16,4,4096]{2,1,0:T(4,128)(2,1)}), bf16[16,4,4096]{2,1,0:T(4,128)(2,1)S(1)}, u32[]{:S(2)}, u32[]{:S(2)}) %all-to-all-start.2) | async-done | bytes 524320 | tf_op jit(solution)/shard_map/all_to_all | solution.py:279
  179.6 1.4 pad_maximum_fusion.1
  181.0 2.2 %gather_fusion.9 = bf16[128,4096]{1,0:T(8,128)(2,1)} fusion(bf16[192,4096]{1,0:T(8,128)(2,1)S(1)} %pad_maximum_fusion.1, s32[1024]{0:T(1024)S(1)} %pad_clamp_fusion.4), kind=kCustom, calls=%fused_computation.3.clone | custom fusion | bytes 2097664 | tf_op jit(solution)/shard_map/jit(_take)/gather | solution.py:282
  183.1 1.4 broadcast_select_fusion
  184.5 1.2 copy.134
  185.8 3.5 %reduce-scatter.2.cloned.1.call-done = bf16[512,512]{1,0:T(8,128)(2,1)} async-done(((bf16[512,4096]{1,0:T(8,128)(2,1)}), bf16[512,512]{1,0:T(8,128)(2,1)}) %reduce-scatter.2.cloned.1.call-update) | async-done | bytes 524304 | tf_op jit(solution)/shard_map/reduce_scatter | solution.py:267
  189.3 13.1 %shard_map.143 = bf16[16,32,512]{2,1,0:T(8,128)(2,1)} custom-call(bf16[16,32,512]{2,1,0:T(8,128)(2,1)} %bitcast.85), custom_call_target="tpu_custom_call" | custom-call | tf_op jit(solution)/shard_map/pallas_call | solution.py:59
  202.3 2.3 %gather_fusion.4 = bf16[256,512]{1,0:T(8,128)(2,1)S(1)} fusion(bf16[512,512]{1,0:T(8,128)(2,1)} %bitcast.76, s32[1024]{0:T(1024)S(1)} %pad_clamp_fusion.1), kind=kCustom, calls=%fused_computation.8 | custom fusion | bytes 525312 | tf_op jit(solution)/shard_map/jit(_take)/gather | solution.py:289
  204.9 0.8 fusion.24
  (98 shorter events, 6.4 us)
Async XLA Ops:
  7.2 150.0 %copy-start = (bf16[256,8,256]{2,1,0:T(8,128)(2,1)S(1)}, bf16[256,8,256]{2,1,0:T(8,128)(2,1)}, u32[]{:S(2)}) copy-start(bf16[256,8,256]{2,1,0:T(8,128)(2,1)} %param.22) | copy-start | bytes 3145732
  7.2 24.4 %copy-start.2 = (bf16[128,4096]{1,0:T(8,128)(2,1)S(1)}, bf16[128,4096]{1,0:T(8,128)(2,1)}, u32[]{:S(2)}) copy-start(bf16[128,4096]{1,0:T(8,128)(2,1)} %param.17) | copy-start | bytes 3145732
  7.2 62.6 %all-gather.2.cloned.1.call-start = ((), (), s32[]{:S(2)}) async-start(), calls=%async_computation.4 | async-start | bytes 4456448 | tf_op jit(solution)/shard_map/all_gather | solution.py:220
  23.1 14.9 %all-to-all-start = ((bf16[16,4,512]{2,1,0:T(4,128)(2,1)}), bf16[16,4,512]{2,1,0:T(4,128)(2,1)S(1)}, u32[]{:S(2)}, u32[]{:S(2)}) async-start(bf16[16,4,512]{2,1,0:T(4,128)(2,1)} %select_select_fusion.4), calls=%async_computation | async-start | bytes 131072 | tf_op jit(solution)/shard_map/all_to_all | solution.py:200
  31.5 13.9 %copy-start.3 = (bf16[128,512]{1,0:T(8,128)(2,1)S(1)}, bf16[128,512]{1,0:T(8,128)(2,1)}, u32[]{:S(2)}) copy-start(bf16[128,512]{1,0:T(8,128)(2,1)} %param.18) | copy-start | bytes 393220
  38.0 24.7 %all-to-all-start.1 = ((bf16[16,4,4096]{2,1,0:T(4,128)(2,1)}), bf16[16,4,4096]{2,1,0:T(4,128)(2,1)S(1)}, u32[]{:S(2)}, u32[]{:S(2)}) async-start(bf16[16,4,4096]{2,1,0:T(4,128)(2,1)} %all_to_all.24), calls=%async_computation.1 | async-start | bytes 1048576 | tf_op jit(solution)/shard_map/all_to_all | solution.py:193
  45.0 144.3 %reduce-scatter.2.cloned.1.call-start = ((), (), s32[]{:S(2)}) async-start(), calls=%async_computation.5 | async-start | bytes 4718592 | tf_op jit(solution)/shard_map/reduce_scatter | solution.py:267
  64.2 5.6 %copy-start.4 = (bf16[128,512]{1,0:T(8,128)(2,1)S(1)}, bf16[128,512]{1,0:T(8,128)(2,1)}, u32[]{:S(2)}) copy-start(bf16[128,512]{1,0:T(8,128)(2,1)} %gather_fusion.2) | copy-start | bytes 393220
  66.4 6.8 %copy-start.5 = (f32[512,8]{0,1:T(8,128)S(1)}, f32[512,8]{0,1:T(8,128)}, u32[]{:S(2)}) copy-start(f32[512,8]{0,1:T(8,128)} %param.20) | copy-start | bytes 49156
  66.4 6.8 %copy-start.7 = (f32[512]{0:T(512)S(1)}, f32[512]{0:T(512)}, u32[]{:S(2)}) copy-start(f32[512]{0:T(512)} %param.21) | copy-start | bytes 6148
  152.5 0.7 copy-start.8
  152.5 1.0 copy-start.9
  152.5 4.6 %copy-start.6 = (s32[128,2]{0,1:T(2,128)S(1)}, s32[128,2]{0,1:T(2,128)}, u32[]{:S(2)}) copy-start(s32[128,2]{0,1:T(2,128)} %param.26) | copy-start | bytes 3076
  159.9 19.6 %copy-start.1 = (bf16[128,4096]{1,0:T(8,128)(2,1)}, bf16[128,4096]{1,0:T(8,128)(2,1)S(1)}, u32[]{:S(2)}) copy-start(bf16[128,4096]{1,0:T(8,128)(2,1)S(1)} %select_select_fusion) | copy-start | bytes 3145732
  161.9 17.5 %all-to-all-start.2 = ((bf16[16,4,4096]{2,1,0:T(4,128)(2,1)}), bf16[16,4,4096]{2,1,0:T(4,128)(2,1)S(1)}, u32[]{:S(2)}, u32[]{:S(2)}) async-start(bf16[16,4,4096]{2,1,0:T(4,128)(2,1)} %all_to_all.27), calls=%async_computation.3 | async-start | bytes 1048576 | tf_op jit(solution)/shard_map/all_to_all | solution.py:279
Sparse Core Ops, SparseCore 0:
  10.2 59.6 all-gather.1
  152.6 36.5 reduce-scatter.1

commit v6 on v5

--- a/solution.py
+++ b/solution.py
@@ -138,6 +138,90 @@
         scratch_shapes=[pltpu.SemaphoreType.DMA((8,)), pltpu.SemaphoreType.DMA((8,))],
         compiler_params=pltpu.CompilerParams(collective_id=collective_id, has_side_effects=True),
     )(x)
+
+
+def exp_scatter_kernel(n, p_ref, o_ref, sib_buf, acc, stage, half_buf, near_buf, send_sems, recv_sems):
+    chips = n // 2
+    width = o_ref.shape[1]
+    half = o_ref.shape[0] // 2
+    me = lax.axis_index("exp")
+    z, core = me // 2, me % 2
+    sib = 2 * z + 1 - core
+    up = 2 * lax.rem(z + 1, chips) + core
+    dn = 2 * lax.rem(z + chips - 1, chips) + core
+    far = 2 * lax.rem(z + 2, chips) + core
+
+    def cols(block):
+        return pl.ds(pl.multiple_of(block * width, width), width)
+
+    def rows(part):
+        return pl.ds(part * half, half)
+
+    barrier = pltpu.get_barrier_semaphore()
+    for peer in (sib, up, dn):
+        pl.semaphore_signal(barrier, inc=1, device_id={"exp": peer}, device_id_type=MESH)
+    pl.semaphore_wait(barrier, 3)
+
+    def remote(src, dst, slot, peer):
+        return pltpu.make_async_remote_copy(
+            src_ref=src, dst_ref=dst, send_sem=send_sems.at[slot],
+            recv_sem=recv_sems.at[slot], device_id={"exp": peer}, device_id_type=MESH,
+        )
+
+    mine = (me, up, dn, far)
+    theirs = tuple(block + 1 - 2 * core for block in mine)
+    sends = []
+    for k in range(4):
+        copy = remote(p_ref.at[:, cols(theirs[k])], sib_buf.at[k], k, sib)
+        copy.start()
+        sends.append(copy)
+    for k in range(4):
+        remote(p_ref.at[:, cols(mine[k])], sib_buf.at[k], k, sib).wait_recv()
+        acc[k] = p_ref[:, cols(mine[k])].astype(jnp.float32) + sib_buf[k].astype(jnp.float32)
+    stage[0] = acc[3].astype(stage.dtype)
+    for part, peer, slot in ((0, up, 4), (1, dn, 5)):
+        copy = remote(stage.at[0, rows(part)], half_buf.at[part], slot, peer)
+        copy.start()
+        sends.append(copy)
+    remote(stage.at[0, rows(0)], half_buf.at[0], 4, dn).wait_recv()
+    acc[1, rows(0)] = acc[1, rows(0)] + half_buf[0].astype(jnp.float32)
+    stage[1] = acc[1].astype(stage.dtype)
+    copy = remote(stage.at[1], near_buf.at[0], 6, up)
+    copy.start()
+    sends.append(copy)
+    remote(stage.at[0, rows(1)], half_buf.at[1], 5, up).wait_recv()
+    acc[2, rows(1)] = acc[2, rows(1)] + half_buf[1].astype(jnp.float32)
+    stage[2] = acc[2].astype(stage.dtype)
+    copy = remote(stage.at[2], near_buf.at[1], 7, dn)
+    copy.start()
+    sends.append(copy)
+    remote(stage.at[1], near_buf.at[0], 6, dn).wait_recv()
+    remote(stage.at[2], near_buf.at[1], 7, up).wait_recv()
+    o_ref[...] = (
+        acc[0] + near_buf[0].astype(jnp.float32) + near_buf[1].astype(jnp.float32)
+    ).astype(o_ref.dtype)
+    for copy in sends:
+        copy.wait_send()
+
+
+def exp_scatter(p, n, collective_id):
+    rows_n, width = p.shape[0], p.shape[1] // n
+    return pl.pallas_call(
+        functools.partial(exp_scatter_kernel, n),
+        out_shape=jax.ShapeDtypeStruct((rows_n, width), p.dtype),
+        in_specs=[pl.BlockSpec(memory_space=pltpu.VMEM)],
+        out_specs=pl.BlockSpec(memory_space=pltpu.VMEM),
+        scratch_shapes=[
+            pltpu.VMEM((4, rows_n, width), p.dtype),
+            pltpu.VMEM((4, rows_n, width), jnp.float32),
+            pltpu.VMEM((3, rows_n, width), p.dtype),
+            pltpu.VMEM((2, rows_n // 2, width), p.dtype),
+            pltpu.VMEM((2, rows_n, width), p.dtype),
+            pltpu.SemaphoreType.DMA((8,)),
+            pltpu.SemaphoreType.DMA((8,)),
+        ],
+        compiler_params=pltpu.CompilerParams(collective_id=collective_id, has_side_effects=True),
+    )(p)
 
 
 def pick_rows(source, row_index, live_slot):
@@ -189,22 +273,25 @@
     )
     send_index = jnp.sum(jnp.where(chosen_send, local_ids[None, None, :], 0), axis=2).reshape(-1)
     send_live = jnp.any(chosen_send, axis=2).reshape(-1)
-    moved_attn, moved_resid = (
-        lax.all_to_all(
-            pick_rows(attention_out, send_index, send_live),
-            "req",
-            split_axis=0,
-            concat_axis=0,
-            tiled=True,
-        ),
-        lax.all_to_all(
-            pick_rows(residual, send_index, send_live),
-            "req",
-            split_axis=0,
-            concat_axis=0,
-            tiled=True,
-        ),
-    )
+    page_rows = jnp.take(page_pool, page_table.reshape(-1), axis=0).reshape(
+        row_req, pages_req, page_len, kv_slice
+    )
+    position = (
+        jnp.arange(pages_req, dtype=jnp.int32)[:, None] * page_len
+        + jnp.arange(page_len, dtype=jnp.int32)[None, :]
+    )
+    kept_mask = position[None, :, :] < cache_len[:, None, None]
+    page_rows = jnp.where(kept_mask[..., None], page_rows, jnp.zeros((), page_rows.dtype)).reshape(
+        row_req, -1
+    )
+    payload = jnp.concatenate([attention_out, page_rows, residual], axis=1)
+    moved = exchange(
+        pick_rows(payload, send_index, send_live).reshape(groups, MIG_PAIR, -1),
+        "req",
+        groups,
+        False,
+        5,
+    ).reshape(groups * MIG_PAIR, -1)
     new_source = lax.dynamic_slice_in_dim(came_from, own_group * row_req, row_req)
     source_group = new_source // row_req
     stays_home = source_group == own_group
@@ -213,8 +300,13 @@
         new_source - own_group * row_req,
         row_req + source_group * MIG_PAIR + jnp.take(pair_rank, new_source),
     )
-    attn_new = jnp.take(jnp.concatenate([attention_out, moved_attn], axis=0), arrival, axis=0)
-    resid_new = jnp.take(jnp.concatenate([residual, moved_resid], axis=0), arrival, axis=0)
+    payload_new = jnp.take(jnp.concatenate([payload, moved], axis=0), arrival, axis=0)
+    d_attn, d_page = attention_out.shape[1], page_rows.shape[1]
+    attn_new = payload_new[:, :d_attn]
+    new_pages = payload_new[:, d_attn:d_attn + d_page].reshape(
+        row_req, pages_req, page_len, kv_slice
+    )
+    resid_new = payload_new[:, d_attn + d_page:]
     projected = jnp.dot(
         attn_new,
         lax.all_gather(w_out, "req", axis=0, tiled=True),
@@ -263,25 +355,7 @@
     partial_value = lax.optimization_barrier(
         jnp.dot(active, w_down[0], preferred_element_type=jnp.float32).astype(jnp.bfloat16)
     )
-    partial_value, page_pool = lax.optimization_barrier((partial_value, page_pool))
-    summed_value = lax.psum_scatter(partial_value, "exp", scatter_dimension=1, tiled=True)
-    page_rows = jnp.take(page_pool, page_table.reshape(-1), axis=0).reshape(
-        row_req, pages_req, page_len, kv_slice
-    )
-    position = (
-        jnp.arange(pages_req, dtype=jnp.int32)[:, None] * page_len
-        + jnp.arange(page_len, dtype=jnp.int32)[None, :]
-    )
-    kept_mask = position[None, :, :] < cache_len[:, None, None]
-    page_rows = jnp.where(kept_mask[..., None], page_rows, jnp.zeros((), page_rows.dtype)).reshape(
-        row_req, -1
-    )
-    moved_pages = lax.all_to_all(
-        pick_rows(page_rows, send_index, send_live), "req", split_axis=0, concat_axis=0, tiled=True
-    )
-    new_pages = jnp.take(
-        jnp.concatenate([page_rows, moved_pages], axis=0), arrival, axis=0
-    ).reshape(row_req, pages_req, page_len, kv_slice)
+    summed_value = exp_scatter(partial_value, lax.axis_size("exp"), 4)
     lookup = target_dev * CAP + slot_index
     returned = exchange(
         summed_value.reshape(groups, -1, summed_value.shape[-1]), "req", groups, False, 2

time: 213 us -> 234 us (1.099)
  Pallas kernels: 61.2 us -> 125 us
  waiting for transfers between devices: 35.6 us -> 0.7 us
  starting transfers between devices: 19.6 us -> 0.04 us
  other arithmetic: 17.7 us -> 26.1 us
    pallas_call x3 -> x4, Pallas kernels: 35.1 us -> 68.4 us  [exchange(): pl.pallas_call(functools.partial(exchange_kernel, axis, n, gather), out_s...]
    pallas_call x0 -> x1, Pallas kernels: none -> 29.5 us  [exp_scatter(): pl.pallas_call(functools.partial(exp_scatter_kernel, n), out_shape=jax.Sh...]
    all_to_all x3 -> x0, waiting for transfers between devices: 28 us -> none  [the longest x1 15.7 us: body(): lax.all_to_all(pick_rows(attention_out, send_index, send_live), 'req', sp...]
    all_to_all x3 -> x0, starting transfers between devices: 19.5 us -> none  [the longest x1 7.12 us: body(): lax.all_to_all(pick_rows(residual, send_index, send_live), 'req', split_a...]
    concatenate x3 -> x2, other arithmetic: 2.77 us -> 10.4 us  [the longest x1 9.07 us: body(): jnp.concatenate([payload, moved], axis=0)]
    reduce_scatter x1 -> x0, waiting for transfers between devices: 3.48 us -> none  [body(): lax.psum_scatter(partial_value, 'exp', scatter_dimension=1, tiled=True)]
    all_gather x1, waiting for transfers between devices: 3.41 us -> 0.02 us  [body(): lax.all_gather(w_out, 'req', axis=0, tiled=True)]
    unnamed x25 -> x21, local copies, waits for them, and re-layouts: 4.75 us -> 7.34 us
  transfers between devices with their start and end apart: 5 -> 1, of which waited for: 5 -> 0; matrix products, arithmetic and copies ran while one was open for 19% -> 22% of each run, Pallas kernels for 0% -> 13%
where the time goes in v6:
time: 234 us; the launch traced here: 233 us
  Pallas kernels  125 us (53%)
  local copies, waits for them, and re-layouts  36.4 us (16%)
  matrix products  30.3 us (13%)
  other arithmetic  26.1 us (11%)
  between operations  14.5 us (6%)
    pallas_call x4, Pallas kernels, exchange(): pl.pallas_call(functools.partial(exchange_kernel, axis, n, gather), out_s...  68.4 us
    pallas_call x1, Pallas kernels, exp_scatter(): pl.pallas_call(functools.partial(exp_scatter_kernel, n), out_shape=jax.Sh...  29.5 us
    pallas_call x1, Pallas kernels, exp_gather(): pl.pallas_call(functools.partial(exp_gather_kernel, n), out_shape=jax.Sha...  27.2 us
    dot_general x1, matrix products, body(): jnp.dot(active, w_down[0], preferred_element_type=jnp.float32)  16.6 us
    dot_general x1, matrix products, body(): gate_h = jnp.dot(rows_full, w_gate[0], preferred_element_type=jnp.float32)  10.2 us
    concatenate x1, other arithmetic, body(): jnp.concatenate([payload, moved], axis=0)  9.07 us
    scatter x1, local copies, waits for them, and re-layouts, body(): jnp.zeros((rows_all,), jnp.int32).at[came_from]  8.04 us
    unnamed x21, local copies, waits for them, and re-layouts  7.34 us
  transfers between devices with their start and end apart: 1, of which 0 were waited for; matrix products, arithmetic and copies ran while one was open for 22% of the time, Pallas kernels for 13%

profile of v6, /device:TPU:0, one launch (start us, length us, event | category | flops | bytes accessed | tf_op | source)
XLA Modules:
  0.0 233.1 jit_solution(1564473341319881276)
XLA Ops:
  7.2 0.7 all-gather.2.cloned.1.call-update
  7.9 0.8 copy.120
  9.2 0.6 reduce-window.6
  10.3 0.7 compare_select_fusion.1
  11.0 0.8 compare_select_fusion.14
  11.8 8.0 %scatter_custom_fusion = s32[2048]{0:T(1024)S(1)} fusion(s32[2048]{0:T(1024)S(1)} %compare_select_fusion.1, s32[2048]{0:T(1024)S(1)} %iota.72, s32[]{:T(128)} %constant.163.clone.1), kind=kCustom, calls=%fused_computation.85 | custom fusion | bytes 8196 | tf_op jit(solution)/shard_map/scatter | solution.py:258
  20.0 2.8 %select_reduce_fusion = s32[16,128]{0,1:T(8,128)S(1)} fusion(s32[16,128]{0,1:T(8,128)S(1)} %copy.113), kind=kOutput, calls=%fused_computation.26 | output fusion | flops 4388864 | bytes 16384 | tf_op jit(solution)/shard_map/jit(cumsum)/reduce_window_sum | solution.py:264
  23.5 0.7 compare_and_fusion.3
  24.2 0.8 copy.116
  25.2 0.4 fusion.18
  25.7 1.2 gather_fusion
  27.4 0.9 broadcast_compare_fusion
  28.2 0.4 broadcast_in_dim.173
  28.7 1.1 copy.128
  29.8 0.4 broadcast_in_dim.175
  30.2 1.1 copy.129
  31.3 0.8 gather_fusion.1
  32.1 0.5 gather.34
  32.6 1.4 select_select_fusion.1
  34.0 1.0 copy-done.1
  35.0 1.4 pad_maximum_fusion.1
  36.4 2.2 gather_fusion.2
  38.6 1.4 gather.36
  40.0 1.6 select_select_fusion.x_ref
  41.6 30.9 %shard_map.140 = bf16[16,4,8704]{2,1,0:T(4,128)(2,1)} custom-call(bf16[16,4,8704]{2,1,0:T(4,128)(2,1)} %select_select_fusion.x_ref), custom_call_target="tpu_custom_call" | custom-call | tf_op jit(solution)/shard_map/pallas_call | solution.py:59
  72.5 1.4 reshape.518
  73.9 0.8 compare_and_fusion.4
  74.7 9.1 %pad_maximum_fusion = bf16[192,8704]{1,0:T(8,128)(2,1)} fusion(bf16[64,8704]{1,0:T(8,128)(2,1)S(1)} %reshape.518, bf16[128,512]{1,0:T(8,128)(2,1)S(1)} %copy-done.4, bf16[128,4096]{1,0:T(8,128)(2,1)S(1)} %copy-done.2, bf16[128,4096]{1,0:T(8,128)(2,1)} %param.13), kind=kLoop, calls=%fused_computation.14 | loop fusion | flops 13369344 | bytes 6684672 | tf_op jit(solution)/shard_map/concatenate | solution.py:303
  83.8 6.3 %gather_fusion.3 = bf16[128,8704]{1,0:T(8,128)(2,1)S(1)} fusion(bf16[192,8704]{1,0:T(8,128)(2,1)} %pad_maximum_fusion, s32[1024]{0:T(1024)S(1)} %pad_clamp_fusion.2), kind=kCustom, calls=%fused_computation.3 | custom fusion | bytes 4456960 | tf_op jit(solution)/shard_map/jit(_take)/gather | solution.py:303
  90.1 0.3 broadcast_select_fusion
  90.4 1.4 copy-done.3
  91.9 1.2 copy.130
  93.2 0.4 and_reduce_fusion
  93.6 3.3 %multiply_reduce_fusion = (f32[128]{0:T(128)S(1)}, f32[128,512]{1,0:T(8,128)S(1)}) fusion(bf16[4096,512]{1,0:T(8,128)(2,1)} %all-gather.2.cloned.1.call-done, bf16[128,8704]{1,0:T(8,128)(2,1)} %copy-done.3), kind=kOutput, calls=%fused_computation.42 | convolution fusion | flops 537132928 | bytes 5636608 | tf_op jit(solution)/shard_map/dot_general | solution.py:310
  96.9 0.3 convolution_bitcast_fusion
  97.2 0.7 select_maximum_fusion.x_ref
  97.9 9.0 %shard_map.141 = f32[8,16,128]{2,1,0:T(8,128)} custom-call(f32[16,128]{1,0:T(8,128)} %select_maximum_fusion.x_ref), custom_call_target="tpu_custom_call" | custom-call | tf_op jit(solution)/shard_map/pallas_call | solution.py:59
  106.9 0.9 reduce_sum.70
  107.9 2.0 gather_fusion.4
  109.8 1.0 select_select_fusion.2.x_ref
  110.8 16.3 %shard_map.142 = bf16[16,32,512]{2,1,0:T(8,128)(2,1)} custom-call(bf16[16,32,512]{2,1,0:T(8,128)(2,1)} %select_select_fusion.2.x_ref), custom_call_target="tpu_custom_call" | custom-call | tf_op jit(solution)/shard_map/pallas_call | solution.py:59
  127.2 27.2 %shard_map.143 = bf16[512,4096]{1,0:T(8,128)(2,1)} custom-call(bf16[512,512]{1,0:T(8,128)(2,1)} %bitcast.80), custom_call_target="tpu_custom_call" | custom-call | tf_op jit(solution)/shard_map/pallas_call | solution.py:133
  154.4 10.2 %fusion.4 = f32[512,896]{1,0:T(8,128)} fusion(bf16[512,4096]{1,0:T(8,128)(2,1)} %shard_map.143, bf16[1,4096,896]{2,1,0:T(8,128)(2,1)} %param.23), kind=kOutput, calls=%fused_computation.11 | convolution fusion | flops 3758096384 | bytes 13369344 | tf_op jit(solution)/shard_map/dot_general | solution.py:352
  164.5 16.6 %fusion.6.p_ref = bf16[512,4096]{1,0:T(8,128)(2,1)} fusion(bf16[1,896,4096]{2,1,0:T(8,128)(2,1)} %param.25, f32[512,896]{1,0:T(8,128)} %fusion.4, bf16[512,4096]{1,0:T(8,128)(2,1)} %shard_map.143, bf16[1,4096,896]{2,1,0:T(8,128)(2,1)} %param.24), kind=kOutput, calls=%fused_computation.13 | convolution fusion | flops 7521042432 | bytes 24903680 | tf_op jit(solution)/shard_map/dot_general | solution.py:356
  181.1 29.5 %shard_map.144 = bf16[512,512]{1,0:T(8,128)(2,1)} custom-call(bf16[512,4096]{1,0:T(8,128)(2,1)} %fusion.6.p_ref), custom_call_target="tpu_custom_call" | custom-call | tf_op jit(solution)/shard_map/pallas_call | solution.py:209
  210.6 12.3 %shard_map.145 = bf16[16,32,512]{2,1,0:T(8,128)(2,1)} custom-call(bf16[16,32,512]{2,1,0:T(8,128)(2,1)} %bitcast.81), custom_call_target="tpu_custom_call" | custom-call | tf_op jit(solution)/shard_map/pallas_call | solution.py:59
  222.9 2.3 gather_fusion.5
  225.5 0.8 fusion.22
  (72 shorter events, 3.3 us)
Async XLA Ops:
  7.2 24.1 %copy-start = (bf16[256,8,256]{2,1,0:T(8,128)(2,1)S(1)}, bf16[256,8,256]{2,1,0:T(8,128)(2,1)}, u32[]{:S(2)}) copy-start(bf16[256,8,256]{2,1,0:T(8,128)(2,1)} %param.18) | copy-start | bytes 3145732
  7.2 86.4 %all-gather.2.cloned.1.call-start = ((), (), s32[]{:S(2)}) async-start(), calls=%async_computation | async-start | bytes 4456448 | tf_op jit(solution)/shard_map/all_gather | solution.py:312
  31.3 3.7 %copy-start.4 = (bf16[128,512]{1,0:T(8,128)(2,1)S(1)}, bf16[128,512]{1,0:T(8,128)(2,1)}, u32[]{:S(2)}) copy-start(bf16[128,512]{1,0:T(8,128)(2,1)} %param.14) | copy-start | bytes 393220
  34.0 1.0 copy-start.1
  40.0 34.7 %copy-start.2 = (bf16[128,4096]{1,0:T(8,128)(2,1)S(1)}, bf16[128,4096]{1,0:T(8,128)(2,1)}, u32[]{:S(2)}) copy-start(bf16[128,4096]{1,0:T(8,128)(2,1)} %copy-done.1) | copy-start | bytes 3145732
  90.1 3.4 %copy-start.6 = (s32[128,2]{0,1:T(2,128)S(1)}, s32[128,2]{0,1:T(2,128)}, u32[]{:S(2)}) copy-start(s32[128,2]{0,1:T(2,128)} %param.22) | copy-start | bytes 3076
  90.4 1.4 copy-start.3
  91.9 5.0 %copy-start.5 = (f32[512,8]{0,1:T(8,128)S(1)}, f32[512,8]{0,1:T(8,128)}, u32[]{:S(2)}) copy-start(f32[512,8]{0,1:T(8,128)} %param.16) | copy-start | bytes 49156
  91.9 5.0 %copy-start.7 = (f32[512]{0:T(512)S(1)}, f32[512]{0:T(512)}, u32[]{:S(2)}) copy-start(f32[512]{0:T(512)} %param.17) | copy-start | bytes 6148
Sparse Core Ops, SparseCore 0:
  10.2 65.8 all-gather.1

commit v7 on v5

--- a/solution.py
+++ b/solution.py
@@ -140,6 +140,56 @@
     )(x)
 
 
+def ffn_kernel(x_ref, wg_ref, wu_ref, wd_ref, o_ref, g_acc, u_acc):
+    step = pl.program_id(0)
+
+    @pl.when(step == 0)
+    def _():
+        g_acc[...] = jnp.zeros_like(g_acc)
+        u_acc[...] = jnp.zeros_like(u_acc)
+
+    x = x_ref[...]
+    g_acc[...] += jnp.dot(x, wg_ref[...], preferred_element_type=jnp.float32)
+    u_acc[...] += jnp.dot(x, wu_ref[...], preferred_element_type=jnp.float32)
+
+    @pl.when(step == pl.num_programs(0) - 1)
+    def _():
+        g = g_acc[...]
+        act = (g / (1.0 + jnp.exp(-g)) * u_acc[...]).astype(wd_ref.dtype)
+        o_ref[...] = jnp.dot(act, wd_ref[...], preferred_element_type=jnp.float32).astype(
+            o_ref.dtype
+        )
+
+
+def expert_ffn(x, wg, wu, wd, tk=512):
+    rows_n, d = x.shape
+    ff = wg.shape[1]
+    return pl.pallas_call(
+        ffn_kernel,
+        out_shape=jax.ShapeDtypeStruct((rows_n, wd.shape[1]), x.dtype),
+        grid=(d // tk,),
+        in_specs=[
+            pl.BlockSpec((rows_n, tk), lambda k: (0, k)),
+            pl.BlockSpec((tk, ff), lambda k: (k, 0)),
+            pl.BlockSpec((tk, ff), lambda k: (k, 0)),
+            pl.BlockSpec((ff, wd.shape[1]), lambda k: (0, 0)),
+        ],
+        out_specs=pl.BlockSpec((rows_n, wd.shape[1]), lambda k: (0, 0)),
+        scratch_shapes=[
+            pltpu.VMEM((rows_n, ff), jnp.float32),
+            pltpu.VMEM((rows_n, ff), jnp.float32),
+        ],
+        compiler_params=pltpu.CompilerParams(
+            dimension_semantics=("arbitrary",), vmem_limit_bytes=56 * 1024 * 1024
+        ),
+        cost_estimate=pl.CostEstimate(
+            flops=2 * rows_n * d * ff * 2 + 2 * rows_n * ff * wd.shape[1],
+            transcendentals=rows_n * ff,
+            bytes_accessed=2 * (rows_n * d + 2 * d * ff + ff * wd.shape[1] + rows_n * wd.shape[1]),
+        ),
+    )(x, wg, wu, wd)
+
+
 def pick_rows(source, row_index, live_slot):
     taken_rows = jnp.take(source, row_index, axis=0)
     return jnp.where(live_slot[:, None], taken_rows, jnp.zeros((), source.dtype))
@@ -257,12 +307,7 @@
         outgoing.reshape(groups, -1, outgoing.shape[-1]), "req", groups, False, 1
     ).reshape(outgoing.shape)
     rows_full = exp_gather(arrived, lax.axis_size("exp"), 3)
-    gate_h = jnp.dot(rows_full, w_gate[0], preferred_element_type=jnp.float32)
-    up_h = jnp.dot(rows_full, w_up[0], preferred_element_type=jnp.float32)
-    active = (jax.nn.silu(gate_h) * up_h).astype(jnp.bfloat16)
-    partial_value = lax.optimization_barrier(
-        jnp.dot(active, w_down[0], preferred_element_type=jnp.float32).astype(jnp.bfloat16)
-    )
+    partial_value = expert_ffn(rows_full, w_gate[0], w_up[0], w_down[0])
     partial_value, page_pool = lax.optimization_barrier((partial_value, page_pool))
     summed_value = lax.psum_scatter(partial_value, "exp", scatter_dimension=1, tiled=True)
     page_rows = jnp.take(page_pool, page_table.reshape(-1), axis=0).reshape(

time: 213 us -> 209 us (0.981)
  matrix products: 29.7 us -> 3.62 us
  Pallas kernels: 61.2 us -> 83.2 us
    dot_general x2 -> x0, matrix products: 26.1 us -> none  [the longest x1 16.2 us: body(): jnp.dot(active, w_down[0], preferred_element_type=jnp.float32)]
    pallas_call x0 -> x1, Pallas kernels: none -> 22.2 us  [expert_ffn(): pl.pallas_call(ffn_kernel, out_shape=jax.ShapeDtypeStruct((rows_n, wd.sha...]
    unnamed x25 -> x23, local copies, waits for them, and re-layouts: 4.75 us -> 4.74 us
where the time goes in v7:
time: 209 us; the launch traced here: 208 us
  Pallas kernels  83.2 us (40%)
  waiting for transfers between devices  36.4 us (17%)
  local copies, waits for them, and re-layouts  33.6 us (16%)
  starting transfers between devices  19.1 us (9%)
  other arithmetic  17.8 us (9%)
  between operations  14.6 us (7%)
  matrix products  3.62 us (2%)
    pallas_call x3, Pallas kernels, exchange(): pl.pallas_call(functools.partial(exchange_kernel, axis, n, gather), out_s...  35 us
    pallas_call x1, Pallas kernels, exp_gather(): pl.pallas_call(functools.partial(exp_gather_kernel, n), out_shape=jax.Sha...  26.1 us
    pallas_call x1, Pallas kernels, expert_ffn(): pl.pallas_call(ffn_kernel, out_shape=jax.ShapeDtypeStruct((rows_n, wd.sha...  22.2 us
    all_to_all x1, waiting for transfers between devices, body(): lax.all_to_all(pick_rows(attention_out, send_index, send_live), 'req', sp...  16.4 us
    all_to_all x1, waiting for transfers between devices, body(): lax.all_to_all(pick_rows(page_rows, send_index, send_live), 'req', split_...  12 us
    scatter x1, local copies, waits for them, and re-layouts, body(): jnp.zeros((rows_all,), jnp.int32).at[came_from]  8.04 us
    all_to_all x1, starting transfers between devices, body(): lax.all_to_all(pick_rows(residual, send_index, send_live), 'req', split_a...  7.12 us
    all_to_all x1, starting transfers between devices, body(): lax.all_to_all(pick_rows(attention_out, send_index, send_live), 'req', sp...  6.97 us
  transfers between devices with their start and end apart: 5, of which 5 were waited for; matrix products, arithmetic and copies ran while one was open for 19% of the time, Pallas kernels for 0%

profile of v7, /device:TPU:0, one launch (start us, length us, event | category | flops | bytes accessed | tf_op | source)
XLA Modules:
  0.0 208.4 jit_solution(13841357049470570844)
XLA Ops:
  7.2 0.7 all-gather.2.cloned.1.call-update
  7.9 0.7 compare_select_fusion.1
  8.6 8.0 %scatter_custom_fusion = s32[2048]{0:T(1024)S(1)} fusion(s32[2048]{0:T(1024)S(1)} %compare_select_fusion.1, s32[2048]{0:T(1024)S(1)} %iota.72, s32[]{:T(128)} %constant.181.clone.1), kind=kCustom, calls=%fused_computation.87 | custom fusion | bytes 8196 | tf_op jit(solution)/shard_map/scatter | solution.py:224
  16.8 2.8 %select_reduce_fusion = s32[16,128]{0,1:T(8,128)S(1)} fusion(s32[16,128]{0,1:T(8,128)S(1)} %copy.115), kind=kOutput, calls=%fused_computation.20 | output fusion | flops 4388864 | bytes 16384 | tf_op jit(solution)/shard_map/jit(cumsum)/reduce_window_sum | solution.py:230
  20.6 1.6 gather_fusion.1
  22.4 0.8 select_select_fusion.4
  23.1 7.1 %all-to-all-start = ((bf16[16,4,512]{2,1,0:T(4,128)(2,1)}), bf16[16,4,512]{2,1,0:T(4,128)(2,1)S(1)}, u32[]{:S(2)}, u32[]{:S(2)}) async-start(bf16[16,4,512]{2,1,0:T(4,128)(2,1)} %select_select_fusion.4), calls=%async_computation | async-start | bytes 131072 | tf_op jit(solution)/shard_map/all_to_all | solution.py:250
  30.4 0.8 copy.122
  31.5 0.9 gather_fusion.6
  32.6 1.0 all_to_all.24
  33.6 0.8 compare_select_fusion.15
  34.3 1.1 gather_fusion
  35.5 0.6 reduce-window.6
  36.9 0.8 compare_and_fusion.5
  38.0 7.0 %all-to-all-start.1 = ((bf16[16,4,4096]{2,1,0:T(4,128)(2,1)}), bf16[16,4,4096]{2,1,0:T(4,128)(2,1)S(1)}, u32[]{:S(2)}, u32[]{:S(2)}) async-start(bf16[16,4,4096]{2,1,0:T(4,128)(2,1)} %all_to_all.24), calls=%async_computation.1 | async-start | bytes 1048576 | tf_op jit(solution)/shard_map/all_to_all | solution.py:243
  45.5 0.8 gather_fusion.2
  46.3 16.4 %all-to-all-done.1 = bf16[16,4,4096]{2,1,0:T(4,128)(2,1)S(1)} async-done(((bf16[16,4,4096]{2,1,0:T(4,128)(2,1)}), bf16[16,4,4096]{2,1,0:T(4,128)(2,1)S(1)}, u32[]{:S(2)}, u32[]{:S(2)}) %all-to-all-start.1) | async-done | bytes 524320 | tf_op jit(solution)/shard_map/all_to_all | solution.py:243
  62.9 1.4 pad_maximum_fusion
  64.2 2.2 %gather_fusion.7 = bf16[128,4096]{1,0:T(8,128)(2,1)} fusion(bf16[192,4096]{1,0:T(8,128)(2,1)S(1)} %pad_maximum_fusion, s32[1024]{0:T(1024)S(1)} %pad_clamp_fusion.4), kind=kCustom, calls=%fused_computation.1.clone | custom fusion | bytes 2097664 | tf_op jit(solution)/shard_map/jit(_take)/gather | solution.py:266
  66.4 3.4 %all-gather.2.cloned.1.call-done = bf16[4096,512]{1,0:T(8,128)(2,1)} async-done(((bf16[256,512]{1,0:T(8,128)(2,1)}), bf16[4096,512]{1,0:T(8,128)(2,1)}) %all-gather.2.cloned.1.call-update) | async-done | bytes 4194320 | tf_op jit(solution)/shard_map/all_gather | solution.py:270
  69.8 3.4 %multiply_reduce_fusion = (f32[128]{0:T(128)S(1)}, f32[128,512]{1,0:T(8,128)S(1)}) fusion(bf16[4096,512]{1,0:T(8,128)(2,1)} %all-gather.2.cloned.1.call-done, bf16[128,4096]{1,0:T(8,128)(2,1)} %gather_fusion.7, pred[128]{0:T(512)(128)(4,1)S(1)} %get-tuple-element.8, bf16[128,512]{1,0:T(8,128)(2,1)S(1)} %gather_fusion.2), kind=kOutput, calls=%fused_computation.41 | convolution fusion | flops 537722752 | bytes 5636736 | tf_op jit(solution)/shard_map/dot_general | solution.py:268
  73.5 0.7 select_maximum_fusion.x_ref
  74.2 7.7 %shard_map.140 = f32[8,16,128]{2,1,0:T(8,128)} custom-call(f32[16,128]{1,0:T(8,128)} %select_maximum_fusion.x_ref), custom_call_target="tpu_custom_call" | custom-call | tf_op jit(solution)/shard_map/pallas_call | solution.py:59
  81.8 0.9 reduce_sum.70
  82.8 2.2 %gather_fusion.3 = bf16[512,512]{1,0:T(8,128)(2,1)S(1)} fusion(bf16[128,512]{1,0:T(8,128)(2,1)S(1)} %multiply_convert_fusion, s32[1024]{0:T(1024)S(1)} %pad_clamp_fusion.2), kind=kCustom, calls=%fused_computation.7 | custom fusion | bytes 1050624 | tf_op jit(solution)/shard_map/jit(_take)/gather | solution.py:194
  85.0 1.0 select_select_fusion.3.x_ref
  86.0 14.4 %shard_map.141 = bf16[16,32,512]{2,1,0:T(8,128)(2,1)} custom-call(bf16[16,32,512]{2,1,0:T(8,128)(2,1)} %select_select_fusion.3.x_ref), custom_call_target="tpu_custom_call" | custom-call | tf_op jit(solution)/shard_map/pallas_call | solution.py:59
  100.4 26.1 %shard_map.142.x_ref = bf16[512,4096]{1,0:T(8,128)(2,1)} custom-call(bf16[512,512]{1,0:T(8,128)(2,1)} %bitcast.65), custom_call_target="tpu_custom_call" | custom-call | tf_op jit(solution)/shard_map/pallas_call | solution.py:133
  126.4 22.2 %shard_map.143 = bf16[512,4096]{1,0:T(8,128)(2,1)} custom-call(bf16[512,4096]{1,0:T(8,128)(2,1)} %shard_map.142.x_ref, bf16[4096,896]{1,0:T(8,128)(2,1)} %bitcast.77, bf16[4096,896]{1,0:T(8,128)(2,1)} %bitcast.78, bf16[896,4096]{1,0:T(8,128)(2,1)} %bitcast.79), custom_call_target="tpu_custom_call" | custom-call | flops 11274289152 | bytes 30408704 | tf_op jit(solution)/shard_map/pallas_call | solution.py:167
  149.9 0.4 broadcast_in_dim.231
  150.3 1.1 copy.132
  151.5 0.4 broadcast_in_dim.233
  152.0 1.1 copy.133
  153.3 0.8 gather_fusion.5
  154.0 0.5 gather.47
  154.6 1.6 select_select_fusion
  156.2 0.9 gather_fusion.8
  157.2 1.0 all_to_all.27
  158.2 5.0 %all-to-all-start.2 = ((bf16[16,4,4096]{2,1,0:T(4,128)(2,1)}), bf16[16,4,4096]{2,1,0:T(4,128)(2,1)S(1)}, u32[]{:S(2)}, u32[]{:S(2)}) async-start(bf16[16,4,4096]{2,1,0:T(4,128)(2,1)} %all_to_all.27), calls=%async_computation.3 | async-start | bytes 1048576 | tf_op jit(solution)/shard_map/all_to_all | solution.py:324
  163.3 12.0 %all-to-all-done.2 = bf16[16,4,4096]{2,1,0:T(4,128)(2,1)S(1)} async-done(((bf16[16,4,4096]{2,1,0:T(4,128)(2,1)}), bf16[16,4,4096]{2,1,0:T(4,128)(2,1)S(1)}, u32[]{:S(2)}, u32[]{:S(2)}) %all-to-all-start.2) | async-done | bytes 524320 | tf_op jit(solution)/shard_map/all_to_all | solution.py:324
  175.4 1.4 pad_maximum_fusion.1
  176.8 2.2 %gather_fusion.9 = bf16[128,4096]{1,0:T(8,128)(2,1)} fusion(bf16[192,4096]{1,0:T(8,128)(2,1)S(1)} %pad_maximum_fusion.1, s32[1024]{0:T(1024)S(1)} %pad_clamp_fusion.4), kind=kCustom, calls=%fused_computation.3.clone | custom fusion | bytes 2097664 | tf_op jit(solution)/shard_map/jit(_take)/gather | solution.py:327
  178.9 1.4 broadcast_select_fusion
  180.3 1.2 copy.134
  181.6 3.6 %reduce-scatter.2.cloned.1.call-done = bf16[512,512]{1,0:T(8,128)(2,1)} async-done(((bf16[512,4096]{1,0:T(8,128)(2,1)}), bf16[512,512]{1,0:T(8,128)(2,1)}) %reduce-scatter.2.cloned.1.call-update) | async-done | bytes 524304 | tf_op jit(solution)/shard_map/reduce_scatter | solution.py:312
  185.2 12.9 %shard_map.144 = bf16[16,32,512]{2,1,0:T(8,128)(2,1)} custom-call(bf16[16,32,512]{2,1,0:T(8,128)(2,1)} %bitcast.71), custom_call_target="tpu_custom_call" | custom-call | tf_op jit(solution)/shard_map/pallas_call | solution.py:59
  198.1 2.3 %gather_fusion.4 = bf16[256,512]{1,0:T(8,128)(2,1)S(1)} fusion(bf16[512,512]{1,0:T(8,128)(2,1)} %bitcast.62, s32[1024]{0:T(1024)S(1)} %pad_clamp_fusion.1), kind=kCustom, calls=%fused_computation.8 | custom fusion | bytes 525312 | tf_op jit(solution)/shard_map/jit(_take)/gather | solution.py:334
  200.7 0.8 fusion.11
  (95 shorter events, 5.9 us)
Async XLA Ops:
  7.2 146.1 %copy-start = (bf16[256,8,256]{2,1,0:T(8,128)(2,1)S(1)}, bf16[256,8,256]{2,1,0:T(8,128)(2,1)}, u32[]{:S(2)}) copy-start(bf16[256,8,256]{2,1,0:T(8,128)(2,1)} %param.22) | copy-start | bytes 3145732
  7.2 24.4 %copy-start.2 = (bf16[128,4096]{1,0:T(8,128)(2,1)S(1)}, bf16[128,4096]{1,0:T(8,128)(2,1)}, u32[]{:S(2)}) copy-start(bf16[128,4096]{1,0:T(8,128)(2,1)} %param.17) | copy-start | bytes 3145732
  7.2 62.6 %all-gather.2.cloned.1.call-start = ((), (), s32[]{:S(2)}) async-start(), calls=%async_computation.4 | async-start | bytes 4456448 | tf_op jit(solution)/shard_map/all_gather | solution.py:270
  23.1 14.9 %all-to-all-start = ((bf16[16,4,512]{2,1,0:T(4,128)(2,1)}), bf16[16,4,512]{2,1,0:T(4,128)(2,1)S(1)}, u32[]{:S(2)}, u32[]{:S(2)}) async-start(bf16[16,4,512]{2,1,0:T(4,128)(2,1)} %select_select_fusion.4), calls=%async_computation | async-start | bytes 131072 | tf_op jit(solution)/shard_map/all_to_all | solution.py:250
  32.4 13.0 %copy-start.3 = (bf16[128,512]{1,0:T(8,128)(2,1)S(1)}, bf16[128,512]{1,0:T(8,128)(2,1)}, u32[]{:S(2)}) copy-start(bf16[128,512]{1,0:T(8,128)(2,1)} %param.18) | copy-start | bytes 393220
  38.0 24.7 %all-to-all-start.1 = ((bf16[16,4,4096]{2,1,0:T(4,128)(2,1)}), bf16[16,4,4096]{2,1,0:T(4,128)(2,1)S(1)}, u32[]{:S(2)}, u32[]{:S(2)}) async-start(bf16[16,4,4096]{2,1,0:T(4,128)(2,1)} %all_to_all.24), calls=%async_computation.1 | async-start | bytes 1048576 | tf_op jit(solution)/shard_map/all_to_all | solution.py:243
  45.0 140.2 %reduce-scatter.2.cloned.1.call-start = ((), (), s32[]{:S(2)}) async-start(), calls=%async_computation.5 | async-start | bytes 4718592 | tf_op jit(solution)/shard_map/reduce_scatter | solution.py:312
  66.4 6.8 %copy-start.4 = (f32[512,8]{0,1:T(8,128)S(1)}, f32[512,8]{0,1:T(8,128)}, u32[]{:S(2)}) copy-start(f32[512,8]{0,1:T(8,128)} %param.20) | copy-start | bytes 49156
  66.4 6.8 %copy-start.6 = (f32[512]{0:T(512)S(1)}, f32[512]{0:T(512)}, u32[]{:S(2)}) copy-start(f32[512]{0:T(512)} %param.21) | copy-start | bytes 6148
  148.6 0.7 copy-start.7
  148.6 1.0 copy-start.8
  148.6 4.6 %copy-start.5 = (s32[128,2]{0,1:T(2,128)S(1)}, s32[128,2]{0,1:T(2,128)}, u32[]{:S(2)}) copy-start(s32[128,2]{0,1:T(2,128)} %param.26) | copy-start | bytes 3076
  156.2 2.0 copy-start.1
  158.2 17.0 %all-to-all-start.2 = ((bf16[16,4,4096]{2,1,0:T(4,128)(2,1)}), bf16[16,4,4096]{2,1,0:T(4,128)(2,1)S(1)}, u32[]{:S(2)}, u32[]{:S(2)}) async-start(bf16[16,4,4096]{2,1,0:T(4,128)(2,1)} %all_to_all.27), calls=%async_computation.3 | async-start | bytes 1048576 | tf_op jit(solution)/shard_map/all_to_all | solution.py:324
Sparse Core Ops, SparseCore 0:
  10.2 59.6 all-gather.1
  148.8 36.3 reduce-scatter.1

commit v8 on v7

--- a/solution.py
+++ b/solution.py
@@ -190,6 +190,131 @@
     )(x, wg, wu, wd)
 
 
+def gather_ffn_kernel(
+    n, x_ref, wg_hbm, wu_hbm, wd_hbm, o_ref,
+    y_ref, wg_v, wu_v, wd_v, g_acc, u_acc, send_sems, recv_sems, w_sems,
+):
+    chips = n // 2
+    width = x_ref.shape[1]
+    half = x_ref.shape[0] // 2
+    me = lax.axis_index("exp")
+    z, core = me // 2, me % 2
+    sib = 2 * z + 1 - core
+    up = 2 * lax.rem(z + 1, chips) + core
+    dn = 2 * lax.rem(z + chips - 1, chips) + core
+    far = 2 * lax.rem(z + 2, chips) + core
+
+    weight_copies = [
+        pltpu.make_async_copy(src.at[0], dst, w_sems.at[i])
+        for i, (src, dst) in enumerate(((wg_hbm, wg_v), (wu_hbm, wu_v), (wd_hbm, wd_v)))
+    ]
+    for copy in weight_copies:
+        copy.start()
+
+    def cols(block):
+        return pl.ds(pl.multiple_of(block * width, width), width)
+
+    def rows(part):
+        return pl.ds(part * half, half)
+
+    barrier = pltpu.get_barrier_semaphore()
+    for peer in (sib, up, dn):
+        pl.semaphore_signal(barrier, inc=1, device_id={"exp": peer}, device_id_type=MESH)
+    pl.semaphore_wait(barrier, 3)
+
+    def remote(src, dst, slot, peer):
+        return pltpu.make_async_remote_copy(
+            src_ref=src, dst_ref=dst, send_sem=send_sems.at[slot],
+            recv_sem=recv_sems.at[slot], device_id={"exp": peer}, device_id_type=MESH,
+        )
+
+    def consume(block, first=False):
+        rows_in = x_ref[...] if first else y_ref[:, cols(block)]
+        w_rows = pl.ds(pl.multiple_of(block * width, width), width)
+        g_part = jnp.dot(rows_in, wg_v[w_rows, :], preferred_element_type=jnp.float32)
+        u_part = jnp.dot(rows_in, wu_v[w_rows, :], preferred_element_type=jnp.float32)
+        if first:
+            g_acc[...] = g_part
+            u_acc[...] = u_part
+        else:
+            g_acc[...] += g_part
+            u_acc[...] += u_part
+
+    own_cols = cols(me)
+    sends = [
+        remote(x_ref, y_ref.at[:, own_cols], 0, up),
+        remote(x_ref, y_ref.at[:, own_cols], 1, dn),
+        remote(x_ref, y_ref.at[:, own_cols], 2, sib),
+    ]
+    for copy in sends:
+        copy.start()
+    weight_copies[0].wait()
+    weight_copies[1].wait()
+    consume(me, first=True)
+    remote(x_ref, y_ref.at[:, cols(dn)], 0, dn).wait_recv()
+    remote(x_ref, y_ref.at[:, cols(up)], 1, up).wait_recv()
+    second = [
+        remote(y_ref.at[rows(1), cols(dn)], y_ref.at[rows(1), cols(dn)], 3, up),
+        remote(y_ref.at[rows(0), cols(up)], y_ref.at[rows(0), cols(up)], 4, dn),
+        remote(y_ref.at[:, cols(dn)], y_ref.at[:, cols(dn)], 5, sib),
+        remote(y_ref.at[:, cols(up)], y_ref.at[:, cols(up)], 6, sib),
+    ]
+    for copy in second:
+        copy.start()
+    sends += second
+    consume(dn)
+    consume(up)
+    remote(y_ref.at[rows(1), cols(far)], y_ref.at[rows(1), cols(far)], 3, dn).wait_recv()
+    remote(y_ref.at[rows(0), cols(far)], y_ref.at[rows(0), cols(far)], 4, up).wait_recv()
+    third = remote(y_ref.at[:, cols(far)], y_ref.at[:, cols(far)], 7, sib)
+    third.start()
+    sends.append(third)
+    consume(far)
+    sib_up = 2 * lax.rem(z + 1, chips) + 1 - core
+    sib_dn = 2 * lax.rem(z + chips - 1, chips) + 1 - core
+    sib_far = 2 * lax.rem(z + 2, chips) + 1 - core
+    for block, slot in ((sib, 2), (sib_dn, 5), (sib_up, 6), (sib_far, 7)):
+        remote(y_ref.at[:, cols(block)], y_ref.at[:, cols(block)], slot, sib).wait_recv()
+        consume(block)
+    g = g_acc[...]
+    act = (g / (1.0 + jnp.exp(-g)) * u_acc[...]).astype(wd_v.dtype)
+    weight_copies[2].wait()
+    out_cols = o_ref.shape[1]
+    chunk = out_cols // 8
+    for c in range(8):
+        span = pl.ds(c * chunk, chunk)
+        o_ref[:, span] = jnp.dot(act, wd_v[:, span], preferred_element_type=jnp.float32).astype(
+            o_ref.dtype
+        )
+    for copy in sends:
+        copy.wait_send()
+
+
+def gather_ffn(x, w_gate, w_up, w_down, n, collective_id):
+    rows_n, width = x.shape
+    d, ff = w_gate.shape[1], w_gate.shape[2]
+    return pl.pallas_call(
+        functools.partial(gather_ffn_kernel, n),
+        out_shape=jax.ShapeDtypeStruct((rows_n, w_down.shape[2]), x.dtype),
+        in_specs=[pl.BlockSpec(memory_space=pltpu.VMEM)] + [pl.BlockSpec(memory_space=pl.ANY)] * 3,
+        out_specs=pl.BlockSpec(memory_space=pltpu.VMEM),
+        scratch_shapes=[
+            pltpu.VMEM((rows_n, n * width), x.dtype),
+            pltpu.VMEM((d, ff), w_gate.dtype),
+            pltpu.VMEM((d, ff), w_up.dtype),
+            pltpu.VMEM((ff, w_down.shape[2]), w_down.dtype),
+            pltpu.VMEM((rows_n, ff), jnp.float32),
+            pltpu.VMEM((rows_n, ff), jnp.float32),
+            pltpu.SemaphoreType.DMA((8,)),
+            pltpu.SemaphoreType.DMA((8,)),
+            pltpu.SemaphoreType.DMA((3,)),
+        ],
+        compiler_params=pltpu.CompilerParams(
+            collective_id=collective_id, has_side_effects=True, vmem_limit_bytes=60 * 1024 * 1024
+        ),
+    )(x, w_gate, w_up, w_down)
+
+
 def pick_rows(source, row_index, live_slot):
     taken_rows = jnp.take(source, row_index, axis=0)
     return jnp.where(live_slot[:, None], taken_rows, jnp.zeros((), source.dtype))
@@ -306,8 +431,7 @@
     arrived = exchange(
         outgoing.reshape(groups, -1, outgoing.shape[-1]), "req", groups, False, 1
     ).reshape(outgoing.shape)
-    rows_full = exp_gather(arrived, lax.axis_size("exp"), 3)
-    partial_value = expert_ffn(rows_full, w_gate[0], w_up[0], w_down[0])
+    partial_value = gather_ffn(arrived, w_gate, w_up, w_down, lax.axis_size("exp"), 3)
     partial_value, page_pool = lax.optimization_barrier((partial_value, page_pool))
     summed_value = lax.psum_scatter(partial_value, "exp", scatter_dimension=1, tiled=True)
     page_rows = jnp.take(page_pool, page_table.reshape(-1), axis=0).reshape(

time: 209 us -> 197 us (0.943)
  Pallas kernels: 83.2 us -> 70.7 us
    pallas_call x2 -> x1, Pallas kernels: 48.3 us -> 35.6 us  [gather_ffn(): pl.pallas_call(functools.partial(gather_ffn_kernel, n), out_shape=jax.Sha...]
  transfers between devices with their start and end apart: 5 -> 5, of which waited for: 5 -> 5; matrix products, arithmetic and copies ran while one was open for 19% -> 21% of each run, Pallas kernels for 0% -> 0%
where the time goes in v8:
time: 197 us; the launch traced here: 196 us
  Pallas kernels  70.7 us (36%)
  waiting for transfers between devices  36.2 us (18%)
  local copies, waits for them, and re-layouts  33.6 us (17%)
  starting transfers between devices  19.6 us (10%)
  other arithmetic  17.6 us (9%)
  between operations  14.6 us (7%)
  matrix products  3.62 us (2%)
    pallas_call x1, Pallas kernels, gather_ffn(): pl.pallas_call(functools.partial(gather_ffn_kernel, n), out_shape=jax.Sha...  35.6 us
    pallas_call x3, Pallas kernels, exchange(): pl.pallas_call(functools.partial(exchange_kernel, axis, n, gather), out_s...  35.2 us
    all_to_all x1, waiting for transfers between devices, body(): lax.all_to_all(pick_rows(attention_out, send_index, send_live), 'req', sp...  16.4 us
    all_to_all x1, waiting for transfers between devices, body(): lax.all_to_all(pick_rows(page_rows, send_index, send_live), 'req', split_...  10.1 us
    scatter x1, local copies, waits for them, and re-layouts, body(): jnp.zeros((rows_all,), jnp.int32).at[came_from]  8.04 us
    all_to_all x1, starting transfers between devices, body(): lax.all_to_all(pick_rows(residual, send_index, send_live), 'req', split_a...  7.12 us
    all_to_all x1, starting transfers between devices, body(): lax.all_to_all(pick_rows(attention_out, send_index, send_live), 'req', sp...  6.97 us
    gather x5, local copies, waits for them, and re-layouts, pick_rows(): taken_rows = jnp.take(source, row_index, axis=0)  5.54 us
  transfers between devices with their start and end apart: 5, of which 5 were waited for; matrix products, arithmetic and copies ran while one was open for 21% of the time, Pallas kernels for 0%

profile of v8, /device:TPU:0, one launch (start us, length us, event | category | flops | bytes accessed | tf_op | source)
XLA Modules:
  0.0 196.0 jit_solution(6864768671624498674)
XLA Ops:
  7.2 0.7 all-gather.2.cloned.1.call-update
  7.9 0.7 compare_select_fusion.1
  8.6 8.0 %scatter_custom_fusion = s32[2048]{0:T(1024)S(1)} fusion(s32[2048]{0:T(1024)S(1)} %compare_select_fusion.1, s32[2048]{0:T(1024)S(1)} %iota.72, s32[]{:T(128)} %constant.181.clone.1), kind=kCustom, calls=%fused_computation.87 | custom fusion | bytes 8196 | tf_op jit(solution)/shard_map/scatter | solution.py:349
  16.8 2.8 %select_reduce_fusion = s32[16,128]{0,1:T(8,128)S(1)} fusion(s32[16,128]{0,1:T(8,128)S(1)} %copy.115), kind=kOutput, calls=%fused_computation.20 | output fusion | flops 4388864 | bytes 16384 | tf_op jit(solution)/shard_map/jit(cumsum)/reduce_window_sum | solution.py:355
  20.6 1.6 gather_fusion.1
  22.4 0.8 select_select_fusion.4
  23.1 7.1 %all-to-all-start = ((bf16[16,4,512]{2,1,0:T(4,128)(2,1)}), bf16[16,4,512]{2,1,0:T(4,128)(2,1)S(1)}, u32[]{:S(2)}, u32[]{:S(2)}) async-start(bf16[16,4,512]{2,1,0:T(4,128)(2,1)} %select_select_fusion.4), calls=%async_computation | async-start | bytes 131072 | tf_op jit(solution)/shard_map/all_to_all | solution.py:375
  30.4 0.8 copy.122
  31.5 0.9 gather_fusion.6
  32.6 1.0 all_to_all.24
  33.6 0.8 compare_select_fusion.15
  34.3 1.1 gather_fusion
  35.5 0.6 reduce-window.6
  36.9 0.8 compare_and_fusion.5
  38.0 7.0 %all-to-all-start.1 = ((bf16[16,4,4096]{2,1,0:T(4,128)(2,1)}), bf16[16,4,4096]{2,1,0:T(4,128)(2,1)S(1)}, u32[]{:S(2)}, u32[]{:S(2)}) async-start(bf16[16,4,4096]{2,1,0:T(4,128)(2,1)} %all_to_all.24), calls=%async_computation.1 | async-start | bytes 1048576 | tf_op jit(solution)/shard_map/all_to_all | solution.py:368
  45.1 0.4 and_reduce_fusion
  45.5 0.8 gather_fusion.2
  46.3 16.4 %all-to-all-done.1 = bf16[16,4,4096]{2,1,0:T(4,128)(2,1)S(1)} async-done(((bf16[16,4,4096]{2,1,0:T(4,128)(2,1)}), bf16[16,4,4096]{2,1,0:T(4,128)(2,1)S(1)}, u32[]{:S(2)}, u32[]{:S(2)}) %all-to-all-start.1) | async-done | bytes 524320 | tf_op jit(solution)/shard_map/all_to_all | solution.py:368
  62.9 1.4 pad_maximum_fusion
  64.2 2.2 %gather_fusion.7 = bf16[128,4096]{1,0:T(8,128)(2,1)} fusion(bf16[192,4096]{1,0:T(8,128)(2,1)S(1)} %pad_maximum_fusion, s32[1024]{0:T(1024)S(1)} %pad_clamp_fusion.4), kind=kCustom, calls=%fused_computation.1.clone | custom fusion | bytes 2097664 | tf_op jit(solution)/shard_map/jit(_take)/gather | solution.py:391
  66.4 3.4 %all-gather.2.cloned.1.call-done = bf16[4096,512]{1,0:T(8,128)(2,1)} async-done(((bf16[256,512]{1,0:T(8,128)(2,1)}), bf16[4096,512]{1,0:T(8,128)(2,1)}) %all-gather.2.cloned.1.call-update) | async-done | bytes 4194320 | tf_op jit(solution)/shard_map/all_gather | solution.py:395
  69.8 3.4 %multiply_reduce_fusion = (f32[128]{0:T(128)S(1)}, f32[128,512]{1,0:T(8,128)S(1)}) fusion(bf16[4096,512]{1,0:T(8,128)(2,1)} %all-gather.2.cloned.1.call-done, bf16[128,4096]{1,0:T(8,128)(2,1)} %gather_fusion.7, pred[128]{0:T(512)(128)(4,1)S(1)} %get-tuple-element.8, bf16[128,512]{1,0:T(8,128)(2,1)S(1)} %gather_fusion.2), kind=kOutput, calls=%fused_computation.41 | convolution fusion | flops 537722752 | bytes 5636736 | tf_op jit(solution)/shard_map/dot_general | solution.py:393
  73.5 0.7 select_maximum_fusion.x_ref
  74.2 7.7 %shard_map.140 = f32[8,16,128]{2,1,0:T(8,128)} custom-call(f32[16,128]{1,0:T(8,128)} %select_maximum_fusion.x_ref), custom_call_target="tpu_custom_call" | custom-call | tf_op jit(solution)/shard_map/pallas_call | solution.py:59
  81.8 0.9 reduce_sum.70
  82.8 2.2 %gather_fusion.3 = bf16[512,512]{1,0:T(8,128)(2,1)S(1)} fusion(bf16[128,512]{1,0:T(8,128)(2,1)S(1)} %multiply_convert_fusion, s32[1024]{0:T(1024)S(1)} %pad_clamp_fusion.2), kind=kCustom, calls=%fused_computation.7 | custom fusion | bytes 1050624 | tf_op jit(solution)/shard_map/jit(_take)/gather | solution.py:319
  85.0 1.0 select_select_fusion.3.x_ref
  86.0 14.4 %shard_map.141 = bf16[16,32,512]{2,1,0:T(8,128)(2,1)} custom-call(bf16[16,32,512]{2,1,0:T(8,128)(2,1)} %select_select_fusion.3.x_ref), custom_call_target="tpu_custom_call" | custom-call | tf_op jit(solution)/shard_map/pallas_call | solution.py:59
  100.4 35.6 %shard_map.142 = bf16[512,4096]{1,0:T(8,128)(2,1)} custom-call(bf16[512,512]{1,0:T(8,128)(2,1)} %bitcast.62, bf16[1,4096,896]{2,1,0:T(8,128)(2,1)} %wg_hbm.1, bf16[1,4096,896]{2,1,0:T(8,128)(2,1)} %wu_hbm.1, bf16[1,896,4096]{2,1,0:T(8,128)(2,1)} %wd_hbm.1), custom_call_target="tpu_custom_call" | custom-call | tf_op jit(solution)/shard_map/pallas_call | solution.py:296
  136.8 0.4 broadcast_in_dim.231
  137.2 1.1 copy.132
  138.6 0.7 broadcast_in_dim.233
  139.3 1.1 copy.133
  140.6 0.8 gather_fusion.5
  141.4 0.5 gather.47
  141.9 1.5 select_select_fusion
  143.4 0.9 gather_fusion.8
  144.4 1.0 all_to_all.27
  145.5 5.4 %all-to-all-start.2 = ((bf16[16,4,4096]{2,1,0:T(4,128)(2,1)}), bf16[16,4,4096]{2,1,0:T(4,128)(2,1)S(1)}, u32[]{:S(2)}, u32[]{:S(2)}) async-start(bf16[16,4,4096]{2,1,0:T(4,128)(2,1)} %all_to_all.27), calls=%async_computation.3 | async-start | bytes 1048576 | tf_op jit(solution)/shard_map/all_to_all | solution.py:448
  150.9 10.1 %all-to-all-done.2 = bf16[16,4,4096]{2,1,0:T(4,128)(2,1)S(1)} async-done(((bf16[16,4,4096]{2,1,0:T(4,128)(2,1)}), bf16[16,4,4096]{2,1,0:T(4,128)(2,1)S(1)}, u32[]{:S(2)}, u32[]{:S(2)}) %all-to-all-start.2) | async-done | bytes 524320 | tf_op jit(solution)/shard_map/all_to_all | solution.py:448
  161.1 1.3 pad_maximum_fusion.1
  162.5 2.2 %gather_fusion.9 = bf16[128,4096]{1,0:T(8,128)(2,1)} fusion(bf16[192,4096]{1,0:T(8,128)(2,1)S(1)} %pad_maximum_fusion.1, s32[1024]{0:T(1024)S(1)} %pad_clamp_fusion.4), kind=kCustom, calls=%fused_computation.3.clone | custom fusion | bytes 2097664 | tf_op jit(solution)/shard_map/jit(_take)/gather | solution.py:451
  164.6 1.4 broadcast_select_fusion
  166.1 1.2 copy.134
  167.3 5.4 %reduce-scatter.2.cloned.1.call-done = bf16[512,512]{1,0:T(8,128)(2,1)} async-done(((bf16[512,4096]{1,0:T(8,128)(2,1)}), bf16[512,512]{1,0:T(8,128)(2,1)}) %reduce-scatter.2.cloned.1.call-update) | async-done | bytes 524304 | tf_op jit(solution)/shard_map/reduce_scatter | solution.py:436
  172.7 13.1 %shard_map.143 = bf16[16,32,512]{2,1,0:T(8,128)(2,1)} custom-call(bf16[16,32,512]{2,1,0:T(8,128)(2,1)} %bitcast.68), custom_call_target="tpu_custom_call" | custom-call | tf_op jit(solution)/shard_map/pallas_call | solution.py:59
  185.8 2.3 %gather_fusion.4 = bf16[256,512]{1,0:T(8,128)(2,1)S(1)} fusion(bf16[512,512]{1,0:T(8,128)(2,1)} %bitcast.59, s32[1024]{0:T(1024)S(1)} %pad_clamp_fusion.1), kind=kCustom, calls=%fused_computation.8 | custom fusion | bytes 525312 | tf_op jit(solution)/shard_map/jit(_take)/gather | solution.py:458
  188.3 0.8 fusion.11
  (94 shorter events, 5.4 us)
Async XLA Ops:
  7.2 133.5 %copy-start = (bf16[256,8,256]{2,1,0:T(8,128)(2,1)S(1)}, bf16[256,8,256]{2,1,0:T(8,128)(2,1)}, u32[]{:S(2)}) copy-start(bf16[256,8,256]{2,1,0:T(8,128)(2,1)} %param.22) | copy-start | bytes 3145732
  7.2 24.4 %copy-start.2 = (bf16[128,4096]{1,0:T(8,128)(2,1)S(1)}, bf16[128,4096]{1,0:T(8,128)(2,1)}, u32[]{:S(2)}) copy-start(bf16[128,4096]{1,0:T(8,128)(2,1)} %param.17) | copy-start | bytes 3145732
  7.2 62.6 %all-gather.2.cloned.1.call-start = ((), (), s32[]{:S(2)}) async-start(), calls=%async_computation.4 | async-start | bytes 4456448 | tf_op jit(solution)/shard_map/all_gather | solution.py:395
  23.1 14.9 %all-to-all-start = ((bf16[16,4,512]{2,1,0:T(4,128)(2,1)}), bf16[16,4,512]{2,1,0:T(4,128)(2,1)S(1)}, u32[]{:S(2)}, u32[]{:S(2)}) async-start(bf16[16,4,512]{2,1,0:T(4,128)(2,1)} %select_select_fusion.4), calls=%async_computation | async-start | bytes 131072 | tf_op jit(solution)/shard_map/all_to_all | solution.py:375
  32.4 13.0 %copy-start.3 = (bf16[128,512]{1,0:T(8,128)(2,1)S(1)}, bf16[128,512]{1,0:T(8,128)(2,1)}, u32[]{:S(2)}) copy-start(bf16[128,512]{1,0:T(8,128)(2,1)} %param.18) | copy-start | bytes 393220
  38.0 24.7 %all-to-all-start.1 = ((bf16[16,4,4096]{2,1,0:T(4,128)(2,1)}), bf16[16,4,4096]{2,1,0:T(4,128)(2,1)S(1)}, u32[]{:S(2)}, u32[]{:S(2)}) async-start(bf16[16,4,4096]{2,1,0:T(4,128)(2,1)} %all_to_all.24), calls=%async_computation.1 | async-start | bytes 1048576 | tf_op jit(solution)/shard_map/all_to_all | solution.py:368
  45.0 127.7 %reduce-scatter.2.cloned.1.call-start = ((), (), s32[]{:S(2)}) async-start(), calls=%async_computation.5 | async-start | bytes 4718592 | tf_op jit(solution)/shard_map/reduce_scatter | solution.py:436
  66.4 6.8 %copy-start.4 = (f32[512,8]{0,1:T(8,128)S(1)}, f32[512,8]{0,1:T(8,128)}, u32[]{:S(2)}) copy-start(f32[512,8]{0,1:T(8,128)} %param.20) | copy-start | bytes 49156
  66.4 6.8 %copy-start.6 = (f32[512]{0:T(512)S(1)}, f32[512]{0:T(512)}, u32[]{:S(2)}) copy-start(f32[512]{0:T(512)} %param.21) | copy-start | bytes 6148
  135.9 0.7 copy-start.8
  135.9 2.4 %copy-start.7 = (s32[128,2]{0,1:T(2,128)S(1)}, s32[128,2]{0,1:T(2,128)}, u32[]{:S(2)}) copy-start(s32[128,2]{0,1:T(2,128)} %param.23) | copy-start | bytes 3076
  136.0 4.6 %copy-start.5 = (s32[128,2]{0,1:T(2,128)S(1)}, s32[128,2]{0,1:T(2,128)}, u32[]{:S(2)}) copy-start(s32[128,2]{0,1:T(2,128)} %param.26) | copy-start | bytes 3076
  143.4 2.0 %copy-start.1 = (bf16[128,4096]{1,0:T(8,128)(2,1)}, bf16[128,4096]{1,0:T(8,128)(2,1)S(1)}, u32[]{:S(2)}) copy-start(bf16[128,4096]{1,0:T(8,128)(2,1)S(1)} %select_select_fusion) | copy-start | bytes 3145732
  145.5 15.5 %all-to-all-start.2 = ((bf16[16,4,4096]{2,1,0:T(4,128)(2,1)}), bf16[16,4,4096]{2,1,0:T(4,128)(2,1)S(1)}, u32[]{:S(2)}, u32[]{:S(2)}) async-start(bf16[16,4,4096]{2,1,0:T(4,128)(2,1)} %all_to_all.27), calls=%async_computation.3 | async-start | bytes 1048576 | tf_op jit(solution)/shard_map/all_to_all | solution.py:448
Sparse Core Ops, SparseCore 0:
  10.2 59.6 all-gather.1
  136.1 36.5 reduce-scatter.1

commit v9 on v8

--- a/solution.py
+++ b/solution.py
@@ -193,6 +193,7 @@
 def gather_ffn_kernel(
     n, x_ref, wg_hbm, wu_hbm, wd_hbm, o_ref,
     y_ref, wg_v, wu_v, wd_v, g_acc, u_acc, send_sems, recv_sems, w_sems,
+    sib_out, sib_buf, acc, stage, half_buf, near_buf, rs_send, rs_recv,
 ):
     chips = n // 2
     width = x_ref.shape[1]
@@ -279,13 +280,52 @@
     g = g_acc[...]
     act = (g / (1.0 + jnp.exp(-g)) * u_acc[...]).astype(wd_v.dtype)
     weight_copies[2].wait()
-    out_cols = o_ref.shape[1]
-    chunk = out_cols // 8
-    for c in range(8):
-        span = pl.ds(c * chunk, chunk)
-        o_ref[:, span] = jnp.dot(act, wd_v[:, span], preferred_element_type=jnp.float32).astype(
-            o_ref.dtype
-        )
+
+    def down(block):
+        return jnp.dot(act, wd_v[:, cols(block)], preferred_element_type=jnp.float32).astype(
+            sib_out.dtype
+        )
+
+    def rs_remote(src, dst, slot, peer):
+        return pltpu.make_async_remote_copy(
+            src_ref=src, dst_ref=dst, send_sem=rs_send.at[slot],
+            recv_sem=rs_recv.at[slot], device_id={"exp": peer}, device_id_type=MESH,
+        )
+
+    mine = (me, up, dn, far)
+    theirs = tuple(block + 1 - 2 * core for block in mine)
+    for k in range(4):
+        sib_out[k] = down(theirs[k])
+        copy = rs_remote(sib_out.at[k], sib_buf.at[k], k, sib)
+        copy.start()
+        sends.append(copy)
+    for k in (3, 1, 2, 0):
+        own_part = down(mine[k]).astype(jnp.float32)
+        rs_remote(sib_out.at[k], sib_buf.at[k], k, sib).wait_recv()
+        acc[k] = own_part + sib_buf[k].astype(jnp.float32)
+        if k == 3:
+            stage[0] = acc[3].astype(stage.dtype)
+            for part, peer, slot in ((0, up, 4), (1, dn, 5)):
+                copy = rs_remote(stage.at[0, rows(part)], half_buf.at[part], slot, peer)
+                copy.start()
+                sends.append(copy)
+    rs_remote(stage.at[0, rows(0)], half_buf.at[0], 4, dn).wait_recv()
+    acc[1, rows(0)] = acc[1, rows(0)] + half_buf[0].astype(jnp.float32)
+    stage[1] = acc[1].astype(stage.dtype)
+    copy = rs_remote(stage.at[1], near_buf.at[0], 6, up)
+    copy.start()
+    sends.append(copy)
+    rs_remote(stage.at[0, rows(1)], half_buf.at[1], 5, up).wait_recv()
+    acc[2, rows(1)] = acc[2, rows(1)] + half_buf[1].astype(jnp.float32)
+    stage[2] = acc[2].astype(stage.dtype)
+    copy = rs_remote(stage.at[2], near_buf.at[1], 7, dn)
+    copy.start()
+    sends.append(copy)
+    rs_remote(stage.at[1], near_buf.at[0], 6, dn).wait_recv()
+    rs_remote(stage.at[2], near_buf.at[1], 7, up).wait_recv()
+    o_ref[...] = (
+        acc[0] + near_buf[0].astype(jnp.float32) + near_buf[1].astype(jnp.float32)
+    ).astype(o_ref.dtype)
     for copy in sends:
         copy.wait_send()
 
@@ -295,7 +335,7 @@
     d, ff = w_gate.shape[1], w_gate.shape[2]
     return pl.pallas_call(
         functools.partial(gather_ffn_kernel, n),
-        out_shape=jax.ShapeDtypeStruct((rows_n, w_down.shape[2]), x.dtype),
+        out_shape=jax.ShapeDtypeStruct((rows_n, w_down.shape[2] // n), x.dtype),
         in_specs=[pl.BlockSpec(memory_space=pltpu.VMEM)] + [pl.BlockSpec(memory_space=pl.ANY)] * 3,
         out_specs=pl.BlockSpec(memory_space=pltpu.VMEM),
         scratch_shapes=[
@@ -308,12 +348,19 @@
             pltpu.SemaphoreType.DMA((8,)),
             pltpu.SemaphoreType.DMA((8,)),
             pltpu.SemaphoreType.DMA((3,)),
+            pltpu.VMEM((4, rows_n, width), x.dtype),
+            pltpu.VMEM((4, rows_n, width), x.dtype),
+            pltpu.VMEM((4, rows_n, width), jnp.float32),
+            pltpu.VMEM((3, rows_n, width), x.dtype),
+            pltpu.VMEM((2, rows_n // 2, width), x.dtype),
+            pltpu.VMEM((2, rows_n, width), x.dtype),
+            pltpu.SemaphoreType.DMA((8,)),
+            pltpu.SemaphoreType.DMA((8,)),
         ],
         compiler_params=pltpu.CompilerParams(
             collective_id=collective_id, has_side_effects=True, vmem_limit_bytes=60 * 1024 * 1024
         ),
     )(x, w_gate, w_up, w_down)
-
 
 def pick_rows(source, row_index, live_slot):
     taken_rows = jnp.take(source, row_index, axis=0)
@@ -432,8 +479,8 @@
         outgoing.reshape(groups, -1, outgoing.shape[-1]), "req", groups, False, 1
     ).reshape(outgoing.shape)
     partial_value = gather_ffn(arrived, w_gate, w_up, w_down, lax.axis_size("exp"), 3)
-    partial_value, page_pool = lax.optimization_barrier((partial_value, page_pool))
-    summed_value = lax.psum_scatter(partial_value, "exp", scatter_dimension=1, tiled=True)
+    summed_value = partial_value
+    lookup = target_dev * CAP + slot_index
     page_rows = jnp.take(page_pool, page_table.reshape(-1), axis=0).reshape(
         row_req, pages_req, page_len, kv_slice
     )
@@ -445,16 +492,21 @@
     page_rows = jnp.where(kept_mask[..., None], page_rows, jnp.zeros((), page_rows.dtype)).reshape(
         row_req, -1
     )
-    moved_pages = lax.all_to_all(
-        pick_rows(page_rows, send_index, send_live), "req", split_axis=0, concat_axis=0, tiled=True
-    )
+    page_send = pick_rows(page_rows, send_index, send_live).reshape(groups, summed_value.shape[0] // groups, -1)
+    both = exchange(
+        jnp.concatenate(
+            [summed_value.reshape(groups, -1, summed_value.shape[-1]), page_send], axis=2
+        ),
+        "req",
+        groups,
+        False,
+        2,
+    )
+    returned = both[:, :, :summed_value.shape[-1]].reshape(summed_value.shape)
+    moved_pages = both[:, :, summed_value.shape[-1]:].reshape(groups * MIG_PAIR, -1)
     new_pages = jnp.take(
         jnp.concatenate([page_rows, moved_pages], axis=0), arrival, axis=0
     ).reshape(row_req, pages_req, page_len, kv_slice)
-    lookup = target_dev * CAP + slot_index
-    returned = exchange(
-        summed_value.reshape(groups, -1, summed_value.shape[-1]), "req", groups, False, 2
-    ).reshape(summed_value.shape)
     taken_rows = jnp.take(returned, lookup, axis=0).reshape(row_req, 2, -1).astype(jnp.float32)
     expert_part = gate_first[:, None] * taken_rows[:, 0] + gate_second[:, None] * taken_rows[:, 1]
     mixed = hidden + expert_part

time: 197 us -> 202 us (1.025)
  Pallas kernels: 70.7 us -> 96.1 us
  waiting for transfers between devices: 36.2 us -> 13.8 us
  starting transfers between devices: 19.6 us -> 14.4 us
  other arithmetic: 17.6 us -> 22.7 us
  local copies, waits for them, and re-layouts: 33.6 us -> 35.8 us
    pallas_call x1, Pallas kernels: 35.6 us -> 54.9 us  [gather_ffn(): pl.pallas_call(functools.partial(gather_ffn_kernel, n), out_shape=jax.Sha...]
    all_to_all x1 -> x0, waiting for transfers between devices: 10.1 us -> none  [body(): lax.all_to_all(pick_rows(page_rows, send_index, send_live), 'req', split_...]
    pallas_call x3, Pallas kernels: 35.2 us -> 41.1 us  [exchange(): pl.pallas_call(functools.partial(exchange_kernel, axis, n, gather), out_s...]
    all_to_all x1 -> x0, starting transfers between devices: 5.39 us -> none  [body(): lax.all_to_all(pick_rows(page_rows, send_index, send_live), 'req', split_...]
    reduce_scatter x1 -> x0, waiting for transfers between devices: 5.37 us -> none  [body(): lax.psum_scatter(partial_value, 'exp', scatter_dimension=1, tiled=True)]
    all_gather x1, waiting for transfers between devices: 3.42 us -> 0.01 us  [body(): lax.all_gather(w_out, 'req', axis=0, tiled=True)]
    all_to_all x1, waiting for transfers between devices: 16.4 us -> 13.1 us  [body(): lax.all_to_all(pick_rows(attention_out, send_index, send_live), 'req', sp...]
    concatenate x0 -> x1, other arithmetic: none -> 2.15 us  [body(): jnp.concatenate([summed_value.reshape(groups, -1, summed_value.shape[-1])...]
  transfers between devices with their start and end apart: 5 -> 3, of which waited for: 5 -> 1; matrix products, arithmetic and copies ran while one was open for 21% -> 19% of each run, Pallas kernels for 0% -> 0%
where the time goes in v9:
time: 202 us; the launch traced here: 201 us
  Pallas kernels  96.1 us (48%)
  local copies, waits for them, and re-layouts  35.8 us (18%)
  other arithmetic  22.7 us (11%)
  between operations  14.5 us (7%)
  starting transfers between devices  14.4 us (7%)
  waiting for transfers between devices  13.8 us (7%)
  matrix products  3.64 us (2%)
    pallas_call x1, Pallas kernels, gather_ffn(): pl.pallas_call(functools.partial(gather_ffn_kernel, n), out_shape=jax.Sha...  54.9 us
    pallas_call x3, Pallas kernels, exchange(): pl.pallas_call(functools.partial(exchange_kernel, axis, n, gather), out_s...  41.1 us
    all_to_all x1, waiting for transfers between devices, body(): lax.all_to_all(pick_rows(attention_out, send_index, send_live), 'req', sp...  13.1 us
    scatter x1, local copies, waits for them, and re-layouts, body(): jnp.zeros((rows_all,), jnp.int32).at[came_from]  8.04 us
    all_to_all x1, starting transfers between devices, body(): lax.all_to_all(pick_rows(attention_out, send_index, send_live), 'req', sp...  7.23 us
    all_to_all x1, starting transfers between devices, body(): lax.all_to_all(pick_rows(residual, send_index, send_live), 'req', split_a...  7.12 us
    gather x5, local copies, waits for them, and re-layouts, pick_rows(): taken_rows = jnp.take(source, row_index, axis=0)  6.97 us
    unnamed x29, local copies, waits for them, and re-layouts  4.24 us
  transfers between devices with their start and end apart: 3, of which 1 were waited for; matrix products, arithmetic and copies ran while one was open for 19% of the time, Pallas kernels for 0%

profile of v9, /device:TPU:0, one launch (start us, length us, event | category | flops | bytes accessed | tf_op | source)
XLA Modules:
  0.0 200.9 jit_solution(5612718162084448177)
XLA Ops:
  7.2 0.7 all-gather.2.cloned.1.call-update
  7.9 0.7 compare_select_fusion.1
  8.7 8.0 %scatter_custom_fusion = s32[2048]{0:T(1024)S(1)} fusion(s32[2048]{0:T(1024)S(1)} %compare_select_fusion.1, s32[2048]{0:T(1024)S(1)} %iota.72, s32[]{:T(128)} %constant.181.clone.1), kind=kCustom, calls=%fused_computation.88 | custom fusion | bytes 8196 | tf_op jit(solution)/shard_map/scatter | solution.py:396
  16.8 2.8 %select_reduce_fusion = s32[16,128]{0,1:T(8,128)S(1)} fusion(s32[16,128]{0,1:T(8,128)S(1)} %copy.115), kind=kOutput, calls=%fused_computation.21 | output fusion | flops 4388864 | bytes 16384 | tf_op jit(solution)/shard_map/jit(cumsum)/reduce_window_sum | solution.py:402
  20.6 1.6 gather_fusion.1
  22.4 0.8 select_select_fusion.4
  23.1 7.1 %all-to-all-start = ((bf16[16,4,512]{2,1,0:T(4,128)(2,1)}), bf16[16,4,512]{2,1,0:T(4,128)(2,1)S(1)}, u32[]{:S(2)}, u32[]{:S(2)}) async-start(bf16[16,4,512]{2,1,0:T(4,128)(2,1)} %select_select_fusion.4), calls=%async_computation | async-start | bytes 131072 | tf_op jit(solution)/shard_map/all_to_all | solution.py:422
  30.5 0.8 copy.122
  31.7 0.8 copy.129
  32.6 0.8 gather_fusion.4
  33.4 0.5 gather.45
  34.2 0.4 broadcast_in_dim.230
  34.7 1.1 copy.132
  36.7 1.3 select_select_fusion
  38.0 1.7 gather_fusion.8
  39.7 1.7 gather_fusion.6
  41.4 1.4 select_select_fusion.1
  42.8 1.0 all_to_all.16
  43.8 0.8 compare_select_fusion.15
  44.6 1.1 gather_fusion
  45.7 0.6 reduce-window.6
  47.4 1.4 compare_and_fusion.5
  48.8 0.5 compare_and_fusion.3
  49.4 7.2 %all-to-all-start.1 = ((bf16[16,4,4096]{2,1,0:T(4,128)(2,1)}), bf16[16,4,4096]{2,1,0:T(4,128)(2,1)S(1)}, u32[]{:S(2)}, u32[]{:S(2)}) async-start(bf16[16,4,4096]{2,1,0:T(4,128)(2,1)} %all_to_all.16), calls=%async_computation.1 | async-start | bytes 1048576 | tf_op jit(solution)/shard_map/all_to_all | solution.py:415
  56.6 0.6 pad_clamp_fusion
  57.9 0.8 gather_fusion.2
  58.7 13.1 %all-to-all-done.1 = bf16[16,4,4096]{2,1,0:T(4,128)(2,1)S(1)} async-done(((bf16[16,4,4096]{2,1,0:T(4,128)(2,1)}), bf16[16,4,4096]{2,1,0:T(4,128)(2,1)S(1)}, u32[]{:S(2)}, u32[]{:S(2)}) %all-to-all-start.1) | async-done | bytes 524320 | tf_op jit(solution)/shard_map/all_to_all | solution.py:415
  71.8 0.9 all_to_all.18
  72.7 1.5 pad_maximum_fusion
  74.2 2.2 %gather_fusion.7 = bf16[128,4096]{1,0:T(8,128)(2,1)} fusion(bf16[192,4096]{1,0:T(8,128)(2,1)S(1)} %pad_maximum_fusion, s32[1024]{0:T(1024)S(1)} %pad_clamp_fusion.4), kind=kCustom, calls=%fused_computation.1.clone | custom fusion | bytes 2097664 | tf_op jit(solution)/shard_map/jit(_take)/gather | solution.py:438
  76.4 3.4 %multiply_reduce_fusion = (f32[128]{0:T(128)S(1)}, f32[128,512]{1,0:T(8,128)S(1)}) fusion(bf16[4096,512]{1,0:T(8,128)(2,1)} %all-gather.2.cloned.1.call-done, bf16[128,4096]{1,0:T(8,128)(2,1)} %gather_fusion.7, pred[128]{0:T(512)(128)(4,1)} %get-tuple-element.4, bf16[128,512]{1,0:T(8,128)(2,1)S(1)} %gather_fusion.2), kind=kOutput, calls=%fused_computation.42 | convolution fusion | flops 537722752 | bytes 5636736 | tf_op jit(solution)/shard_map/dot_general | solution.py:440
  80.1 0.7 select_maximum_fusion.x_ref
  80.7 7.7 %shard_map.140 = f32[8,16,128]{2,1,0:T(8,128)} custom-call(f32[16,128]{1,0:T(8,128)} %select_maximum_fusion.x_ref), custom_call_target="tpu_custom_call" | custom-call | tf_op jit(solution)/shard_map/pallas_call | solution.py:59
  88.4 0.9 reduce_sum.70
  89.4 2.0 gather_fusion.3
  91.4 1.0 select_select_fusion.3.x_ref
  92.4 12.4 %shard_map.141 = bf16[16,32,512]{2,1,0:T(8,128)(2,1)} custom-call(bf16[16,32,512]{2,1,0:T(8,128)(2,1)} %select_select_fusion.3.x_ref), custom_call_target="tpu_custom_call" | custom-call | tf_op jit(solution)/shard_map/pallas_call | solution.py:59
  104.8 54.9 %shard_map.142 = bf16[512,512]{1,0:T(8,128)(2,1)} custom-call(bf16[512,512]{1,0:T(8,128)(2,1)} %bitcast.62, bf16[1,4096,896]{2,1,0:T(8,128)(2,1)} %wg_hbm.1, bf16[1,4096,896]{2,1,0:T(8,128)(2,1)} %wu_hbm.1, bf16[1,896,4096]{2,1,0:T(8,128)(2,1)} %wd_hbm.1), custom_call_target="tpu_custom_call" | custom-call | tf_op jit(solution)/shard_map/pallas_call | solution.py:336
  159.7 2.1 %pad_maximum_fusion.2.x_ref = bf16[16,32,1024]{2,1,0:T(8,128)(2,1)} fusion(bf16[16,32,512]{2,1,0:T(8,128)(2,1)S(1)} %reshape.542, bf16[16,32,512]{2,1,0:T(8,128)(2,1)} %bitcast.63), kind=kLoop, calls=%fused_computation.18 | loop fusion | flops 2097152 | bytes 2097152 | tf_op jit(solution)/shard_map/concatenate | solution.py:497
  161.9 21.0 %shard_map.143 = bf16[16,32,1024]{2,1,0:T(8,128)(2,1)} custom-call(bf16[16,32,1024]{2,1,0:T(8,128)(2,1)} %pad_maximum_fusion.2.x_ref), custom_call_target="tpu_custom_call" | custom-call | tf_op jit(solution)/shard_map/pallas_call | solution.py:59
  182.9 1.3 fusion.38
  184.2 1.0 reshape.545
  185.3 1.5 pad_maximum_fusion.1
  186.8 2.3 %gather_fusion.9 = bf16[128,4096]{1,0:T(8,128)(2,1)} fusion(bf16[192,4096]{1,0:T(8,128)(2,1)S(1)} %pad_maximum_fusion.1, s32[1024]{0:T(1024)} %copy-done.7), kind=kCustom, calls=%fused_computation.3.clone | custom fusion | bytes 2097664 | tf_op jit(solution)/shard_map/jit(_take)/gather | solution.py:507
  189.1 1.4 broadcast_select_fusion
  190.4 1.2 copy.134
  191.7 1.3 gather_fusion.5
  193.3 0.8 fusion.11
  (96 shorter events, 5.6 us)
Async XLA Ops:
  7.2 25.5 %copy-start = (bf16[256,8,256]{2,1,0:T(8,128)(2,1)S(1)}, bf16[256,8,256]{2,1,0:T(8,128)(2,1)}, u32[]{:S(2)}) copy-start(bf16[256,8,256]{2,1,0:T(8,128)(2,1)} %param.22) | copy-start | bytes 3145732
  7.2 26.8 %copy-start.11 = (s32[128]{0:T(128)S(1)}, s32[128]{0:T(128)}, u32[]{:S(2)}) copy-start(s32[128]{0:T(128)} %param.24) | copy-start | bytes 1540
  7.2 69.2 %all-gather.2.cloned.1.call-start = ((), (), s32[]{:S(2)}) async-start(), calls=%async_computation.2 | async-start | bytes 4456448 | tf_op jit(solution)/shard_map/all_gather | solution.py:442
  23.1 26.2 %all-to-all-start = ((bf16[16,4,512]{2,1,0:T(4,128)(2,1)}), bf16[16,4,512]{2,1,0:T(4,128)(2,1)S(1)}, u32[]{:S(2)}, u32[]{:S(2)}) async-start(bf16[16,4,512]{2,1,0:T(4,128)(2,1)} %select_select_fusion.4), calls=%async_computation | async-start | bytes 131072 | tf_op jit(solution)/shard_map/all_to_all | solution.py:422
  30.4 5.3 %copy-start.10 = (s32[128,2]{0,1:T(2,128)S(1)}, s32[128,2]{0,1:T(2,128)}, u32[]{:S(2)}) copy-start(s32[128,2]{0,1:T(2,128)} %param.23) | copy-start | bytes 3076
  38.0 3.4 %copy-start.1 = (bf16[128,4096]{1,0:T(8,128)(2,1)}, bf16[128,4096]{1,0:T(8,128)(2,1)S(1)}, u32[]{:S(2)}) copy-start(bf16[128,4096]{1,0:T(8,128)(2,1)S(1)} %select_select_fusion) | copy-start | bytes 3145732
  38.0 1.7 copy-start.2
  41.3 7.4 %copy-start.5 = (s32[128,2]{0,1:T(2,128)S(1)}, s32[128,2]{0,1:T(2,128)}, u32[]{:S(2)}) copy-start(s32[128,2]{0,1:T(2,128)} %param.26) | copy-start | bytes 3076
  41.3 16.5 %copy-start.3 = (bf16[128,512]{1,0:T(8,128)(2,1)S(1)}, bf16[128,512]{1,0:T(8,128)(2,1)}, u32[]{:S(2)}) copy-start(bf16[128,512]{1,0:T(8,128)(2,1)} %param.18) | copy-start | bytes 393220
  48.8 25.5 %copy-start.7 = (s32[1024]{0:T(1024)}, s32[1024]{0:T(1024)S(1)}, u32[]{:S(2)}) copy-start(s32[1024]{0:T(1024)S(1)} %pad_clamp_fusion.4) | copy-start | bytes 12292
  49.4 22.5 %all-to-all-start.1 = ((bf16[16,4,4096]{2,1,0:T(4,128)(2,1)}), bf16[16,4,4096]{2,1,0:T(4,128)(2,1)S(1)}, u32[]{:S(2)}, u32[]{:S(2)}) async-start(bf16[16,4,4096]{2,1,0:T(4,128)(2,1)} %all_to_all.16), calls=%async_computation.1 | async-start | bytes 1048576 | tf_op jit(solution)/shard_map/all_to_all | solution.py:415
  76.4 3.4 %copy-start.4 = (f32[512,8]{0,1:T(8,128)S(1)}, f32[512,8]{0,1:T(8,128)}, u32[]{:S(2)}) copy-start(f32[512,8]{0,1:T(8,128)} %param.20) | copy-start | bytes 49156
  76.4 3.4 %copy-start.6 = (f32[512]{0:T(512)S(1)}, f32[512]{0:T(512)}, u32[]{:S(2)}) copy-start(f32[512]{0:T(512)} %param.21) | copy-start | bytes 6148
  186.8 2.3 %copy-start.8 = (pred[128]{0:T(512)(128)(4,1)S(1)}, pred[128]{0:T(512)(128)(4,1)}, u32[]{:S(2)}) copy-start(pred[128]{0:T(512)(128)(4,1)} %get-tuple-element.4) | copy-start | bytes 388
  189.1 4.1 %copy-start.9 = (pred[128,2]{0,1:T(4,128)(4,1)S(1)}, pred[128,2]{0,1:T(4,128)(4,1)}, u32[]{:S(2)}) copy-start(pred[128,2]{0,1:T(4,128)(4,1)} %compare_and_fusion.3) | copy-start | bytes 772
Sparse Core Ops, SparseCore 0:
  10.2 59.2 all-gather.1

commit v10 on v9

--- a/solution.py
+++ b/solution.py
@@ -360,6 +360,11 @@
         compiler_params=pltpu.CompilerParams(
             collective_id=collective_id, has_side_effects=True, vmem_limit_bytes=60 * 1024 * 1024
         ),
+        cost_estimate=pl.CostEstimate(
+            flops=2 * rows_n * d * ff * 3,
+            transcendentals=rows_n * ff,
+            bytes_accessed=2 * (3 * d * ff + 2 * rows_n * d),
+        ),
     )(x, w_gate, w_up, w_down)
 
 def pick_rows(source, row_index, live_slot):
@@ -478,35 +483,30 @@
     arrived = exchange(
         outgoing.reshape(groups, -1, outgoing.shape[-1]), "req", groups, False, 1
     ).reshape(outgoing.shape)
+    page_rows = jnp.take(page_pool, page_table.reshape(-1), axis=0).reshape(
+        row_req, pages_req, page_len, kv_slice
+    )
+    position = (
+        jnp.arange(pages_req, dtype=jnp.int32)[:, None] * page_len
+        + jnp.arange(page_len, dtype=jnp.int32)[None, :]
+    )
+    kept_mask = position[None, :, :] < cache_len[:, None, None]
+    page_rows = jnp.where(kept_mask[..., None], page_rows, jnp.zeros((), page_rows.dtype)).reshape(
+        row_req, -1
+    )
+    page_send, arrived = lax.optimization_barrier(
+        (pick_rows(page_rows, send_index, send_live), arrived)
+    )
+    moved_pages = lax.all_to_all(page_send, "req", split_axis=0, concat_axis=0, tiled=True)
     partial_value = gather_ffn(arrived, w_gate, w_up, w_down, lax.axis_size("exp"), 3)
     summed_value = partial_value
     lookup = target_dev * CAP + slot_index
-    page_rows = jnp.take(page_pool, page_table.reshape(-1), axis=0).reshape(
-        row_req, pages_req, page_len, kv_slice
-    )
-    position = (
-        jnp.arange(pages_req, dtype=jnp.int32)[:, None] * page_len
-        + jnp.arange(page_len, dtype=jnp.int32)[None, :]
-    )
-    kept_mask = position[None, :, :] < cache_len[:, None, None]
-    page_rows = jnp.where(kept_mask[..., None], page_rows, jnp.zeros((), page_rows.dtype)).reshape(
-        row_req, -1
-    )
-    page_send = pick_rows(page_rows, send_index, send_live).reshape(groups, summed_value.shape[0] // groups, -1)
-    both = exchange(
-        jnp.concatenate(
-            [summed_value.reshape(groups, -1, summed_value.shape[-1]), page_send], axis=2
-        ),
-        "req",
-        groups,
-        False,
-        2,
-    )
-    returned = both[:, :, :summed_value.shape[-1]].reshape(summed_value.shape)
-    moved_pages = both[:, :, summed_value.shape[-1]:].reshape(groups * MIG_PAIR, -1)
     new_pages = jnp.take(
         jnp.concatenate([page_rows, moved_pages], axis=0), arrival, axis=0
     ).reshape(row_req, pages_req, page_len, kv_slice)
+    returned = exchange(
+        summed_value.reshape(groups, -1, summed_value.shape[-1]), "req", groups, False, 2
+    ).reshape(summed_value.shape)
     taken_rows = jnp.take(returned, lookup, axis=0).reshape(row_req, 2, -1).astype(jnp.float32)
     expert_part = gate_first[:, None] * taken_rows[:, 0] + gate_second[:, None] * taken_rows[:, 1]
     mixed = hidden + expert_part

time: 202 us -> 199 us (0.985)
  Pallas kernels: 96.1 us -> 90.4 us
  starting transfers between devices: 14.4 us -> 19.7 us
  other arithmetic: 22.7 us -> 18.7 us
    pallas_call x3, Pallas kernels: 41.1 us -> 35.7 us  [exchange(): pl.pallas_call(functools.partial(exchange_kernel, axis, n, gather), out_s...]
    all_to_all x0 -> x1, starting transfers between devices: none -> 5.35 us  [body(): lax.all_to_all(page_send, 'req', split_axis=0, concat_axis=0, tiled=True)]
    concatenate x1 -> x0, other arithmetic: 2.15 us -> none  [body(): jnp.concatenate([summed_value.reshape(groups, -1, summed_value.shape[-1])...]
    unnamed x29 -> x23, local copies, waits for them, and re-layouts: 4.24 us -> 4.23 us
  transfers between devices with their start and end apart: 3 -> 4, of which waited for: 1 -> 1; matrix products, arithmetic and copies ran while one was open for 19% -> 20% of each run, Pallas kernels for 0% -> 36%
where the time goes in v10:
time: 199 us; the launch traced here: 198 us
  Pallas kernels  90.4 us (45%)
  local copies, waits for them, and re-layouts  35.3 us (18%)
  starting transfers between devices  19.7 us (10%)
  other arithmetic  18.7 us (9%)
  waiting for transfers between devices  15.7 us (8%)
  between operations  14.6 us (7%)
  matrix products  3.64 us (2%)
    pallas_call x1, Pallas kernels, gather_ffn(): pl.pallas_call(functools.partial(gather_ffn_kernel, n), out_shape=jax.Sha...  54.8 us
    pallas_call x3, Pallas kernels, exchange(): pl.pallas_call(functools.partial(exchange_kernel, axis, n, gather), out_s...  35.7 us
    all_to_all x1, waiting for transfers between devices, body(): lax.all_to_all(pick_rows(attention_out, send_index, send_live), 'req', sp...  15 us
    scatter x1, local copies, waits for them, and re-layouts, body(): jnp.zeros((rows_all,), jnp.int32).at[came_from]  8.04 us
    all_to_all x1, starting transfers between devices, body(): lax.all_to_all(pick_rows(attention_out, send_index, send_live), 'req', sp...  7.23 us
    all_to_all x1, starting transfers between devices, body(): lax.all_to_all(pick_rows(residual, send_index, send_live), 'req', split_a...  7.12 us
    gather x5, local copies, waits for them, and re-layouts, pick_rows(): taken_rows = jnp.take(source, row_index, axis=0)  6.97 us
    all_to_all x1, starting transfers between devices, body(): lax.all_to_all(page_send, 'req', split_axis=0, concat_axis=0, tiled=True)  5.35 us
  transfers between devices with their start and end apart: 4, of which 1 were waited for; matrix products, arithmetic and copies ran while one was open for 20% of the time, Pallas kernels for 36%

profile of v10, /device:TPU:0, one launch (start us, length us, event | category | flops | bytes accessed | tf_op | source)
XLA Modules:
  0.0 198.0 jit_solution(14189072436402026036)
XLA Ops:
  7.2 0.7 all-gather.2.cloned.1.call-update
  7.9 0.7 compare_select_fusion.1
  8.7 8.0 %scatter_custom_fusion = s32[2048]{0:T(1024)S(1)} fusion(s32[2048]{0:T(1024)S(1)} %compare_select_fusion.1, s32[2048]{0:T(1024)S(1)} %iota.72, s32[]{:T(128)} %constant.181.clone.1), kind=kCustom, calls=%fused_computation.87 | custom fusion | bytes 8196 | tf_op jit(solution)/shard_map/scatter | solution.py:401
  16.8 2.8 %select_reduce_fusion = s32[16,128]{0,1:T(8,128)S(1)} fusion(s32[16,128]{0,1:T(8,128)S(1)} %copy.115), kind=kOutput, calls=%fused_computation.20 | output fusion | flops 4388864 | bytes 16384 | tf_op jit(solution)/shard_map/jit(cumsum)/reduce_window_sum | solution.py:407
  20.6 1.6 gather_fusion.1
  22.4 0.8 select_select_fusion.4
  23.1 7.1 %all-to-all-start = ((bf16[16,4,512]{2,1,0:T(4,128)(2,1)}), bf16[16,4,512]{2,1,0:T(4,128)(2,1)S(1)}, u32[]{:S(2)}, u32[]{:S(2)}) async-start(bf16[16,4,512]{2,1,0:T(4,128)(2,1)} %select_select_fusion.4), calls=%async_computation | async-start | bytes 131072 | tf_op jit(solution)/shard_map/all_to_all | solution.py:427
  30.5 0.8 copy.122
  31.7 0.8 copy.129
  32.6 0.8 gather_fusion.3
  33.4 0.5 gather.43
  34.2 0.4 broadcast_in_dim.224
  34.7 1.1 copy.132
  35.9 0.4 broadcast_in_dim.226
  36.7 1.3 select_select_fusion
  38.0 1.7 gather_fusion.8
  39.7 1.7 gather_fusion.6
  41.4 1.4 select_select_fusion.1
  42.8 1.0 all_to_all.24
  43.8 0.8 compare_select_fusion.15
  44.6 1.1 gather_fusion
  45.7 0.6 reduce-window.6
  46.9 0.4 fusion.6
  47.4 0.8 compare_and_fusion.5
  48.3 7.2 %all-to-all-start.1 = ((bf16[16,4,4096]{2,1,0:T(4,128)(2,1)}), bf16[16,4,4096]{2,1,0:T(4,128)(2,1)S(1)}, u32[]{:S(2)}, u32[]{:S(2)}) async-start(bf16[16,4,4096]{2,1,0:T(4,128)(2,1)} %all_to_all.24), calls=%async_computation.1 | async-start | bytes 1048576 | tf_op jit(solution)/shard_map/all_to_all | solution.py:420
  55.5 0.4 and_reduce_fusion
  56.0 0.8 gather_fusion.2
  56.8 15.0 %all-to-all-done.1 = bf16[16,4,4096]{2,1,0:T(4,128)(2,1)S(1)} async-done(((bf16[16,4,4096]{2,1,0:T(4,128)(2,1)}), bf16[16,4,4096]{2,1,0:T(4,128)(2,1)S(1)}, u32[]{:S(2)}, u32[]{:S(2)}) %all-to-all-start.1) | async-done | bytes 524320 | tf_op jit(solution)/shard_map/all_to_all | solution.py:420
  71.8 0.9 all_to_all.26
  72.7 1.5 pad_maximum_fusion
  74.2 2.2 %gather_fusion.7 = bf16[128,4096]{1,0:T(8,128)(2,1)} fusion(bf16[192,4096]{1,0:T(8,128)(2,1)S(1)} %pad_maximum_fusion, s32[1024]{0:T(1024)S(1)} %pad_clamp_fusion.4), kind=kCustom, calls=%fused_computation.1.clone | custom fusion | bytes 2097664 | tf_op jit(solution)/shard_map/jit(_take)/gather | solution.py:443
  76.4 3.4 %multiply_reduce_fusion = (f32[128]{0:T(128)S(1)}, f32[128,512]{1,0:T(8,128)S(1)}) fusion(bf16[4096,512]{1,0:T(8,128)(2,1)} %all-gather.2.cloned.1.call-done, bf16[128,4096]{1,0:T(8,128)(2,1)} %gather_fusion.7, pred[128]{0:T(512)(128)(4,1)S(1)} %get-tuple-element.8, bf16[128,512]{1,0:T(8,128)(2,1)S(1)} %gather_fusion.2), kind=kOutput, calls=%fused_computation.41 | convolution fusion | flops 537722752 | bytes 5636736 | tf_op jit(solution)/shard_map/dot_general | solution.py:445
  80.1 0.7 select_maximum_fusion.x_ref
  80.7 7.7 %shard_map.140 = f32[8,16,128]{2,1,0:T(8,128)} custom-call(f32[16,128]{1,0:T(8,128)} %select_maximum_fusion.x_ref), custom_call_target="tpu_custom_call" | custom-call | tf_op jit(solution)/shard_map/pallas_call | solution.py:59
  88.4 0.9 reduce_sum.70
  89.4 2.0 gather_fusion.4
  91.4 1.0 select_select_fusion.3.x_ref
  92.4 12.4 %shard_map.141 = bf16[16,32,512]{2,1,0:T(8,128)(2,1)} custom-call(bf16[16,32,512]{2,1,0:T(8,128)(2,1)} %select_select_fusion.3.x_ref), custom_call_target="tpu_custom_call" | custom-call | tf_op jit(solution)/shard_map/pallas_call | solution.py:59
  104.8 1.0 all_to_all.27
  105.8 5.4 %all-to-all-start.2 = ((bf16[16,4,4096]{2,1,0:T(4,128)(2,1)}), bf16[16,4,4096]{2,1,0:T(4,128)(2,1)S(1)}, u32[]{:S(2)}, u32[]{:S(2)}) async-start(bf16[16,4,4096]{2,1,0:T(4,128)(2,1)} %all_to_all.27), calls=%async_computation.2 | async-start | bytes 1048576 | tf_op jit(solution)/shard_map/all_to_all | solution.py:500
  111.2 54.8 %shard_map.142 = bf16[512,512]{1,0:T(8,128)(2,1)} custom-call(bf16[512,512]{1,0:T(8,128)(2,1)} %bitcast.67, bf16[1,4096,896]{2,1,0:T(8,128)(2,1)} %wg_hbm.1, bf16[1,4096,896]{2,1,0:T(8,128)(2,1)} %wu_hbm.1, bf16[1,896,4096]{2,1,0:T(8,128)(2,1)} %wd_hbm.1), custom_call_target="tpu_custom_call" | custom-call | flops 11274289152 | bytes 30408704 | tf_op jit(solution)/shard_map/pallas_call | solution.py:336
  166.0 15.5 %shard_map.143 = bf16[16,32,512]{2,1,0:T(8,128)(2,1)} custom-call(bf16[16,32,512]{2,1,0:T(8,128)(2,1)} %bitcast.68), custom_call_target="tpu_custom_call" | custom-call | tf_op jit(solution)/shard_map/pallas_call | solution.py:59
  181.5 2.3 %gather_fusion.5 = bf16[256,512]{1,0:T(8,128)(2,1)S(1)} fusion(bf16[512,512]{1,0:T(8,128)(2,1)} %bitcast.59, s32[1024]{0:T(1024)S(1)} %pad_clamp_fusion), kind=kCustom, calls=%fused_computation.9 | custom fusion | bytes 525312 | tf_op jit(solution)/shard_map/jit(_take)/gather | solution.py:510
  184.1 0.8 fusion.11
  185.0 1.3 pad_maximum_fusion.1
  186.4 2.2 %gather_fusion.9 = bf16[128,4096]{1,0:T(8,128)(2,1)} fusion(bf16[192,4096]{1,0:T(8,128)(2,1)S(1)} %pad_maximum_fusion.1, s32[1024]{0:T(1024)S(1)} %pad_clamp_fusion.4), kind=kCustom, calls=%fused_computation.3.clone | custom fusion | bytes 2097664 | tf_op jit(solution)/shard_map/jit(_take)/gather | solution.py:504
  188.5 1.4 broadcast_select_fusion
  189.9 1.2 copy.134
  (90 shorter events, 4.3 us)
Async XLA Ops:
  7.2 25.5 %copy-start = (bf16[256,8,256]{2,1,0:T(8,128)(2,1)S(1)}, bf16[256,8,256]{2,1,0:T(8,128)(2,1)}, u32[]{:S(2)}) copy-start(bf16[256,8,256]{2,1,0:T(8,128)(2,1)} %param.22) | copy-start | bytes 3145732
  7.2 26.8 %copy-start.8 = (s32[128]{0:T(128)S(1)}, s32[128]{0:T(128)}, u32[]{:S(2)}) copy-start(s32[128]{0:T(128)} %param.24) | copy-start | bytes 1540
  7.2 69.2 %all-gather.2.cloned.1.call-start = ((), (), s32[]{:S(2)}) async-start(), calls=%async_computation.3 | async-start | bytes 4456448 | tf_op jit(solution)/shard_map/all_gather | solution.py:447
  23.1 25.1 %all-to-all-start = ((bf16[16,4,512]{2,1,0:T(4,128)(2,1)}), bf16[16,4,512]{2,1,0:T(4,128)(2,1)S(1)}, u32[]{:S(2)}, u32[]{:S(2)}) async-start(bf16[16,4,512]{2,1,0:T(4,128)(2,1)} %select_select_fusion.4), calls=%async_computation | async-start | bytes 131072 | tf_op jit(solution)/shard_map/all_to_all | solution.py:427
  30.4 5.3 %copy-start.7 = (s32[128,2]{0,1:T(2,128)S(1)}, s32[128,2]{0,1:T(2,128)}, u32[]{:S(2)}) copy-start(s32[128,2]{0,1:T(2,128)} %param.23) | copy-start | bytes 3076
  38.0 3.4 %copy-start.1 = (bf16[128,4096]{1,0:T(8,128)(2,1)}, bf16[128,4096]{1,0:T(8,128)(2,1)S(1)}, u32[]{:S(2)}) copy-start(bf16[128,4096]{1,0:T(8,128)(2,1)S(1)} %select_select_fusion) | copy-start | bytes 3145732
  38.0 1.7 copy-start.2
  41.3 6.8 %copy-start.5 = (s32[128,2]{0,1:T(2,128)S(1)}, s32[128,2]{0,1:T(2,128)}, u32[]{:S(2)}) copy-start(s32[128,2]{0,1:T(2,128)} %param.26) | copy-start | bytes 3076
  41.3 14.6 %copy-start.3 = (bf16[128,512]{1,0:T(8,128)(2,1)S(1)}, bf16[128,512]{1,0:T(8,128)(2,1)}, u32[]{:S(2)}) copy-start(bf16[128,512]{1,0:T(8,128)(2,1)} %param.18) | copy-start | bytes 393220
  48.3 23.5 %all-to-all-start.1 = ((bf16[16,4,4096]{2,1,0:T(4,128)(2,1)}), bf16[16,4,4096]{2,1,0:T(4,128)(2,1)S(1)}, u32[]{:S(2)}, u32[]{:S(2)}) async-start(bf16[16,4,4096]{2,1,0:T(4,128)(2,1)} %all_to_all.24), calls=%async_computation.1 | async-start | bytes 1048576 | tf_op jit(solution)/shard_map/all_to_all | solution.py:420
  76.4 3.4 %copy-start.4 = (f32[512,8]{0,1:T(8,128)S(1)}, f32[512,8]{0,1:T(8,128)}, u32[]{:S(2)}) copy-start(f32[512,8]{0,1:T(8,128)} %param.20) | copy-start | bytes 49156
  76.4 3.4 %copy-start.6 = (f32[512]{0:T(512)S(1)}, f32[512]{0:T(512)}, u32[]{:S(2)}) copy-start(f32[512]{0:T(512)} %param.21) | copy-start | bytes 6148
  105.8 79.1 %all-to-all-start.2 = ((bf16[16,4,4096]{2,1,0:T(4,128)(2,1)}), bf16[16,4,4096]{2,1,0:T(4,128)(2,1)S(1)}, u32[]{:S(2)}, u32[]{:S(2)}) async-start(bf16[16,4,4096]{2,1,0:T(4,128)(2,1)} %all_to_all.27), calls=%async_computation.2 | async-start | bytes 1048576 | tf_op jit(solution)/shard_map/all_to_all | solution.py:500
Sparse Core Ops, SparseCore 0:
  10.2 59.2 all-gather.1

commit v11 on v10

--- a/solution.py
+++ b/solution.py
@@ -483,6 +483,7 @@
     arrived = exchange(
         outgoing.reshape(groups, -1, outgoing.shape[-1]), "req", groups, False, 1
     ).reshape(outgoing.shape)
+    page_pool, attn_new = lax.optimization_barrier((page_pool, attn_new))
     page_rows = jnp.take(page_pool, page_table.reshape(-1), axis=0).reshape(
         row_req, pages_req, page_len, kv_slice
     )

time: 199 us -> 199 us (level)
  no operation moved by 1% of the time
where the time goes in v11:
time: 199 us; the launch traced here: 198 us
  Pallas kernels  90.4 us (45%)
  local copies, waits for them, and re-layouts  35.3 us (18%)
  starting transfers between devices  19.7 us (10%)
  other arithmetic  18.7 us (9%)
  waiting for transfers between devices  15.7 us (8%)
  between operations  14.6 us (7%)
  matrix products  3.64 us (2%)
    pallas_call x1, Pallas kernels, gather_ffn(): pl.pallas_call(functools.partial(gather_ffn_kernel, n), out_shape=jax.Sha...  54.8 us
    pallas_call x3, Pallas kernels, exchange(): pl.pallas_call(functools.partial(exchange_kernel, axis, n, gather), out_s...  35.7 us
    all_to_all x1, waiting for transfers between devices, body(): lax.all_to_all(pick_rows(attention_out, send_index, send_live), 'req', sp...  15 us
    scatter x1, local copies, waits for them, and re-layouts, body(): jnp.zeros((rows_all,), jnp.int32).at[came_from]  8.04 us
    all_to_all x1, starting transfers between devices, body(): lax.all_to_all(pick_rows(attention_out, send_index, send_live), 'req', sp...  7.23 us
    all_to_all x1, starting transfers between devices, body(): lax.all_to_all(pick_rows(residual, send_index, send_live), 'req', split_a...  7.12 us
    gather x5, local copies, waits for them, and re-layouts, pick_rows(): taken_rows = jnp.take(source, row_index, axis=0)  6.97 us
    all_to_all x1, starting transfers between devices, body(): lax.all_to_all(page_send, 'req', split_axis=0, concat_axis=0, tiled=True)  5.35 us
  transfers between devices with their start and end apart: 4, of which 1 were waited for; matrix products, arithmetic and copies ran while one was open for 20% of the time, Pallas kernels for 36%

profile of v11, /device:TPU:0, one launch (start us, length us, event | category | flops | bytes accessed | tf_op | source)
XLA Modules:
  0.0 198.0 jit_solution(14189072436402026036)
XLA Ops:
  7.2 0.7 all-gather.2.cloned.1.call-update
  7.9 0.7 compare_select_fusion.1
  8.7 8.0 %scatter_custom_fusion = s32[2048]{0:T(1024)S(1)} fusion(s32[2048]{0:T(1024)S(1)} %compare_select_fusion.1, s32[2048]{0:T(1024)S(1)} %iota.72, s32[]{:T(128)} %constant.181.clone.1), kind=kCustom, calls=%fused_computation.85 | custom fusion | bytes 8196 | tf_op jit(solution)/shard_map/scatter | solution.py:401
  16.8 2.8 %select_reduce_fusion = s32[16,128]{0,1:T(8,128)S(1)} fusion(s32[16,128]{0,1:T(8,128)S(1)} %copy.115), kind=kOutput, calls=%fused_computation.19 | output fusion | flops 4388864 | bytes 16384 | tf_op jit(solution)/shard_map/jit(cumsum)/reduce_window_sum | solution.py:407
  20.6 1.6 gather_fusion.1
  22.4 0.8 select_select_fusion.4
  23.1 7.1 %all-to-all-start = ((bf16[16,4,512]{2,1,0:T(4,128)(2,1)}), bf16[16,4,512]{2,1,0:T(4,128)(2,1)S(1)}, u32[]{:S(2)}, u32[]{:S(2)}) async-start(bf16[16,4,512]{2,1,0:T(4,128)(2,1)} %select_select_fusion.4), calls=%async_computation | async-start | bytes 131072 | tf_op jit(solution)/shard_map/all_to_all | solution.py:427
  30.5 0.8 copy.122
  31.7 0.8 copy.129
  32.6 0.8 gather_fusion.3
  33.4 0.5 gather.43
  34.2 0.4 broadcast_in_dim.224
  34.7 1.1 copy.132
  35.9 0.4 broadcast_in_dim.226
  36.7 1.3 select_select_fusion
  38.0 1.7 gather_fusion.8
  39.7 1.7 gather_fusion.6
  41.4 1.4 select_select_fusion.1
  42.8 1.0 all_to_all.24
  43.8 0.8 compare_select_fusion.15
  44.6 1.1 gather_fusion
  45.7 0.6 reduce-window.6
  46.9 0.4 fusion.4
  47.4 0.8 compare_and_fusion.5
  48.3 7.2 %all-to-all-start.1 = ((bf16[16,4,4096]{2,1,0:T(4,128)(2,1)}), bf16[16,4,4096]{2,1,0:T(4,128)(2,1)S(1)}, u32[]{:S(2)}, u32[]{:S(2)}) async-start(bf16[16,4,4096]{2,1,0:T(4,128)(2,1)} %all_to_all.24), calls=%async_computation.1 | async-start | bytes 1048576 | tf_op jit(solution)/shard_map/all_to_all | solution.py:420
  55.5 0.4 and_reduce_fusion
  56.0 0.8 gather_fusion.2
  56.8 15.0 %all-to-all-done.1 = bf16[16,4,4096]{2,1,0:T(4,128)(2,1)S(1)} async-done(((bf16[16,4,4096]{2,1,0:T(4,128)(2,1)}), bf16[16,4,4096]{2,1,0:T(4,128)(2,1)S(1)}, u32[]{:S(2)}, u32[]{:S(2)}) %all-to-all-start.1) | async-done | bytes 524320 | tf_op jit(solution)/shard_map/all_to_all | solution.py:420
  71.8 0.9 all_to_all.26
  72.7 1.5 pad_maximum_fusion
  74.2 2.2 %gather_fusion.7 = bf16[128,4096]{1,0:T(8,128)(2,1)} fusion(bf16[192,4096]{1,0:T(8,128)(2,1)S(1)} %pad_maximum_fusion, s32[1024]{0:T(1024)S(1)} %pad_clamp_fusion.4), kind=kCustom, calls=%fused_computation.1.clone | custom fusion | bytes 2097664 | tf_op jit(solution)/shard_map/jit(_take)/gather | solution.py:443
  76.4 3.4 %multiply_reduce_fusion = (f32[128]{0:T(128)S(1)}, f32[128,512]{1,0:T(8,128)S(1)}) fusion(bf16[4096,512]{1,0:T(8,128)(2,1)} %all-gather.2.cloned.1.call-done, bf16[128,4096]{1,0:T(8,128)(2,1)} %gather_fusion.7, pred[128]{0:T(512)(128)(4,1)S(1)} %get-tuple-element.10, bf16[128,512]{1,0:T(8,128)(2,1)S(1)} %gather_fusion.2), kind=kOutput, calls=%fused_computation.39 | convolution fusion | flops 537722752 | bytes 5636736 | tf_op jit(solution)/shard_map/dot_general | solution.py:445
  80.1 0.7 select_maximum_fusion.x_ref
  80.7 7.7 %shard_map.140 = f32[8,16,128]{2,1,0:T(8,128)} custom-call(f32[16,128]{1,0:T(8,128)} %select_maximum_fusion.x_ref), custom_call_target="tpu_custom_call" | custom-call | tf_op jit(solution)/shard_map/pallas_call | solution.py:59
  88.4 0.9 reduce_sum.70
  89.4 2.0 gather_fusion.4
  91.4 1.0 select_select_fusion.3.x_ref
  92.4 12.4 %shard_map.141 = bf16[16,32,512]{2,1,0:T(8,128)(2,1)} custom-call(bf16[16,32,512]{2,1,0:T(8,128)(2,1)} %select_select_fusion.3.x_ref), custom_call_target="tpu_custom_call" | custom-call | tf_op jit(solution)/shard_map/pallas_call | solution.py:59
  104.8 1.0 all_to_all.27
  105.8 5.4 %all-to-all-start.2 = ((bf16[16,4,4096]{2,1,0:T(4,128)(2,1)}), bf16[16,4,4096]{2,1,0:T(4,128)(2,1)S(1)}, u32[]{:S(2)}, u32[]{:S(2)}) async-start(bf16[16,4,4096]{2,1,0:T(4,128)(2,1)} %all_to_all.27), calls=%async_computation.2 | async-start | bytes 1048576 | tf_op jit(solution)/shard_map/all_to_all | solution.py:501
  111.2 54.8 %shard_map.142 = bf16[512,512]{1,0:T(8,128)(2,1)} custom-call(bf16[512,512]{1,0:T(8,128)(2,1)} %bitcast.67, bf16[1,4096,896]{2,1,0:T(8,128)(2,1)} %wg_hbm.1, bf16[1,4096,896]{2,1,0:T(8,128)(2,1)} %wu_hbm.1, bf16[1,896,4096]{2,1,0:T(8,128)(2,1)} %wd_hbm.1), custom_call_target="tpu_custom_call" | custom-call | flops 11274289152 | bytes 30408704 | tf_op jit(solution)/shard_map/pallas_call | solution.py:336
  166.0 15.5 %shard_map.143 = bf16[16,32,512]{2,1,0:T(8,128)(2,1)} custom-call(bf16[16,32,512]{2,1,0:T(8,128)(2,1)} %bitcast.68), custom_call_target="tpu_custom_call" | custom-call | tf_op jit(solution)/shard_map/pallas_call | solution.py:59
  181.5 2.3 %gather_fusion.5 = bf16[256,512]{1,0:T(8,128)(2,1)S(1)} fusion(bf16[512,512]{1,0:T(8,128)(2,1)} %bitcast.59, s32[1024]{0:T(1024)S(1)} %pad_clamp_fusion), kind=kCustom, calls=%fused_computation.9 | custom fusion | bytes 525312 | tf_op jit(solution)/shard_map/jit(_take)/gather | solution.py:511
  184.1 0.8 fusion.8
  185.0 1.3 pad_maximum_fusion.1
  186.4 2.2 %gather_fusion.9 = bf16[128,4096]{1,0:T(8,128)(2,1)} fusion(bf16[192,4096]{1,0:T(8,128)(2,1)S(1)} %pad_maximum_fusion.1, s32[1024]{0:T(1024)S(1)} %pad_clamp_fusion.4), kind=kCustom, calls=%fused_computation.3.clone | custom fusion | bytes 2097664 | tf_op jit(solution)/shard_map/jit(_take)/gather | solution.py:505
  188.5 1.4 broadcast_select_fusion
  189.9 1.2 copy.134
  (90 shorter events, 4.3 us)
Async XLA Ops:
  7.2 25.5 %copy-start = (bf16[256,8,256]{2,1,0:T(8,128)(2,1)S(1)}, bf16[256,8,256]{2,1,0:T(8,128)(2,1)}, u32[]{:S(2)}) copy-start(bf16[256,8,256]{2,1,0:T(8,128)(2,1)} %param.22) | copy-start | bytes 3145732
  7.2 26.8 %copy-start.8 = (s32[128]{0:T(128)S(1)}, s32[128]{0:T(128)}, u32[]{:S(2)}) copy-start(s32[128]{0:T(128)} %param.24) | copy-start | bytes 1540
  7.2 69.2 %all-gather.2.cloned.1.call-start = ((), (), s32[]{:S(2)}) async-start(), calls=%async_computation.3 | async-start | bytes 4456448 | tf_op jit(solution)/shard_map/all_gather | solution.py:447
  23.1 25.1 %all-to-all-start = ((bf16[16,4,512]{2,1,0:T(4,128)(2,1)}), bf16[16,4,512]{2,1,0:T(4,128)(2,1)S(1)}, u32[]{:S(2)}, u32[]{:S(2)}) async-start(bf16[16,4,512]{2,1,0:T(4,128)(2,1)} %select_select_fusion.4), calls=%async_computation | async-start | bytes 131072 | tf_op jit(solution)/shard_map/all_to_all | solution.py:427
  30.4 5.3 %copy-start.7 = (s32[128,2]{0,1:T(2,128)S(1)}, s32[128,2]{0,1:T(2,128)}, u32[]{:S(2)}) copy-start(s32[128,2]{0,1:T(2,128)} %param.23) | copy-start | bytes 3076
  38.0 3.4 %copy-start.1 = (bf16[128,4096]{1,0:T(8,128)(2,1)}, bf16[128,4096]{1,0:T(8,128)(2,1)S(1)}, u32[]{:S(2)}) copy-start(bf16[128,4096]{1,0:T(8,128)(2,1)S(1)} %select_select_fusion) | copy-start | bytes 3145732
  38.0 1.7 copy-start.2
  41.3 6.8 %copy-start.5 = (s32[128,2]{0,1:T(2,128)S(1)}, s32[128,2]{0,1:T(2,128)}, u32[]{:S(2)}) copy-start(s32[128,2]{0,1:T(2,128)} %param.26) | copy-start | bytes 3076
  41.3 14.6 %copy-start.3 = (bf16[128,512]{1,0:T(8,128)(2,1)S(1)}, bf16[128,512]{1,0:T(8,128)(2,1)}, u32[]{:S(2)}) copy-start(bf16[128,512]{1,0:T(8,128)(2,1)} %param.18) | copy-start | bytes 393220
  48.3 23.5 %all-to-all-start.1 = ((bf16[16,4,4096]{2,1,0:T(4,128)(2,1)}), bf16[16,4,4096]{2,1,0:T(4,128)(2,1)S(1)}, u32[]{:S(2)}, u32[]{:S(2)}) async-start(bf16[16,4,4096]{2,1,0:T(4,128)(2,1)} %all_to_all.24), calls=%async_computation.1 | async-start | bytes 1048576 | tf_op jit(solution)/shard_map/all_to_all | solution.py:420
  76.4 3.4 %copy-start.4 = (f32[512,8]{0,1:T(8,128)S(1)}, f32[512,8]{0,1:T(8,128)}, u32[]{:S(2)}) copy-start(f32[512,8]{0,1:T(8,128)} %param.20) | copy-start | bytes 49156
  76.4 3.4 %copy-start.6 = (f32[512]{0:T(512)S(1)}, f32[512]{0:T(512)}, u32[]{:S(2)}) copy-start(f32[512]{0:T(512)} %param.21) | copy-start | bytes 6148
  105.8 79.1 %all-to-all-start.2 = ((bf16[16,4,4096]{2,1,0:T(4,128)(2,1)}), bf16[16,4,4096]{2,1,0:T(4,128)(2,1)S(1)}, u32[]{:S(2)}, u32[]{:S(2)}) async-start(bf16[16,4,4096]{2,1,0:T(4,128)(2,1)} %all_to_all.27), calls=%async_computation.2 | async-start | bytes 1048576 | tf_op jit(solution)/shard_map/all_to_all | solution.py:501
Sparse Core Ops, SparseCore 0:
  10.2 59.2 all-gather.1

commit v12 on v8

--- a/solution.py
+++ b/solution.py
@@ -398,7 +398,7 @@
     hidden = resid_new.astype(jnp.float32) + projected
     squares = jnp.sum(hidden * hidden, axis=1)
     scaled = hidden * norm_gain[None, :]
-    raw_logits = jnp.dot(scaled, router_w, precision=lax.Precision.HIGHEST)
+    raw_logits = jnp.sum(scaled[:, None, :] * router_w.T[None, :, :], axis=2)
     stats_t = jnp.concatenate([squares[None, :], raw_logits.T], axis=0)
     stats_t = jnp.pad(stats_t, ((0, 16 - stats_t.shape[0]), (0, 0)))
     n_exp = lax.axis_size("exp")

time: 197 us -> 197 us (level)
    unnamed x23 -> x25, local copies, waits for them, and re-layouts: 4.56 us -> 4.57 us
where the time goes in v12:
time: 197 us; the launch traced here: 196 us
  Pallas kernels  70.7 us (36%)
  waiting for transfers between devices  35.6 us (18%)
  local copies, waits for them, and re-layouts  34.3 us (17%)
  starting transfers between devices  19.5 us (10%)
  other arithmetic  17.8 us (9%)
  between operations  14.6 us (7%)
  matrix products  3.36 us (2%)
    pallas_call x1, Pallas kernels, gather_ffn(): pl.pallas_call(functools.partial(gather_ffn_kernel, n), out_shape=jax.Sha...  35.6 us
    pallas_call x3, Pallas kernels, exchange(): pl.pallas_call(functools.partial(exchange_kernel, axis, n, gather), out_s...  35.2 us
    all_to_all x1, waiting for transfers between devices, body(): lax.all_to_all(pick_rows(attention_out, send_index, send_live), 'req', sp...  15.7 us
    all_to_all x1, waiting for transfers between devices, body(): lax.all_to_all(pick_rows(page_rows, send_index, send_live), 'req', split_...  10.1 us
    scatter x1, local copies, waits for them, and re-layouts, body(): jnp.zeros((rows_all,), jnp.int32).at[came_from]  8.04 us
    all_to_all x1, starting transfers between devices, body(): lax.all_to_all(pick_rows(residual, send_index, send_live), 'req', split_a...  7.12 us
    all_to_all x1, starting transfers between devices, body(): lax.all_to_all(pick_rows(attention_out, send_index, send_live), 'req', sp...  6.97 us
    gather x5, local copies, waits for them, and re-layouts, pick_rows(): taken_rows = jnp.take(source, row_index, axis=0)  5.54 us
  transfers between devices with their start and end apart: 5, of which 5 were waited for; matrix products, arithmetic and copies ran while one was open for 21% of the time, Pallas kernels for 0%

profile of v12, /device:TPU:0, one launch (start us, length us, event | category | flops | bytes accessed | tf_op | source)
XLA Modules:
  0.0 196.0 jit_solution(16249709095605975737)
XLA Ops:
  7.2 0.7 all-gather.2.cloned.1.call-update
  7.9 0.7 compare_select_fusion.1
  8.6 8.0 %scatter_custom_fusion = s32[2048]{0:T(1024)S(1)} fusion(s32[2048]{0:T(1024)S(1)} %compare_select_fusion.1, s32[2048]{0:T(1024)S(1)} %iota.72, s32[]{:T(128)} %constant.181.clone.1), kind=kCustom, calls=%fused_computation.86 | custom fusion | bytes 8196 | tf_op jit(solution)/shard_map/scatter | solution.py:349
  16.8 2.8 %select_reduce_fusion = s32[16,128]{0,1:T(8,128)S(1)} fusion(s32[16,128]{0,1:T(8,128)S(1)} %copy.116), kind=kOutput, calls=%fused_computation.20 | output fusion | flops 4388864 | bytes 16384 | tf_op jit(solution)/shard_map/jit(cumsum)/reduce_window_sum | solution.py:355
  20.6 1.6 gather_fusion.1
  22.4 0.8 select_select_fusion.4
  23.1 7.1 %all-to-all-start = ((bf16[16,4,512]{2,1,0:T(4,128)(2,1)}), bf16[16,4,512]{2,1,0:T(4,128)(2,1)S(1)}, u32[]{:S(2)}, u32[]{:S(2)}) async-start(bf16[16,4,512]{2,1,0:T(4,128)(2,1)} %select_select_fusion.4), calls=%async_computation | async-start | bytes 131072 | tf_op jit(solution)/shard_map/all_to_all | solution.py:375
  30.4 0.8 copy.124
  31.5 0.9 gather_fusion.6
  32.6 1.0 all_to_all.24
  33.6 0.8 compare_select_fusion.15
  34.3 1.1 gather_fusion
  35.5 0.6 reduce-window.6
  36.9 0.8 compare_and_fusion.5
  38.0 7.0 %all-to-all-start.1 = ((bf16[16,4,4096]{2,1,0:T(4,128)(2,1)}), bf16[16,4,4096]{2,1,0:T(4,128)(2,1)S(1)}, u32[]{:S(2)}, u32[]{:S(2)}) async-start(bf16[16,4,4096]{2,1,0:T(4,128)(2,1)} %all_to_all.24), calls=%async_computation.1 | async-start | bytes 1048576 | tf_op jit(solution)/shard_map/all_to_all | solution.py:368
  45.1 0.4 and_reduce_fusion
  45.5 1.5 gather_fusion.2
  47.0 15.7 %all-to-all-done.1 = bf16[16,4,4096]{2,1,0:T(4,128)(2,1)S(1)} async-done(((bf16[16,4,4096]{2,1,0:T(4,128)(2,1)}), bf16[16,4,4096]{2,1,0:T(4,128)(2,1)S(1)}, u32[]{:S(2)}, u32[]{:S(2)}) %all-to-all-start.1) | async-done | bytes 524320 | tf_op jit(solution)/shard_map/all_to_all | solution.py:368
  62.9 1.4 pad_maximum_fusion
  64.3 2.2 %gather_fusion.7 = bf16[128,4096]{1,0:T(8,128)(2,1)} fusion(bf16[192,4096]{1,0:T(8,128)(2,1)S(1)} %pad_maximum_fusion, s32[1024]{0:T(1024)S(1)} %pad_clamp_fusion.4), kind=kCustom, calls=%fused_computation.1.clone | custom fusion | bytes 2097664 | tf_op jit(solution)/shard_map/jit(_take)/gather | solution.py:391
  66.4 3.4 %all-gather.2.cloned.1.call-done = bf16[4096,512]{1,0:T(8,128)(2,1)} async-done(((bf16[256,512]{1,0:T(8,128)(2,1)}), bf16[4096,512]{1,0:T(8,128)(2,1)}) %all-gather.2.cloned.1.call-update) | async-done | bytes 4194320 | tf_op jit(solution)/shard_map/all_gather | solution.py:395
  69.8 3.4 %multiply_reduce_fusion.1 = (f32[128]{0:T(128)S(1)}, f32[128,512]{1,0:T(8,128)S(1)}, f32[128,512]{1,0:T(8,128)S(1)}) fusion(f32[512]{0:T(512)S(1)} %copy-done.9, bf16[4096,512]{1,0:T(8,128)(2,1)} %all-gather.2.cloned.1.call-done, bf16[128,4096]{1,0:T(8,128)(2,1)} %gather_fusion.7, pred[128]{0:T(512)(128)(4,1)S(1)} %get-tuple-element.8, ...), kind=kOutput, calls=%fused_computation.41 | convolution fusion | flops 537788288 | bytes 5900928 | tf_op jit(solution)/shard_map/dot_general | solution.py:393
  73.5 0.6 select_maximum_fusion.x_ref
  74.1 7.7 %shard_map.140 = f32[8,16,128]{2,1,0:T(8,128)} custom-call(f32[16,128]{1,0:T(8,128)} %select_maximum_fusion.x_ref), custom_call_target="tpu_custom_call" | custom-call | tf_op jit(solution)/shard_map/pallas_call | solution.py:59
  81.8 0.9 reduce_sum.80
  82.8 2.2 %gather_fusion.3 = bf16[512,512]{1,0:T(8,128)(2,1)S(1)} fusion(bf16[128,512]{1,0:T(8,128)(2,1)S(1)} %multiply_convert_fusion, s32[1024]{0:T(1024)S(1)} %pad_clamp_fusion.2), kind=kCustom, calls=%fused_computation.7 | custom fusion | bytes 1050624 | tf_op jit(solution)/shard_map/jit(_take)/gather | solution.py:319
  84.9 1.0 select_select_fusion.3.x_ref
  85.9 14.4 %shard_map.141 = bf16[16,32,512]{2,1,0:T(8,128)(2,1)} custom-call(bf16[16,32,512]{2,1,0:T(8,128)(2,1)} %select_select_fusion.3.x_ref), custom_call_target="tpu_custom_call" | custom-call | tf_op jit(solution)/shard_map/pallas_call | solution.py:59
  100.3 35.6 %shard_map.142 = bf16[512,4096]{1,0:T(8,128)(2,1)} custom-call(bf16[512,512]{1,0:T(8,128)(2,1)} %bitcast.61, bf16[1,4096,896]{2,1,0:T(8,128)(2,1)} %wg_hbm.1, bf16[1,4096,896]{2,1,0:T(8,128)(2,1)} %wu_hbm.1, bf16[1,896,4096]{2,1,0:T(8,128)(2,1)} %wd_hbm.1), custom_call_target="tpu_custom_call" | custom-call | tf_op jit(solution)/shard_map/pallas_call | solution.py:296
  136.8 0.4 broadcast_in_dim.233
  137.2 1.1 copy.134
  138.6 0.7 broadcast_in_dim.235
  139.2 1.1 copy.135
  140.6 0.8 gather_fusion.5
  141.4 0.5 gather.47
  141.9 1.5 select_select_fusion
  143.4 0.9 gather_fusion.8
  144.4 1.0 all_to_all.27
  145.4 5.4 %all-to-all-start.2 = ((bf16[16,4,4096]{2,1,0:T(4,128)(2,1)}), bf16[16,4,4096]{2,1,0:T(4,128)(2,1)S(1)}, u32[]{:S(2)}, u32[]{:S(2)}) async-start(bf16[16,4,4096]{2,1,0:T(4,128)(2,1)} %all_to_all.27), calls=%async_computation.3 | async-start | bytes 1048576 | tf_op jit(solution)/shard_map/all_to_all | solution.py:448
  150.9 10.1 %all-to-all-done.2 = bf16[16,4,4096]{2,1,0:T(4,128)(2,1)S(1)} async-done(((bf16[16,4,4096]{2,1,0:T(4,128)(2,1)}), bf16[16,4,4096]{2,1,0:T(4,128)(2,1)S(1)}, u32[]{:S(2)}, u32[]{:S(2)}) %all-to-all-start.2) | async-done | bytes 524320 | tf_op jit(solution)/shard_map/all_to_all | solution.py:448
  161.1 1.3 pad_maximum_fusion.1
  162.4 2.2 %gather_fusion.9 = bf16[128,4096]{1,0:T(8,128)(2,1)} fusion(bf16[192,4096]{1,0:T(8,128)(2,1)S(1)} %pad_maximum_fusion.1, s32[1024]{0:T(1024)S(1)} %pad_clamp_fusion.4), kind=kCustom, calls=%fused_computation.3.clone | custom fusion | bytes 2097664 | tf_op jit(solution)/shard_map/jit(_take)/gather | solution.py:451
  164.6 1.4 broadcast_select_fusion
  166.0 1.2 copy.136
  167.2 5.4 %reduce-scatter.2.cloned.1.call-done = bf16[512,512]{1,0:T(8,128)(2,1)} async-done(((bf16[512,4096]{1,0:T(8,128)(2,1)}), bf16[512,512]{1,0:T(8,128)(2,1)}) %reduce-scatter.2.cloned.1.call-update) | async-done | bytes 524304 | tf_op jit(solution)/shard_map/reduce_scatter | solution.py:436
  172.6 13.1 %shard_map.143 = bf16[16,32,512]{2,1,0:T(8,128)(2,1)} custom-call(bf16[16,32,512]{2,1,0:T(8,128)(2,1)} %bitcast.67), custom_call_target="tpu_custom_call" | custom-call | tf_op jit(solution)/shard_map/pallas_call | solution.py:59
  185.8 2.3 %gather_fusion.4 = bf16[256,512]{1,0:T(8,128)(2,1)S(1)} fusion(bf16[512,512]{1,0:T(8,128)(2,1)} %bitcast.58, s32[1024]{0:T(1024)S(1)} %pad_clamp_fusion.1), kind=kCustom, calls=%fused_computation.8 | custom fusion | bytes 525312 | tf_op jit(solution)/shard_map/jit(_take)/gather | solution.py:458
  188.3 0.8 fusion.11
  (97 shorter events, 5.4 us)
Async XLA Ops:
  7.2 133.4 %copy-start = (bf16[256,8,256]{2,1,0:T(8,128)(2,1)S(1)}, bf16[256,8,256]{2,1,0:T(8,128)(2,1)}, u32[]{:S(2)}) copy-start(bf16[256,8,256]{2,1,0:T(8,128)(2,1)} %param.22) | copy-start | bytes 3145732
  7.2 24.4 %copy-start.2 = (bf16[128,4096]{1,0:T(8,128)(2,1)S(1)}, bf16[128,4096]{1,0:T(8,128)(2,1)}, u32[]{:S(2)}) copy-start(bf16[128,4096]{1,0:T(8,128)(2,1)} %param.17) | copy-start | bytes 3145732
  7.2 62.6 %all-gather.2.cloned.1.call-start = ((), (), s32[]{:S(2)}) async-start(), calls=%async_computation.4 | async-start | bytes 4456448 | tf_op jit(solution)/shard_map/all_gather | solution.py:395
  23.1 14.9 %all-to-all-start = ((bf16[16,4,512]{2,1,0:T(4,128)(2,1)}), bf16[16,4,512]{2,1,0:T(4,128)(2,1)S(1)}, u32[]{:S(2)}, u32[]{:S(2)}) async-start(bf16[16,4,512]{2,1,0:T(4,128)(2,1)} %select_select_fusion.4), calls=%async_computation | async-start | bytes 131072 | tf_op jit(solution)/shard_map/all_to_all | solution.py:375
  32.4 13.0 %copy-start.3 = (bf16[128,512]{1,0:T(8,128)(2,1)S(1)}, bf16[128,512]{1,0:T(8,128)(2,1)}, u32[]{:S(2)}) copy-start(bf16[128,512]{1,0:T(8,128)(2,1)} %param.18) | copy-start | bytes 393220
  38.0 24.7 %all-to-all-start.1 = ((bf16[16,4,4096]{2,1,0:T(4,128)(2,1)}), bf16[16,4,4096]{2,1,0:T(4,128)(2,1)S(1)}, u32[]{:S(2)}, u32[]{:S(2)}) async-start(bf16[16,4,4096]{2,1,0:T(4,128)(2,1)} %all_to_all.24), calls=%async_computation.1 | async-start | bytes 1048576 | tf_op jit(solution)/shard_map/all_to_all | solution.py:368
  45.0 127.6 %reduce-scatter.2.cloned.1.call-start = ((), (), s32[]{:S(2)}) async-start(), calls=%async_computation.5 | async-start | bytes 4718592 | tf_op jit(solution)/shard_map/reduce_scatter | solution.py:436
  64.2 5.6 %copy-start.4 = (bf16[128,512]{1,0:T(8,128)(2,1)S(1)}, bf16[128,512]{1,0:T(8,128)(2,1)}, u32[]{:S(2)}) copy-start(bf16[128,512]{1,0:T(8,128)(2,1)} %gather_fusion.2) | copy-start | bytes 393220
  64.3 5.6 %copy-start.9 = (f32[512]{0:T(512)S(1)}, f32[512]{0:T(512)}, u32[]{:S(2)}) copy-start(f32[512]{0:T(512)} %param.21) | copy-start | bytes 6148
  66.4 6.8 %copy-start.5 = (f32[512,8]{0,1:T(8,128)S(1)}, f32[512,8]{0,1:T(8,128)}, u32[]{:S(2)}) copy-start(f32[512,8]{0,1:T(8,128)} %param.20) | copy-start | bytes 49156
  135.9 0.7 copy-start.8
  135.9 2.4 %copy-start.7 = (s32[128,2]{0,1:T(2,128)S(1)}, s32[128,2]{0,1:T(2,128)}, u32[]{:S(2)}) copy-start(s32[128,2]{0,1:T(2,128)} %param.23) | copy-start | bytes 3076
  135.9 4.6 %copy-start.6 = (s32[128,2]{0,1:T(2,128)S(1)}, s32[128,2]{0,1:T(2,128)}, u32[]{:S(2)}) copy-start(s32[128,2]{0,1:T(2,128)} %param.26) | copy-start | bytes 3076
  143.4 2.0 %copy-start.1 = (bf16[128,4096]{1,0:T(8,128)(2,1)}, bf16[128,4096]{1,0:T(8,128)(2,1)S(1)}, u32[]{:S(2)}) copy-start(bf16[128,4096]{1,0:T(8,128)(2,1)S(1)} %select_select_fusion) | copy-start | bytes 3145732
  145.4 15.5 %all-to-all-start.2 = ((bf16[16,4,4096]{2,1,0:T(4,128)(2,1)}), bf16[16,4,4096]{2,1,0:T(4,128)(2,1)S(1)}, u32[]{:S(2)}, u32[]{:S(2)}) async-start(bf16[16,4,4096]{2,1,0:T(4,128)(2,1)} %all_to_all.27), calls=%async_computation.3 | async-start | bytes 1048576 | tf_op jit(solution)/shard_map/all_to_all | solution.py:448
Sparse Core Ops, SparseCore 0:
  10.2 59.6 all-gather.1
  136.1 36.5 reduce-scatter.1

commit v13 on v10

--- a/solution.py
+++ b/solution.py
@@ -191,9 +191,9 @@
 
 
 def gather_ffn_kernel(
-    n, x_ref, wg_hbm, wu_hbm, wd_hbm, o_ref,
+    n, groups, x_ref, wg_hbm, wu_hbm, wd_hbm, pg_ref, o_ref, pg_out,
     y_ref, wg_v, wu_v, wd_v, g_acc, u_acc, send_sems, recv_sems, w_sems,
-    sib_out, sib_buf, acc, stage, half_buf, near_buf, rs_send, rs_recv,
+    sib_out, sib_buf, acc, stage, half_buf, near_buf, rs_send, rs_recv, pg_send, pg_recv,
 ):
     chips = n // 2
     width = x_ref.shape[1]
@@ -221,7 +221,23 @@
     barrier = pltpu.get_barrier_semaphore()
     for peer in (sib, up, dn):
         pl.semaphore_signal(barrier, inc=1, device_id={"exp": peer}, device_id_type=MESH)
-    pl.semaphore_wait(barrier, 3)
+    own_group = lax.axis_index("req")
+    for k in range(1, groups):
+        pl.semaphore_signal(
+            barrier, inc=1, device_id={"req": lax.rem(own_group + k, groups)},
+            device_id_type=MESH,
+        )
+    pl.semaphore_wait(barrier, 3 + groups - 1)
+    page_copies = []
+    for k in range(1, groups):
+        peer = lax.rem(own_group + k, groups)
+        copy = pltpu.make_async_remote_copy(
+            src_ref=pg_ref.at[peer], dst_ref=pg_out.at[own_group], send_sem=pg_send.at[k],
+            recv_sem=pg_recv.at[k], device_id={"req": peer}, device_id_type=MESH,
+        )
+        copy.start()
+        page_copies.append(copy)
+    pg_out[own_group] = pg_ref[own_group]
 
     def remote(src, dst, slot, peer):
         return pltpu.make_async_remote_copy(
@@ -328,16 +344,27 @@
     ).astype(o_ref.dtype)
     for copy in sends:
         copy.wait_send()
-
-
-def gather_ffn(x, w_gate, w_up, w_down, n, collective_id):
+    for k in range(1, groups):
+        page_copies[k - 1].wait_send()
+        source = lax.rem(own_group + groups - k, groups)
+        pltpu.make_async_remote_copy(
+            src_ref=pg_ref.at[source], dst_ref=pg_out.at[source], send_sem=pg_send.at[k],
+            recv_sem=pg_recv.at[k], device_id={"req": source}, device_id_type=MESH,
+        ).wait_recv()
+
+
+def gather_ffn(x, w_gate, w_up, w_down, pages, n, groups, collective_id):
     rows_n, width = x.shape
     d, ff = w_gate.shape[1], w_gate.shape[2]
     return pl.pallas_call(
-        functools.partial(gather_ffn_kernel, n),
-        out_shape=jax.ShapeDtypeStruct((rows_n, w_down.shape[2] // n), x.dtype),
-        in_specs=[pl.BlockSpec(memory_space=pltpu.VMEM)] + [pl.BlockSpec(memory_space=pl.ANY)] * 3,
-        out_specs=pl.BlockSpec(memory_space=pltpu.VMEM),
+        functools.partial(gather_ffn_kernel, n, groups),
+        out_shape=(
+            jax.ShapeDtypeStruct((rows_n, w_down.shape[2] // n), x.dtype),
+            jax.ShapeDtypeStruct(pages.shape, pages.dtype),
+        ),
+        in_specs=[pl.BlockSpec(memory_space=pltpu.VMEM)] + [pl.BlockSpec(memory_space=pl.ANY)] * 3
+        + [pl.BlockSpec(memory_space=pltpu.VMEM)],
+        out_specs=(pl.BlockSpec(memory_space=pltpu.VMEM), pl.BlockSpec(memory_space=pltpu.VMEM)),
         scratch_shapes=[
             pltpu.VMEM((rows_n, n * width), x.dtype),
             pltpu.VMEM((d, ff), w_gate.dtype),
@@ -356,16 +383,13 @@
             pltpu.VMEM((2, rows_n, width), x.dtype),
             pltpu.SemaphoreType.DMA((8,)),
             pltpu.SemaphoreType.DMA((8,)),
+            pltpu.SemaphoreType.DMA((groups,)),
+            pltpu.SemaphoreType.DMA((groups,)),
         ],
         compiler_params=pltpu.CompilerParams(
             collective_id=collective_id, has_side_effects=True, vmem_limit_bytes=60 * 1024 * 1024
         ),
-        cost_estimate=pl.CostEstimate(
-            flops=2 * rows_n * d * ff * 3,
-            transcendentals=rows_n * ff,
-            bytes_accessed=2 * (3 * d * ff + 2 * rows_n * d),
-        ),
-    )(x, w_gate, w_up, w_down)
+    )(x, w_gate, w_up, w_down, pages)
 
 def pick_rows(source, row_index, live_slot):
     taken_rows = jnp.take(source, row_index, axis=0)
@@ -494,11 +518,18 @@
     page_rows = jnp.where(kept_mask[..., None], page_rows, jnp.zeros((), page_rows.dtype)).reshape(
         row_req, -1
     )
-    page_send, arrived = lax.optimization_barrier(
-        (pick_rows(page_rows, send_index, send_live), arrived)
-    )
-    moved_pages = lax.all_to_all(page_send, "req", split_axis=0, concat_axis=0, tiled=True)
-    partial_value = gather_ffn(arrived, w_gate, w_up, w_down, lax.axis_size("exp"), 3)
+    page_send = pick_rows(page_rows, send_index, send_live)
+    partial_value, moved_pages = gather_ffn(
+        arrived,
+        w_gate,
+        w_up,
+        w_down,
+        page_send.reshape(groups, MIG_PAIR, -1),
+        lax.axis_size("exp"),
+        groups,
+        3,
+    )
+    moved_pages = moved_pages.reshape(groups * MIG_PAIR, -1)
     summed_value = partial_value
     lookup = target_dev * CAP + slot_index
     new_pages = jnp.take(

time: 199 us -> 193 us (0.970)
  starting transfers between devices: 19.7 us -> 14.4 us
    all_to_all x1 -> x0, starting transfers between devices: 5.35 us -> none  [body(): lax.all_to_all(page_send, 'req', split_axis=0, concat_axis=0, tiled=True)]
    reshape x0 -> x2, local copies, waits for them, and re-layouts: none -> 2.16 us  [the longest x1 1.16 us: body(): moved_pages = moved_pages.reshape(groups * MIG_PAIR, -1)]
    pallas_call x1, Pallas kernels: 54.8 us -> 56.8 us  [gather_ffn(): pl.pallas_call(functools.partial(gather_ffn_kernel, n, groups), out_shape...]
  transfers between devices with their start and end apart: 4 -> 3, of which waited for: 1 -> 1; matrix products, arithmetic and copies ran while one was open for 20% -> 20% of each run, Pallas kernels for 36% -> 0%
where the time goes in v13:
time: 193 us; the launch traced here: 192 us
  Pallas kernels  90.8 us (47%)
  local copies, waits for them, and re-layouts  35.5 us (18%)
  other arithmetic  18.5 us (10%)
  waiting for transfers between devices  14.7 us (8%)
  between operations  14.5 us (8%)
  starting transfers between devices  14.4 us (7%)
  matrix products  3.64 us (2%)
    pallas_call x1, Pallas kernels, gather_ffn(): pl.pallas_call(functools.partial(gather_ffn_kernel, n, groups), out_shape...  56.8 us
    pallas_call x3, Pallas kernels, exchange(): pl.pallas_call(functools.partial(exchange_kernel, axis, n, gather), out_s...  33.9 us
    all_to_all x1, waiting for transfers between devices, body(): lax.all_to_all(pick_rows(attention_out, send_index, send_live), 'req', sp...  14 us
    scatter x1, local copies, waits for them, and re-layouts, body(): jnp.zeros((rows_all,), jnp.int32).at[came_from]  8.04 us
    all_to_all x1, starting transfers between devices, body(): lax.all_to_all(pick_rows(attention_out, send_index, send_live), 'req', sp...  7.23 us
    all_to_all x1, starting transfers between devices, body(): lax.all_to_all(pick_rows(residual, send_index, send_live), 'req', split_a...  7.12 us
    gather x5, local copies, waits for them, and re-layouts, pick_rows(): taken_rows = jnp.take(source, row_index, axis=0)  6.97 us
    unnamed x23, local copies, waits for them, and re-layouts  4.23 us
  transfers between devices with their start and end apart: 3, of which 1 were waited for; matrix products, arithmetic and copies ran while one was open for 20% of the time, Pallas kernels for 0%

profile of v13, /device:TPU:0, one launch (start us, length us, event | category | flops | bytes accessed | tf_op | source)
XLA Modules:
  0.0 192.1 jit_solution(11540181697108156329)
XLA Ops:
  7.2 0.7 all-gather.2.cloned.1.call-update
  7.9 0.7 compare_select_fusion.1
  8.7 8.0 %scatter_custom_fusion = s32[2048]{0:T(1024)S(1)} fusion(s32[2048]{0:T(1024)S(1)} %compare_select_fusion.1, s32[2048]{0:T(1024)S(1)} %iota.72, s32[]{:T(128)} %constant.181.clone.1), kind=kCustom, calls=%fused_computation.87 | custom fusion | bytes 8196 | tf_op jit(solution)/shard_map/scatter | solution.py:425
  16.8 2.8 %select_reduce_fusion = s32[16,128]{0,1:T(8,128)S(1)} fusion(s32[16,128]{0,1:T(8,128)S(1)} %copy.115), kind=kOutput, calls=%fused_computation.20 | output fusion | flops 4388864 | bytes 16384 | tf_op jit(solution)/shard_map/jit(cumsum)/reduce_window_sum | solution.py:431
  20.6 1.6 gather_fusion.1
  22.4 0.8 select_select_fusion.4
  23.1 7.1 %all-to-all-start = ((bf16[16,4,512]{2,1,0:T(4,128)(2,1)}), bf16[16,4,512]{2,1,0:T(4,128)(2,1)S(1)}, u32[]{:S(2)}, u32[]{:S(2)}) async-start(bf16[16,4,512]{2,1,0:T(4,128)(2,1)} %select_select_fusion.4), calls=%async_computation | async-start | bytes 131072 | tf_op jit(solution)/shard_map/all_to_all | solution.py:451
  30.5 0.8 copy.122
  31.7 0.8 copy.129
  32.6 0.8 gather_fusion.4
  33.4 0.5 gather.45
  34.2 0.4 broadcast_in_dim.230
  34.7 1.1 copy.132
  35.9 0.4 broadcast_in_dim.232
  36.4 0.3 copy.133
  36.7 1.3 select_select_fusion
  38.0 1.7 gather_fusion.8
  39.7 1.7 gather_fusion.6
  41.4 1.4 select_select_fusion.1
  42.8 1.0 all_to_all.16
  43.8 0.8 compare_select_fusion.15
  44.6 1.1 gather_fusion
  45.7 0.6 reduce-window.6
  46.9 0.4 fusion.6
  47.4 0.8 compare_and_fusion.5
  48.3 7.2 %all-to-all-start.1 = ((bf16[16,4,4096]{2,1,0:T(4,128)(2,1)}), bf16[16,4,4096]{2,1,0:T(4,128)(2,1)S(1)}, u32[]{:S(2)}, u32[]{:S(2)}) async-start(bf16[16,4,4096]{2,1,0:T(4,128)(2,1)} %all_to_all.16), calls=%async_computation.1 | async-start | bytes 1048576 | tf_op jit(solution)/shard_map/all_to_all | solution.py:444
  55.5 1.0 reshape.541.pg_ref
  56.5 0.4 and_reduce_fusion
  57.0 0.8 gather_fusion.2
  57.8 14.0 %all-to-all-done.1 = bf16[16,4,4096]{2,1,0:T(4,128)(2,1)S(1)} async-done(((bf16[16,4,4096]{2,1,0:T(4,128)(2,1)}), bf16[16,4,4096]{2,1,0:T(4,128)(2,1)S(1)}, u32[]{:S(2)}, u32[]{:S(2)}) %all-to-all-start.1) | async-done | bytes 524320 | tf_op jit(solution)/shard_map/all_to_all | solution.py:444
  71.9 1.3 pad_maximum_fusion
  73.3 2.2 %gather_fusion.7 = bf16[128,4096]{1,0:T(8,128)(2,1)} fusion(bf16[192,4096]{1,0:T(8,128)(2,1)S(1)} %pad_maximum_fusion, s32[1024]{0:T(1024)S(1)} %pad_clamp_fusion.4), kind=kCustom, calls=%fused_computation.1.clone | custom fusion | bytes 2097664 | tf_op jit(solution)/shard_map/jit(_take)/gather | solution.py:467
  75.5 3.4 %multiply_reduce_fusion = (f32[128]{0:T(128)S(1)}, f32[128,512]{1,0:T(8,128)S(1)}) fusion(bf16[4096,512]{1,0:T(8,128)(2,1)} %all-gather.2.cloned.1.call-done, bf16[128,4096]{1,0:T(8,128)(2,1)} %gather_fusion.7, pred[128]{0:T(512)(128)(4,1)S(1)} %get-tuple-element.8, bf16[128,512]{1,0:T(8,128)(2,1)S(1)} %gather_fusion.2), kind=kOutput, calls=%fused_computation.41 | convolution fusion | flops 537722752 | bytes 5636736 | tf_op jit(solution)/shard_map/dot_general | solution.py:469
  79.1 0.7 select_maximum_fusion.x_ref
  79.8 7.7 %shard_map.140 = f32[8,16,128]{2,1,0:T(8,128)} custom-call(f32[16,128]{1,0:T(8,128)} %select_maximum_fusion.x_ref), custom_call_target="tpu_custom_call" | custom-call | tf_op jit(solution)/shard_map/pallas_call | solution.py:59
  87.5 0.9 reduce_sum.70
  88.5 2.0 %gather_fusion.3 = bf16[512,512]{1,0:T(8,128)(2,1)S(1)} fusion(bf16[128,512]{1,0:T(8,128)(2,1)S(1)} %multiply_convert_fusion, s32[1024]{0:T(1024)S(1)} %pad_clamp_fusion.2), kind=kCustom, calls=%fused_computation.7 | custom fusion | bytes 1050624 | tf_op jit(solution)/shard_map/jit(_take)/gather | solution.py:395
  90.4 1.0 select_select_fusion.3.x_ref
  91.4 12.4 %shard_map.141 = bf16[16,32,512]{2,1,0:T(8,128)(2,1)} custom-call(bf16[16,32,512]{2,1,0:T(8,128)(2,1)} %select_select_fusion.3.x_ref), custom_call_target="tpu_custom_call" | custom-call | tf_op jit(solution)/shard_map/pallas_call | solution.py:59
  103.9 56.8 %shard_map.142 = (bf16[512,512]{1,0:T(8,128)(2,1)}, bf16[16,4,4096]{2,1,0:T(4,128)(2,1)}) custom-call(bf16[512,512]{1,0:T(8,128)(2,1)} %bitcast.62, bf16[1,4096,896]{2,1,0:T(8,128)(2,1)} %wg_hbm.1, bf16[1,4096,896]{2,1,0:T(8,128)(2,1)} %wu_hbm.1, bf16[1,896,4096]{2,1,0:T(8,128)(2,1)} %wd_hbm.1, bf16[16,4,4096]{2,1,0:T(4,128)(2,1)} %reshape.541.pg_ref), custom_call_target="tpu_custom_call" | custom-call | tf_op jit(solution)/shard_map/pallas_call | solution.py:359
  160.7 1.2 reshape.545
  161.9 1.3 pad_maximum_fusion.1
  163.3 2.2 %gather_fusion.9 = bf16[128,4096]{1,0:T(8,128)(2,1)} fusion(bf16[192,4096]{1,0:T(8,128)(2,1)S(1)} %pad_maximum_fusion.1, s32[1024]{0:T(1024)S(1)} %pad_clamp_fusion.4), kind=kCustom, calls=%fused_computation.3.clone | custom fusion | bytes 2097664 | tf_op jit(solution)/shard_map/jit(_take)/gather | solution.py:535
  165.4 1.4 broadcast_select_fusion
  166.8 1.2 copy.134
  168.1 13.8 %shard_map.143 = bf16[16,32,512]{2,1,0:T(8,128)(2,1)} custom-call(bf16[16,32,512]{2,1,0:T(8,128)(2,1)} %bitcast.68), custom_call_target="tpu_custom_call" | custom-call | tf_op jit(solution)/shard_map/pallas_call | solution.py:59
  181.9 2.3 %gather_fusion.5 = bf16[256,512]{1,0:T(8,128)(2,1)S(1)} fusion(bf16[512,512]{1,0:T(8,128)(2,1)} %bitcast.59, s32[1024]{0:T(1024)S(1)} %pad_clamp_fusion), kind=kCustom, calls=%fused_computation.9 | custom fusion | bytes 525312 | tf_op jit(solution)/shard_map/jit(_take)/gather | solution.py:541
  184.4 0.8 fusion.11
  (88 shorter events, 4.0 us)
Async XLA Ops:
  7.2 25.5 %copy-start = (bf16[256,8,256]{2,1,0:T(8,128)(2,1)S(1)}, bf16[256,8,256]{2,1,0:T(8,128)(2,1)}, u32[]{:S(2)}) copy-start(bf16[256,8,256]{2,1,0:T(8,128)(2,1)} %param.22) | copy-start | bytes 3145732
  7.2 26.8 %copy-start.8 = (s32[128]{0:T(128)S(1)}, s32[128]{0:T(128)}, u32[]{:S(2)}) copy-start(s32[128]{0:T(128)} %param.24) | copy-start | bytes 1540
  7.2 68.3 %all-gather.2.cloned.1.call-start = ((), (), s32[]{:S(2)}) async-start(), calls=%async_computation.2 | async-start | bytes 4456448 | tf_op jit(solution)/shard_map/all_gather | solution.py:471
  23.1 25.1 %all-to-all-start = ((bf16[16,4,512]{2,1,0:T(4,128)(2,1)}), bf16[16,4,512]{2,1,0:T(4,128)(2,1)S(1)}, u32[]{:S(2)}, u32[]{:S(2)}) async-start(bf16[16,4,512]{2,1,0:T(4,128)(2,1)} %select_select_fusion.4), calls=%async_computation | async-start | bytes 131072 | tf_op jit(solution)/shard_map/all_to_all | solution.py:451
  30.4 5.3 %copy-start.7 = (s32[128,2]{0,1:T(2,128)S(1)}, s32[128,2]{0,1:T(2,128)}, u32[]{:S(2)}) copy-start(s32[128,2]{0,1:T(2,128)} %param.23) | copy-start | bytes 3076
  38.0 3.4 %copy-start.1 = (bf16[128,4096]{1,0:T(8,128)(2,1)}, bf16[128,4096]{1,0:T(8,128)(2,1)S(1)}, u32[]{:S(2)}) copy-start(bf16[128,4096]{1,0:T(8,128)(2,1)S(1)} %select_select_fusion) | copy-start | bytes 3145732
  38.0 1.7 copy-start.2
  41.3 6.8 %copy-start.5 = (s32[128,2]{0,1:T(2,128)S(1)}, s32[128,2]{0,1:T(2,128)}, u32[]{:S(2)}) copy-start(s32[128,2]{0,1:T(2,128)} %param.26) | copy-start | bytes 3076
  41.3 15.6 %copy-start.3 = (bf16[128,512]{1,0:T(8,128)(2,1)S(1)}, bf16[128,512]{1,0:T(8,128)(2,1)}, u32[]{:S(2)}) copy-start(bf16[128,512]{1,0:T(8,128)(2,1)} %param.18) | copy-start | bytes 393220
  48.3 23.5 %all-to-all-start.1 = ((bf16[16,4,4096]{2,1,0:T(4,128)(2,1)}), bf16[16,4,4096]{2,1,0:T(4,128)(2,1)S(1)}, u32[]{:S(2)}, u32[]{:S(2)}) async-start(bf16[16,4,4096]{2,1,0:T(4,128)(2,1)} %all_to_all.16), calls=%async_computation.1 | async-start | bytes 1048576 | tf_op jit(solution)/shard_map/all_to_all | solution.py:444
  75.5 3.4 %copy-start.4 = (f32[512,8]{0,1:T(8,128)S(1)}, f32[512,8]{0,1:T(8,128)}, u32[]{:S(2)}) copy-start(f32[512,8]{0,1:T(8,128)} %param.20) | copy-start | bytes 49156
  75.5 3.4 %copy-start.6 = (f32[512]{0:T(512)S(1)}, f32[512]{0:T(512)}, u32[]{:S(2)}) copy-start(f32[512]{0:T(512)} %param.21) | copy-start | bytes 6148
Sparse Core Ops, SparseCore 0:
  10.2 59.2 all-gather.1

commit v14 on v13

--- a/solution.py
+++ b/solution.py
@@ -440,9 +440,12 @@
     )
     send_index = jnp.sum(jnp.where(chosen_send, local_ids[None, None, :], 0), axis=2).reshape(-1)
     send_live = jnp.any(chosen_send, axis=2).reshape(-1)
+    attn_send, page_pool = lax.optimization_barrier(
+        (pick_rows(attention_out, send_index, send_live), page_pool)
+    )
     moved_attn, moved_resid = (
         lax.all_to_all(
-            pick_rows(attention_out, send_index, send_live),
+            attn_send,
             "req",
             split_axis=0,
             concat_axis=0,

time: 193 us -> 193 us (level)
    unnamed x23 -> x27, local copies, waits for them, and re-layouts: 4.23 us -> 4.39 us
  transfers between devices with their start and end apart: 3 -> 3, of which waited for: 1 -> 1; matrix products, arithmetic and copies ran while one was open for 20% -> 18% of each run, Pallas kernels for 0% -> 0%
where the time goes in v14:
time: 193 us; the launch traced here: 192 us
  Pallas kernels  92 us (48%)
  local copies, waits for them, and re-layouts  33.8 us (18%)
  other arithmetic  17.6 us (9%)
  waiting for transfers between devices  16.2 us (8%)
  between operations  14.6 us (8%)
  starting transfers between devices  14.4 us (7%)
  matrix products  3.64 us (2%)
    pallas_call x1, Pallas kernels, gather_ffn(): pl.pallas_call(functools.partial(gather_ffn_kernel, n, groups), out_shape...  56.8 us
    pallas_call x3, Pallas kernels, exchange(): pl.pallas_call(functools.partial(exchange_kernel, axis, n, gather), out_s...  35.1 us
    all_to_all x1, waiting for transfers between devices, body(): lax.all_to_all(attn_send, 'req', split_axis=0, concat_axis=0, tiled=True)  15.5 us
    scatter x1, local copies, waits for them, and re-layouts, body(): jnp.zeros((rows_all,), jnp.int32).at[came_from]  8.04 us
    all_to_all x1, starting transfers between devices, body(): lax.all_to_all(attn_send, 'req', split_axis=0, concat_axis=0, tiled=True)  7.24 us
    all_to_all x1, starting transfers between devices, body(): lax.all_to_all(pick_rows(residual, send_index, send_live), 'req', split_a...  7.12 us
    gather x5, local copies, waits for them, and re-layouts, pick_rows(): taken_rows = jnp.take(source, row_index, axis=0)  5.36 us
    unnamed x27, local copies, waits for them, and re-layouts  4.39 us
  transfers between devices with their start and end apart: 3, of which 1 were waited for; matrix products, arithmetic and copies ran while one was open for 18% of the time, Pallas kernels for 0%

profile of v14, /device:TPU:0, one launch (start us, length us, event | category | flops | bytes accessed | tf_op | source)
XLA Modules:
  0.0 192.1 jit_solution(17602208695626294749)
XLA Ops:
  7.2 0.7 all-gather.2.cloned.1.call-update
  7.9 0.7 compare_select_fusion.1
  8.6 8.0 %scatter_custom_fusion = s32[2048]{0:T(1024)S(1)} fusion(s32[2048]{0:T(1024)S(1)} %compare_select_fusion.1, s32[2048]{0:T(1024)S(1)} %iota.72, s32[]{:T(128)} %constant.181.clone.1), kind=kCustom, calls=%fused_computation.87 | custom fusion | bytes 8196 | tf_op jit(solution)/shard_map/scatter | solution.py:425
  16.8 2.8 %select_reduce_fusion = s32[16,128]{0,1:T(8,128)S(1)} fusion(s32[16,128]{0,1:T(8,128)S(1)} %copy.115), kind=kOutput, calls=%fused_computation.20 | output fusion | flops 4388864 | bytes 16384 | tf_op jit(solution)/shard_map/jit(cumsum)/reduce_window_sum | solution.py:431
  19.9 0.2 select_reduce_fusion.1
  20.6 1.6 gather_fusion.1
  22.4 0.8 select_select_fusion.4
  23.1 7.1 %all-to-all-start = ((bf16[16,4,512]{2,1,0:T(4,128)(2,1)}), bf16[16,4,512]{2,1,0:T(4,128)(2,1)S(1)}, u32[]{:S(2)}, u32[]{:S(2)}) async-start(bf16[16,4,512]{2,1,0:T(4,128)(2,1)} %select_select_fusion.4), calls=%async_computation | async-start | bytes 131072 | tf_op jit(solution)/shard_map/all_to_all | solution.py:454
  30.4 0.8 copy.122
  31.7 0.9 gather_fusion.6
  32.7 1.0 all_to_all.16
  33.7 0.8 compare_select_fusion.15
  34.5 1.1 gather_fusion
  35.7 0.6 reduce-window.6
  36.8 0.4 fusion.6
  37.5 0.4 broadcast_in_dim.230
  38.0 1.1 copy.132
  39.3 0.4 broadcast_in_dim.232
  39.8 1.1 copy.133
  41.1 0.8 gather_fusion.4
  41.8 0.5 gather.45
  42.4 1.4 select_select_fusion
  43.8 0.9 gather_fusion.8
  44.8 0.8 compare_and_fusion.5
  45.8 7.2 %all-to-all-start.1 = ((bf16[16,4,4096]{2,1,0:T(4,128)(2,1)}), bf16[16,4,4096]{2,1,0:T(4,128)(2,1)S(1)}, u32[]{:S(2)}, u32[]{:S(2)}) async-start(bf16[16,4,4096]{2,1,0:T(4,128)(2,1)} %all_to_all.16), calls=%async_computation.1 | async-start | bytes 1048576 | tf_op jit(solution)/shard_map/all_to_all | solution.py:447
  53.1 1.0 reshape.541.pg_ref
  54.1 0.4 and_reduce_fusion
  54.5 0.8 gather_fusion.2
  55.4 15.5 %all-to-all-done.1 = bf16[16,4,4096]{2,1,0:T(4,128)(2,1)S(1)} async-done(((bf16[16,4,4096]{2,1,0:T(4,128)(2,1)}), bf16[16,4,4096]{2,1,0:T(4,128)(2,1)S(1)}, u32[]{:S(2)}, u32[]{:S(2)}) %all-to-all-start.1) | async-done | bytes 524320 | tf_op jit(solution)/shard_map/all_to_all | solution.py:447
  71.0 1.3 pad_maximum_fusion
  72.4 2.2 %gather_fusion.7 = bf16[128,4096]{1,0:T(8,128)(2,1)} fusion(bf16[192,4096]{1,0:T(8,128)(2,1)S(1)} %pad_maximum_fusion, s32[1024]{0:T(1024)S(1)} %pad_clamp_fusion.4), kind=kCustom, calls=%fused_computation.1.clone | custom fusion | bytes 2097664 | tf_op jit(solution)/shard_map/jit(_take)/gather | solution.py:470
  74.5 3.4 %multiply_reduce_fusion = (f32[128]{0:T(128)S(1)}, f32[128,512]{1,0:T(8,128)S(1)}) fusion(bf16[4096,512]{1,0:T(8,128)(2,1)} %all-gather.2.cloned.1.call-done, bf16[128,4096]{1,0:T(8,128)(2,1)} %gather_fusion.7, pred[128]{0:T(512)(128)(4,1)S(1)} %get-tuple-element.12, bf16[128,512]{1,0:T(8,128)(2,1)S(1)} %gather_fusion.2), kind=kOutput, calls=%fused_computation.41 | convolution fusion | flops 537722752 | bytes 5636736 | tf_op jit(solution)/shard_map/dot_general | solution.py:472
  77.9 0.3 convolution_bitcast_fusion
  78.2 0.7 select_maximum_fusion.x_ref
  78.9 8.6 %shard_map.140 = f32[8,16,128]{2,1,0:T(8,128)} custom-call(f32[16,128]{1,0:T(8,128)} %select_maximum_fusion.x_ref), custom_call_target="tpu_custom_call" | custom-call | tf_op jit(solution)/shard_map/pallas_call | solution.py:59
  87.5 0.9 reduce_sum.70
  88.4 2.0 %gather_fusion.3 = bf16[512,512]{1,0:T(8,128)(2,1)S(1)} fusion(bf16[128,512]{1,0:T(8,128)(2,1)S(1)} %multiply_convert_fusion, s32[1024]{0:T(1024)S(1)} %pad_clamp_fusion.2), kind=kCustom, calls=%fused_computation.7 | custom fusion | bytes 1050624 | tf_op jit(solution)/shard_map/jit(_take)/gather | solution.py:395
  90.4 1.0 select_select_fusion.3.x_ref
  91.4 12.4 %shard_map.141 = bf16[16,32,512]{2,1,0:T(8,128)(2,1)} custom-call(bf16[16,32,512]{2,1,0:T(8,128)(2,1)} %select_select_fusion.3.x_ref), custom_call_target="tpu_custom_call" | custom-call | tf_op jit(solution)/shard_map/pallas_call | solution.py:59
  103.9 56.8 %shard_map.142 = (bf16[512,512]{1,0:T(8,128)(2,1)}, bf16[16,4,4096]{2,1,0:T(4,128)(2,1)}) custom-call(bf16[512,512]{1,0:T(8,128)(2,1)} %bitcast.62, bf16[1,4096,896]{2,1,0:T(8,128)(2,1)} %wg_hbm.1, bf16[1,4096,896]{2,1,0:T(8,128)(2,1)} %wu_hbm.1, bf16[1,896,4096]{2,1,0:T(8,128)(2,1)} %wd_hbm.1, bf16[16,4,4096]{2,1,0:T(4,128)(2,1)} %reshape.541.pg_ref), custom_call_target="tpu_custom_call" | custom-call | tf_op jit(solution)/shard_map/pallas_call | solution.py:359
  160.7 14.1 %shard_map.143 = bf16[16,32,512]{2,1,0:T(8,128)(2,1)} custom-call(bf16[16,32,512]{2,1,0:T(8,128)(2,1)} %bitcast.68), custom_call_target="tpu_custom_call" | custom-call | tf_op jit(solution)/shard_map/pallas_call | solution.py:59
  174.8 2.3 %gather_fusion.5 = bf16[256,512]{1,0:T(8,128)(2,1)S(1)} fusion(bf16[512,512]{1,0:T(8,128)(2,1)} %bitcast.59, s32[1024]{0:T(1024)S(1)} %pad_clamp_fusion), kind=kCustom, calls=%fused_computation.9 | custom fusion | bytes 525312 | tf_op jit(solution)/shard_map/jit(_take)/gather | solution.py:544
  177.2 0.8 gather.47
  178.1 1.3 pad_maximum_fusion.1
  179.5 2.2 %gather_fusion.9 = bf16[128,4096]{1,0:T(8,128)(2,1)} fusion(bf16[192,4096]{1,0:T(8,128)(2,1)S(1)} %pad_maximum_fusion.1, s32[1024]{0:T(1024)S(1)} %pad_clamp_fusion.4), kind=kCustom, calls=%fused_computation.3.clone | custom fusion | bytes 2097664 | tf_op jit(solution)/shard_map/jit(_take)/gather | solution.py:538
  181.7 1.4 broadcast_select_fusion
  183.1 1.2 copy.134
  184.4 0.8 fusion.11
  (93 shorter events, 4.0 us)
Async XLA Ops:
  7.2 33.9 %copy-start = (bf16[256,8,256]{2,1,0:T(8,128)(2,1)S(1)}, bf16[256,8,256]{2,1,0:T(8,128)(2,1)}, u32[]{:S(2)}) copy-start(bf16[256,8,256]{2,1,0:T(8,128)(2,1)} %param.22) | copy-start | bytes 3145732
  7.2 24.5 %copy-start.2 = (bf16[128,4096]{1,0:T(8,128)(2,1)S(1)}, bf16[128,4096]{1,0:T(8,128)(2,1)}, u32[]{:S(2)}) copy-start(bf16[128,4096]{1,0:T(8,128)(2,1)} %param.17) | copy-start | bytes 3145732
  7.2 67.3 %all-gather.2.cloned.1.call-start = ((), (), s32[]{:S(2)}) async-start(), calls=%async_computation.2 | async-start | bytes 4456448 | tf_op jit(solution)/shard_map/all_gather | solution.py:474
  23.1 22.7 %all-to-all-start = ((bf16[16,4,512]{2,1,0:T(4,128)(2,1)}), bf16[16,4,512]{2,1,0:T(4,128)(2,1)S(1)}, u32[]{:S(2)}, u32[]{:S(2)}) async-start(bf16[16,4,512]{2,1,0:T(4,128)(2,1)} %select_select_fusion.4), calls=%async_computation | async-start | bytes 131072 | tf_op jit(solution)/shard_map/all_to_all | solution.py:454
  31.7 5.7 %copy-start.10 = (s32[128]{0:T(128)S(1)}, s32[128]{0:T(128)}, u32[]{:S(2)}) copy-start(s32[128]{0:T(128)} %param.24) | copy-start | bytes 1540
  32.6 6.5 %copy-start.9 = (s32[128,2]{0,1:T(2,128)S(1)}, s32[128,2]{0,1:T(2,128)}, u32[]{:S(2)}) copy-start(s32[128,2]{0,1:T(2,128)} %param.23) | copy-start | bytes 3076
  43.8 2.0 %copy-start.1 = (bf16[128,4096]{1,0:T(8,128)(2,1)}, bf16[128,4096]{1,0:T(8,128)(2,1)S(1)}, u32[]{:S(2)}) copy-start(bf16[128,4096]{1,0:T(8,128)(2,1)S(1)} %select_select_fusion) | copy-start | bytes 3145732
  43.8 1.8 copy-start.7
  43.8 10.7 %copy-start.3 = (bf16[128,512]{1,0:T(8,128)(2,1)S(1)}, bf16[128,512]{1,0:T(8,128)(2,1)}, u32[]{:S(2)}) copy-start(bf16[128,512]{1,0:T(8,128)(2,1)} %param.18) | copy-start | bytes 393220
  45.8 25.1 %all-to-all-start.1 = ((bf16[16,4,4096]{2,1,0:T(4,128)(2,1)}), bf16[16,4,4096]{2,1,0:T(4,128)(2,1)S(1)}, u32[]{:S(2)}, u32[]{:S(2)}) async-start(bf16[16,4,4096]{2,1,0:T(4,128)(2,1)} %all_to_all.16), calls=%async_computation.1 | async-start | bytes 1048576 | tf_op jit(solution)/shard_map/all_to_all | solution.py:447
  74.5 3.4 %copy-start.6 = (f32[512,8]{0,1:T(8,128)S(1)}, f32[512,8]{0,1:T(8,128)}, u32[]{:S(2)}) copy-start(f32[512,8]{0,1:T(8,128)} %param.20) | copy-start | bytes 49156
  74.5 3.4 %copy-start.8 = (f32[512]{0:T(512)S(1)}, f32[512]{0:T(512)}, u32[]{:S(2)}) copy-start(f32[512]{0:T(512)} %param.21) | copy-start | bytes 6148
  160.7 17.3 %copy-start.5 = (bf16[16,4,4096]{2,1,0:T(4,128)(2,1)S(1)}, bf16[16,4,4096]{2,1,0:T(4,128)(2,1)}, u32[]{:S(2)}) copy-start(bf16[16,4,4096]{2,1,0:T(4,128)(2,1)} %get-tuple-element.11) | copy-start | bytes 1572868
  181.7 2.7 %copy-start.4 = (bf16[128,2,512]{2,1,0:T(2,128)(2,1)S(1)}, bf16[128,2,512]{2,1,0:T(2,128)(2,1)}, u32[]{:S(2)}) copy-start(bf16[128,2,512]{2,1,0:T(2,128)(2,1)} %gather.47) | copy-start | bytes 786436
Sparse Core Ops, SparseCore 0:
  10.2 59.6 all-gather.1

commit v15 on v14

--- a/solution.py
+++ b/solution.py
@@ -535,9 +535,14 @@
     moved_pages = moved_pages.reshape(groups * MIG_PAIR, -1)
     summed_value = partial_value
     lookup = target_dev * CAP + slot_index
-    new_pages = jnp.take(
-        jnp.concatenate([page_rows, moved_pages], axis=0), arrival, axis=0
-    ).reshape(row_req, pages_req, page_len, kv_slice)
+    pick_home = (arrival[:, None] == jnp.arange(row_req)[None, :]).astype(page_rows.dtype)
+    pick_moved = (
+        arrival[:, None] == row_req + jnp.arange(moved_pages.shape[0])[None, :]
+    ).astype(page_rows.dtype)
+    new_pages = (
+        jnp.dot(pick_home, page_rows, preferred_element_type=jnp.float32)
+        + jnp.dot(pick_moved, moved_pages, preferred_element_type=jnp.float32)
+    ).astype(page_rows.dtype).reshape(row_req, pages_req, page_len, kv_slice)
     returned = exchange(
         summed_value.reshape(groups, -1, summed_value.shape[-1]), "req", groups, False, 2
     ).reshape(summed_value.shape)

time: 193 us -> 193 us (level)
  matrix products: 3.64 us -> 7.02 us
  other arithmetic: 17.6 us -> 14.8 us
    dot_general x0 -> x2, matrix products: none -> 3.38 us  [the longest x1 1.81 us: body(): jnp.dot(pick_home, page_rows, preferred_element_type=jnp.float32)]
    gather x1 -> x0, local copies, waits for them, and re-layouts: 2.16 us -> none  [body(): jnp.take(jnp.concatenate([page_rows, moved_pages], axis=0), arrival, axis=0)]
    unnamed x27 -> x25, local copies, waits for them, and re-layouts: 4.39 us -> 3.71 us
  transfers between devices with their start and end apart: 3 -> 3, of which waited for: 1 -> 1; matrix products, arithmetic and copies ran while one was open for 18% -> 19% of each run, Pallas kernels for 0% -> 0%
where the time goes in v15:
time: 193 us; the launch traced here: 192 us
  Pallas kernels  91.1 us (47%)
  local copies, waits for them, and re-layouts  34.4 us (18%)
  waiting for transfers between devices  15.8 us (8%)
  other arithmetic  14.8 us (8%)
  between operations  14.6 us (8%)
  starting transfers between devices  14.4 us (7%)
  matrix products  7.02 us (4%)
    pallas_call x1, Pallas kernels, gather_ffn(): pl.pallas_call(functools.partial(gather_ffn_kernel, n, groups), out_shape...  56.8 us
    pallas_call x3, Pallas kernels, exchange(): pl.pallas_call(functools.partial(exchange_kernel, axis, n, gather), out_s...  34.3 us
    all_to_all x1, waiting for transfers between devices, body(): lax.all_to_all(attn_send, 'req', split_axis=0, concat_axis=0, tiled=True)  15.1 us
    scatter x1, local copies, waits for them, and re-layouts, body(): jnp.zeros((rows_all,), jnp.int32).at[came_from]  8.04 us
    all_to_all x1, starting transfers between devices, body(): lax.all_to_all(attn_send, 'req', split_axis=0, concat_axis=0, tiled=True)  7.24 us
    all_to_all x1, starting transfers between devices, body(): lax.all_to_all(pick_rows(residual, send_index, send_live), 'req', split_a...  7.12 us
    gather x5, local copies, waits for them, and re-layouts, pick_rows(): taken_rows = jnp.take(source, row_index, axis=0)  5.36 us
    gather x2, local copies, waits for them, and re-layouts, body(): jnp.take(returned, lookup, axis=0).reshape(row_req, 2, -1)  4.77 us
  transfers between devices with their start and end apart: 3, of which 1 were waited for; matrix products, arithmetic and copies ran while one was open for 19% of the time, Pallas kernels for 0%

profile of v15, /device:TPU:0, one launch (start us, length us, event | category | flops | bytes accessed | tf_op | source)
XLA Modules:
  0.0 192.1 jit_solution(2125146876698127528)
XLA Ops:
  7.2 0.7 all-gather.2.cloned.1.call-update
  7.9 0.7 compare_select_fusion.1
  8.6 8.0 %scatter_custom_fusion = s32[2048]{0:T(1024)S(1)} fusion(s32[2048]{0:T(1024)S(1)} %compare_select_fusion.1, s32[2048]{0:T(1024)S(1)} %iota.81, s32[]{:T(128)} %constant.184.clone.1), kind=kCustom, calls=%fused_computation.92 | custom fusion | bytes 8196 | tf_op jit(solution)/shard_map/scatter | solution.py:425
  16.8 2.8 %select_reduce_fusion = s32[16,128]{0,1:T(8,128)S(1)} fusion(s32[16,128]{0,1:T(8,128)S(1)} %copy.115), kind=kOutput, calls=%fused_computation.20 | output fusion | flops 4388864 | bytes 16384 | tf_op jit(solution)/shard_map/jit(cumsum)/reduce_window_sum | solution.py:431
  19.9 0.2 select_reduce_fusion.1
  20.6 1.6 gather_fusion.1
  22.4 0.8 select_select_fusion.4
  23.1 7.1 %all-to-all-start = ((bf16[16,4,512]{2,1,0:T(4,128)(2,1)}), bf16[16,4,512]{2,1,0:T(4,128)(2,1)S(1)}, u32[]{:S(2)}, u32[]{:S(2)}) async-start(bf16[16,4,512]{2,1,0:T(4,128)(2,1)} %select_select_fusion.4), calls=%async_computation | async-start | bytes 131072 | tf_op jit(solution)/shard_map/all_to_all | solution.py:454
  30.5 0.9 gather_fusion.7
  32.1 1.0 all_to_all.16
  33.1 0.8 compare_select_fusion.15
  33.8 1.1 gather_fusion
  35.0 0.6 reduce-window.6
  35.6 0.2 slice_reduce_fusion
  36.2 0.4 fusion.7
  36.9 0.4 broadcast_in_dim.235
  37.3 1.1 copy.132
  38.7 0.4 broadcast_in_dim.237
  39.1 1.1 copy.133
  40.4 0.8 gather_fusion.5
  41.2 0.5 gather.47
  41.7 1.4 select_select_fusion
  43.1 0.9 gather_fusion.8
  44.2 1.0 reshape.542.pg_ref
  45.2 0.8 compare_and_fusion.5
  46.1 0.4 and_reduce_fusion
  46.5 7.2 %all-to-all-start.1 = ((bf16[16,4,4096]{2,1,0:T(4,128)(2,1)}), bf16[16,4,4096]{2,1,0:T(4,128)(2,1)S(1)}, u32[]{:S(2)}, u32[]{:S(2)}) async-start(bf16[16,4,4096]{2,1,0:T(4,128)(2,1)} %all_to_all.16), calls=%async_computation.1 | async-start | bytes 1048576 | tf_op jit(solution)/shard_map/all_to_all | solution.py:447
  53.8 1.8 fusion.17
  55.6 0.8 gather_fusion.2
  56.5 15.1 %all-to-all-done.1 = bf16[16,4,4096]{2,1,0:T(4,128)(2,1)S(1)} async-done(((bf16[16,4,4096]{2,1,0:T(4,128)(2,1)}), bf16[16,4,4096]{2,1,0:T(4,128)(2,1)S(1)}, u32[]{:S(2)}, u32[]{:S(2)}) %all-to-all-start.1) | async-done | bytes 524320 | tf_op jit(solution)/shard_map/all_to_all | solution.py:447
  71.7 1.3 pad_maximum_fusion
  73.1 2.2 %gather_fusion.3 = bf16[128,4096]{1,0:T(8,128)(2,1)} fusion(bf16[192,4096]{1,0:T(8,128)(2,1)S(1)} %pad_maximum_fusion, s32[1024]{0:T(1024)S(1)} %pad_clamp_fusion.4), kind=kCustom, calls=%fused_computation.5 | custom fusion | bytes 2097664 | tf_op jit(solution)/shard_map/jit(_take)/gather | solution.py:470
  75.2 3.4 %multiply_reduce_fusion = (f32[128]{0:T(128)S(1)}, f32[128,512]{1,0:T(8,128)S(1)}) fusion(bf16[4096,512]{1,0:T(8,128)(2,1)} %all-gather.2.cloned.1.call-done, bf16[128,4096]{1,0:T(8,128)(2,1)} %gather_fusion.3, pred[128]{0:T(512)(128)(4,1)S(1)} %get-tuple-element.11, bf16[128,512]{1,0:T(8,128)(2,1)S(1)} %gather_fusion.2), kind=kOutput, calls=%fused_computation.40 | convolution fusion | flops 537722752 | bytes 5636736 | tf_op jit(solution)/shard_map/dot_general | solution.py:472
  78.6 0.3 convolution_bitcast_fusion
  78.9 0.7 select_maximum_fusion.x_ref
  79.6 7.9 %shard_map.140 = f32[8,16,128]{2,1,0:T(8,128)} custom-call(f32[16,128]{1,0:T(8,128)} %select_maximum_fusion.x_ref), custom_call_target="tpu_custom_call" | custom-call | tf_op jit(solution)/shard_map/pallas_call | solution.py:59
  87.5 0.9 reduce_sum.70
  88.4 2.0 %gather_fusion.4 = bf16[512,512]{1,0:T(8,128)(2,1)S(1)} fusion(bf16[128,512]{1,0:T(8,128)(2,1)S(1)} %multiply_convert_fusion, s32[1024]{0:T(1024)S(1)} %pad_clamp_fusion.2), kind=kCustom, calls=%fused_computation.6 | custom fusion | bytes 1050624 | tf_op jit(solution)/shard_map/jit(_take)/gather | solution.py:395
  90.4 1.0 select_select_fusion.3.x_ref
  91.4 12.4 %shard_map.141 = bf16[16,32,512]{2,1,0:T(8,128)(2,1)} custom-call(bf16[16,32,512]{2,1,0:T(8,128)(2,1)} %select_select_fusion.3.x_ref), custom_call_target="tpu_custom_call" | custom-call | tf_op jit(solution)/shard_map/pallas_call | solution.py:59
  103.9 56.8 %shard_map.142 = (bf16[512,512]{1,0:T(8,128)(2,1)}, bf16[16,4,4096]{2,1,0:T(4,128)(2,1)}) custom-call(bf16[512,512]{1,0:T(8,128)(2,1)} %bitcast.64, bf16[1,4096,896]{2,1,0:T(8,128)(2,1)} %wg_hbm.1, bf16[1,4096,896]{2,1,0:T(8,128)(2,1)} %wu_hbm.1, bf16[1,896,4096]{2,1,0:T(8,128)(2,1)} %wd_hbm.1, bf16[16,4,4096]{2,1,0:T(4,128)(2,1)} %reshape.542.pg_ref), custom_call_target="tpu_custom_call" | custom-call | tf_op jit(solution)/shard_map/pallas_call | solution.py:359
  160.7 14.0 %shard_map.143 = bf16[16,32,512]{2,1,0:T(8,128)(2,1)} custom-call(bf16[16,32,512]{2,1,0:T(8,128)(2,1)} %bitcast.70), custom_call_target="tpu_custom_call" | custom-call | tf_op jit(solution)/shard_map/pallas_call | solution.py:59
  174.7 3.0 %gather_fusion.6 = bf16[256,512]{1,0:T(8,128)(2,1)} fusion(bf16[512,512]{1,0:T(8,128)(2,1)} %bitcast.61, s32[1024]{0:T(1024)S(1)} %pad_clamp_fusion), kind=kCustom, calls=%fused_computation.8 | custom fusion | bytes 525312 | tf_op jit(solution)/shard_map/jit(_take)/gather | solution.py:549
  177.7 1.8 gather.49
  179.5 2.0 %reshape.546 = bf16[64,4096]{1,0:T(8,128)(2,1)} reshape(bf16[16,4,4096]{2,1,0:T(4,128)(2,1)} %get-tuple-element.10) | data formatting | bytes 1048576 | tf_op jit(solution)/shard_map/reshape | solution.py:535
  181.5 1.6 fusion
  183.1 1.2 copy.134
  184.4 0.8 fusion.12
  (92 shorter events, 3.7 us)
Async XLA Ops:
  7.2 33.3 %copy-start = (bf16[256,8,256]{2,1,0:T(8,128)(2,1)S(1)}, bf16[256,8,256]{2,1,0:T(8,128)(2,1)}, u32[]{:S(2)}) copy-start(bf16[256,8,256]{2,1,0:T(8,128)(2,1)} %param.20) | copy-start | bytes 3145732
  7.2 23.3 %copy-start.1 = (bf16[128,4096]{1,0:T(8,128)(2,1)S(1)}, bf16[128,4096]{1,0:T(8,128)(2,1)}, u32[]{:S(2)}) copy-start(bf16[128,4096]{1,0:T(8,128)(2,1)} %param.15) | copy-start | bytes 3145732
  7.2 68.0 %all-gather.2.cloned.1.call-start = ((), (), s32[]{:S(2)}) async-start(), calls=%async_computation.2 | async-start | bytes 4456448 | tf_op jit(solution)/shard_map/all_gather | solution.py:474
  22.2 9.3 %copy-start.6 = (s32[128,2]{0,1:T(2,128)S(1)}, s32[128,2]{0,1:T(2,128)}, u32[]{:S(2)}) copy-start(s32[128,2]{0,1:T(2,128)} %param.24) | copy-start | bytes 3076
  23.1 23.4 %all-to-all-start = ((bf16[16,4,512]{2,1,0:T(4,128)(2,1)}), bf16[16,4,512]{2,1,0:T(4,128)(2,1)S(1)}, u32[]{:S(2)}, u32[]{:S(2)}) async-start(bf16[16,4,512]{2,1,0:T(4,128)(2,1)} %select_select_fusion.4), calls=%async_computation | async-start | bytes 131072 | tf_op jit(solution)/shard_map/all_to_all | solution.py:454
  30.5 6.2 %copy-start.9 = (s32[128]{0:T(128)S(1)}, s32[128]{0:T(128)}, u32[]{:S(2)}) copy-start(s32[128]{0:T(128)} %param.22) | copy-start | bytes 1540
  31.4 7.1 %copy-start.8 = (s32[128,2]{0,1:T(2,128)S(1)}, s32[128,2]{0,1:T(2,128)}, u32[]{:S(2)}) copy-start(s32[128,2]{0,1:T(2,128)} %param.21) | copy-start | bytes 3076
  44.0 11.6 %copy-start.3 = (bf16[128,512]{1,0:T(8,128)(2,1)S(1)}, bf16[128,512]{1,0:T(8,128)(2,1)}, u32[]{:S(2)}) copy-start(bf16[128,512]{1,0:T(8,128)(2,1)} %param.16) | copy-start | bytes 393220
  46.5 25.1 %all-to-all-start.1 = ((bf16[16,4,4096]{2,1,0:T(4,128)(2,1)}), bf16[16,4,4096]{2,1,0:T(4,128)(2,1)S(1)}, u32[]{:S(2)}, u32[]{:S(2)}) async-start(bf16[16,4,4096]{2,1,0:T(4,128)(2,1)} %all_to_all.16), calls=%async_computation.1 | async-start | bytes 1048576 | tf_op jit(solution)/shard_map/all_to_all | solution.py:447
  75.2 3.4 %copy-start.5 = (f32[512,8]{0,1:T(8,128)S(1)}, f32[512,8]{0,1:T(8,128)}, u32[]{:S(2)}) copy-start(f32[512,8]{0,1:T(8,128)} %param.18) | copy-start | bytes 49156
  75.2 3.4 %copy-start.7 = (f32[512]{0:T(512)S(1)}, f32[512]{0:T(512)}, u32[]{:S(2)}) copy-start(f32[512]{0:T(512)} %param.19) | copy-start | bytes 6148
  160.7 20.8 %copy-start.2 = (f32[128,4096]{1,0:T(8,128)S(1)}, f32[128,4096]{1,0:T(8,128)}, u32[]{:S(2)}) copy-start(f32[128,4096]{1,0:T(8,128)} %fusion.17) | copy-start | bytes 6291460
  181.5 2.8 %copy-start.4 = (bf16[128,2,512]{2,1,0:T(2,128)(2,1)S(1)}, bf16[128,2,512]{2,1,0:T(2,128)(2,1)}, u32[]{:S(2)}) copy-start(bf16[128,2,512]{2,1,0:T(2,128)(2,1)} %gather.49) | copy-start | bytes 786436
Sparse Core Ops, SparseCore 0:
  10.2 59.6 all-gather.1

commit v16 on v14

--- a/solution.py
+++ b/solution.py
@@ -265,9 +265,11 @@
     ]
     for copy in sends:
         copy.start()
+    w_rows = pl.ds(pl.multiple_of(me * width, width), width)
     weight_copies[0].wait()
+    g_acc[...] = jnp.dot(x_ref[...], wg_v[w_rows, :], preferred_element_type=jnp.float32)
     weight_copies[1].wait()
-    consume(me, first=True)
+    u_acc[...] = jnp.dot(x_ref[...], wu_v[w_rows, :], preferred_element_type=jnp.float32)
     remote(x_ref, y_ref.at[:, cols(dn)], 0, dn).wait_recv()
     remote(x_ref, y_ref.at[:, cols(up)], 1, up).wait_recv()
     second = [

time: 193 us -> 193 us (level)
  no operation moved by 1% of the time
where the time goes in v16:
time: 193 us; the launch traced here: 192 us
  Pallas kernels  92 us (48%)
  local copies, waits for them, and re-layouts  33.8 us (18%)
  other arithmetic  17.6 us (9%)
  waiting for transfers between devices  16.2 us (8%)
  between operations  14.6 us (8%)
  starting transfers between devices  14.4 us (7%)
  matrix products  3.64 us (2%)
    pallas_call x1, Pallas kernels, gather_ffn(): pl.pallas_call(functools.partial(gather_ffn_kernel, n, groups), out_shape...  56.8 us
    pallas_call x3, Pallas kernels, exchange(): pl.pallas_call(functools.partial(exchange_kernel, axis, n, gather), out_s...  35.1 us
    all_to_all x1, waiting for transfers between devices, body(): lax.all_to_all(attn_send, 'req', split_axis=0, concat_axis=0, tiled=True)  15.5 us
    scatter x1, local copies, waits for them, and re-layouts, body(): jnp.zeros((rows_all,), jnp.int32).at[came_from]  8.04 us
    all_to_all x1, starting transfers between devices, body(): lax.all_to_all(attn_send, 'req', split_axis=0, concat_axis=0, tiled=True)  7.24 us
    all_to_all x1, starting transfers between devices, body(): lax.all_to_all(pick_rows(residual, send_index, send_live), 'req', split_a...  7.12 us
    gather x5, local copies, waits for them, and re-layouts, pick_rows(): taken_rows = jnp.take(source, row_index, axis=0)  5.36 us
    unnamed x27, local copies, waits for them, and re-layouts  4.39 us
  transfers between devices with their start and end apart: 3, of which 1 were waited for; matrix products, arithmetic and copies ran while one was open for 18% of the time, Pallas kernels for 0%

profile of v16, /device:TPU:0, one launch (start us, length us, event | category | flops | bytes accessed | tf_op | source)
XLA Modules:
  0.0 192.1 jit_solution(7395302198045199057)
XLA Ops:
  7.2 0.7 all-gather.2.cloned.1.call-update
  7.9 0.7 compare_select_fusion.1
  8.6 8.0 %scatter_custom_fusion = s32[2048]{0:T(1024)S(1)} fusion(s32[2048]{0:T(1024)S(1)} %compare_select_fusion.1, s32[2048]{0:T(1024)S(1)} %iota.72, s32[]{:T(128)} %constant.181.clone.1), kind=kCustom, calls=%fused_computation.87 | custom fusion | bytes 8196 | tf_op jit(solution)/shard_map/scatter | solution.py:427
  16.8 2.8 %select_reduce_fusion = s32[16,128]{0,1:T(8,128)S(1)} fusion(s32[16,128]{0,1:T(8,128)S(1)} %copy.115), kind=kOutput, calls=%fused_computation.20 | output fusion | flops 4388864 | bytes 16384 | tf_op jit(solution)/shard_map/jit(cumsum)/reduce_window_sum | solution.py:433
  19.9 0.2 select_reduce_fusion.1
  20.6 1.6 gather_fusion.1
  22.4 0.8 select_select_fusion.4
  23.1 7.1 %all-to-all-start = ((bf16[16,4,512]{2,1,0:T(4,128)(2,1)}), bf16[16,4,512]{2,1,0:T(4,128)(2,1)S(1)}, u32[]{:S(2)}, u32[]{:S(2)}) async-start(bf16[16,4,512]{2,1,0:T(4,128)(2,1)} %select_select_fusion.4), calls=%async_computation | async-start | bytes 131072 | tf_op jit(solution)/shard_map/all_to_all | solution.py:456
  30.4 0.8 copy.122
  31.7 0.9 gather_fusion.6
  32.7 1.0 all_to_all.16
  33.7 0.8 compare_select_fusion.15
  34.5 1.1 gather_fusion
  35.7 0.6 reduce-window.6
  36.8 0.4 fusion.6
  37.5 0.4 broadcast_in_dim.230
  38.0 1.1 copy.132
  39.3 0.4 broadcast_in_dim.232
  39.8 1.1 copy.133
  41.1 0.8 gather_fusion.4
  41.8 0.5 gather.45
  42.4 1.4 select_select_fusion
  43.8 0.9 gather_fusion.8
  44.8 0.8 compare_and_fusion.5
  45.8 7.2 %all-to-all-start.1 = ((bf16[16,4,4096]{2,1,0:T(4,128)(2,1)}), bf16[16,4,4096]{2,1,0:T(4,128)(2,1)S(1)}, u32[]{:S(2)}, u32[]{:S(2)}) async-start(bf16[16,4,4096]{2,1,0:T(4,128)(2,1)} %all_to_all.16), calls=%async_computation.1 | async-start | bytes 1048576 | tf_op jit(solution)/shard_map/all_to_all | solution.py:449
  53.1 1.0 reshape.541.pg_ref
  54.1 0.4 and_reduce_fusion
  54.5 0.8 gather_fusion.2
  55.4 15.5 %all-to-all-done.1 = bf16[16,4,4096]{2,1,0:T(4,128)(2,1)S(1)} async-done(((bf16[16,4,4096]{2,1,0:T(4,128)(2,1)}), bf16[16,4,4096]{2,1,0:T(4,128)(2,1)S(1)}, u32[]{:S(2)}, u32[]{:S(2)}) %all-to-all-start.1) | async-done | bytes 524320 | tf_op jit(solution)/shard_map/all_to_all | solution.py:449
  71.0 1.3 pad_maximum_fusion
  72.4 2.2 %gather_fusion.7 = bf16[128,4096]{1,0:T(8,128)(2,1)} fusion(bf16[192,4096]{1,0:T(8,128)(2,1)S(1)} %pad_maximum_fusion, s32[1024]{0:T(1024)S(1)} %pad_clamp_fusion.4), kind=kCustom, calls=%fused_computation.1.clone | custom fusion | bytes 2097664 | tf_op jit(solution)/shard_map/jit(_take)/gather | solution.py:472
  74.5 3.4 %multiply_reduce_fusion = (f32[128]{0:T(128)S(1)}, f32[128,512]{1,0:T(8,128)S(1)}) fusion(bf16[4096,512]{1,0:T(8,128)(2,1)} %all-gather.2.cloned.1.call-done, bf16[128,4096]{1,0:T(8,128)(2,1)} %gather_fusion.7, pred[128]{0:T(512)(128)(4,1)S(1)} %get-tuple-element.12, bf16[128,512]{1,0:T(8,128)(2,1)S(1)} %gather_fusion.2), kind=kOutput, calls=%fused_computation.41 | convolution fusion | flops 537722752 | bytes 5636736 | tf_op jit(solution)/shard_map/dot_general | solution.py:474
  77.9 0.3 convolution_bitcast_fusion
  78.2 0.7 select_maximum_fusion.x_ref
  78.9 8.6 %shard_map.140 = f32[8,16,128]{2,1,0:T(8,128)} custom-call(f32[16,128]{1,0:T(8,128)} %select_maximum_fusion.x_ref), custom_call_target="tpu_custom_call" | custom-call | tf_op jit(solution)/shard_map/pallas_call | solution.py:59
  87.5 0.9 reduce_sum.70
  88.4 2.0 %gather_fusion.3 = bf16[512,512]{1,0:T(8,128)(2,1)S(1)} fusion(bf16[128,512]{1,0:T(8,128)(2,1)S(1)} %multiply_convert_fusion, s32[1024]{0:T(1024)S(1)} %pad_clamp_fusion.2), kind=kCustom, calls=%fused_computation.7 | custom fusion | bytes 1050624 | tf_op jit(solution)/shard_map/jit(_take)/gather | solution.py:397
  90.4 1.0 select_select_fusion.3.x_ref
  91.4 12.4 %shard_map.141 = bf16[16,32,512]{2,1,0:T(8,128)(2,1)} custom-call(bf16[16,32,512]{2,1,0:T(8,128)(2,1)} %select_select_fusion.3.x_ref), custom_call_target="tpu_custom_call" | custom-call | tf_op jit(solution)/shard_map/pallas_call | solution.py:59
  103.9 56.8 %shard_map.142 = (bf16[512,512]{1,0:T(8,128)(2,1)}, bf16[16,4,4096]{2,1,0:T(4,128)(2,1)}) custom-call(bf16[512,512]{1,0:T(8,128)(2,1)} %bitcast.62, bf16[1,4096,896]{2,1,0:T(8,128)(2,1)} %wg_hbm.1, bf16[1,4096,896]{2,1,0:T(8,128)(2,1)} %wu_hbm.1, bf16[1,896,4096]{2,1,0:T(8,128)(2,1)} %wd_hbm.1, bf16[16,4,4096]{2,1,0:T(4,128)(2,1)} %reshape.541.pg_ref), custom_call_target="tpu_custom_call" | custom-call | tf_op jit(solution)/shard_map/pallas_call | solution.py:361
  160.7 14.1 %shard_map.143 = bf16[16,32,512]{2,1,0:T(8,128)(2,1)} custom-call(bf16[16,32,512]{2,1,0:T(8,128)(2,1)} %bitcast.68), custom_call_target="tpu_custom_call" | custom-call | tf_op jit(solution)/shard_map/pallas_call | solution.py:59
  174.8 2.3 %gather_fusion.5 = bf16[256,512]{1,0:T(8,128)(2,1)S(1)} fusion(bf16[512,512]{1,0:T(8,128)(2,1)} %bitcast.59, s32[1024]{0:T(1024)S(1)} %pad_clamp_fusion), kind=kCustom, calls=%fused_computation.9 | custom fusion | bytes 525312 | tf_op jit(solution)/shard_map/jit(_take)/gather | solution.py:546
  177.2 0.8 gather.47
  178.1 1.3 pad_maximum_fusion.1
  179.5 2.2 %gather_fusion.9 = bf16[128,4096]{1,0:T(8,128)(2,1)} fusion(bf16[192,4096]{1,0:T(8,128)(2,1)S(1)} %pad_maximum_fusion.1, s32[1024]{0:T(1024)S(1)} %pad_clamp_fusion.4), kind=kCustom, calls=%fused_computation.3.clone | custom fusion | bytes 2097664 | tf_op jit(solution)/shard_map/jit(_take)/gather | solution.py:540
  181.7 1.4 broadcast_select_fusion
  183.1 1.2 copy.134
  184.4 0.8 fusion.11
  (93 shorter events, 4.0 us)
Async XLA Ops:
  7.2 33.9 %copy-start = (bf16[256,8,256]{2,1,0:T(8,128)(2,1)S(1)}, bf16[256,8,256]{2,1,0:T(8,128)(2,1)}, u32[]{:S(2)}) copy-start(bf16[256,8,256]{2,1,0:T(8,128)(2,1)} %param.22) | copy-start | bytes 3145732
  7.2 24.5 %copy-start.2 = (bf16[128,4096]{1,0:T(8,128)(2,1)S(1)}, bf16[128,4096]{1,0:T(8,128)(2,1)}, u32[]{:S(2)}) copy-start(bf16[128,4096]{1,0:T(8,128)(2,1)} %param.17) | copy-start | bytes 3145732
  7.2 67.3 %all-gather.2.cloned.1.call-start = ((), (), s32[]{:S(2)}) async-start(), calls=%async_computation.2 | async-start | bytes 4456448 | tf_op jit(solution)/shard_map/all_gather | solution.py:476
  23.1 22.7 %all-to-all-start = ((bf16[16,4,512]{2,1,0:T(4,128)(2,1)}), bf16[16,4,512]{2,1,0:T(4,128)(2,1)S(1)}, u32[]{:S(2)}, u32[]{:S(2)}) async-start(bf16[16,4,512]{2,1,0:T(4,128)(2,1)} %select_select_fusion.4), calls=%async_computation | async-start | bytes 131072 | tf_op jit(solution)/shard_map/all_to_all | solution.py:456
  31.7 5.7 %copy-start.10 = (s32[128]{0:T(128)S(1)}, s32[128]{0:T(128)}, u32[]{:S(2)}) copy-start(s32[128]{0:T(128)} %param.24) | copy-start | bytes 1540
  32.6 6.5 %copy-start.9 = (s32[128,2]{0,1:T(2,128)S(1)}, s32[128,2]{0,1:T(2,128)}, u32[]{:S(2)}) copy-start(s32[128,2]{0,1:T(2,128)} %param.23) | copy-start | bytes 3076
  43.8 2.0 %copy-start.1 = (bf16[128,4096]{1,0:T(8,128)(2,1)}, bf16[128,4096]{1,0:T(8,128)(2,1)S(1)}, u32[]{:S(2)}) copy-start(bf16[128,4096]{1,0:T(8,128)(2,1)S(1)} %select_select_fusion) | copy-start | bytes 3145732
  43.8 1.8 copy-start.7
  43.8 10.7 %copy-start.3 = (bf16[128,512]{1,0:T(8,128)(2,1)S(1)}, bf16[128,512]{1,0:T(8,128)(2,1)}, u32[]{:S(2)}) copy-start(bf16[128,512]{1,0:T(8,128)(2,1)} %param.18) | copy-start | bytes 393220
  45.8 25.1 %all-to-all-start.1 = ((bf16[16,4,4096]{2,1,0:T(4,128)(2,1)}), bf16[16,4,4096]{2,1,0:T(4,128)(2,1)S(1)}, u32[]{:S(2)}, u32[]{:S(2)}) async-start(bf16[16,4,4096]{2,1,0:T(4,128)(2,1)} %all_to_all.16), calls=%async_computation.1 | async-start | bytes 1048576 | tf_op jit(solution)/shard_map/all_to_all | solution.py:449
  74.5 3.4 %copy-start.6 = (f32[512,8]{0,1:T(8,128)S(1)}, f32[512,8]{0,1:T(8,128)}, u32[]{:S(2)}) copy-start(f32[512,8]{0,1:T(8,128)} %param.20) | copy-start | bytes 49156
  74.5 3.4 %copy-start.8 = (f32[512]{0:T(512)S(1)}, f32[512]{0:T(512)}, u32[]{:S(2)}) copy-start(f32[512]{0:T(512)} %param.21) | copy-start | bytes 6148
  160.7 17.3 %copy-start.5 = (bf16[16,4,4096]{2,1,0:T(4,128)(2,1)S(1)}, bf16[16,4,4096]{2,1,0:T(4,128)(2,1)}, u32[]{:S(2)}) copy-start(bf16[16,4,4096]{2,1,0:T(4,128)(2,1)} %get-tuple-element.11) | copy-start | bytes 1572868
  181.7 2.7 %copy-start.4 = (bf16[128,2,512]{2,1,0:T(2,128)(2,1)S(1)}, bf16[128,2,512]{2,1,0:T(2,128)(2,1)}, u32[]{:S(2)}) copy-start(bf16[128,2,512]{2,1,0:T(2,128)(2,1)} %gather.47) | copy-start | bytes 786436
Sparse Core Ops, SparseCore 0:
  10.2 59.6 all-gather.1
